TPU v7x, 128 devices: a whole 4x4x4 slice. The times are simulated.
128 devices in a mesh: chan: 16 (over x_hi, z, core), tm: 8 (over x_lo, y).
Axes of the slice: x: 4 (x_hi: 2, x_lo: 2; x = x_hi * 2 + x_lo), y: 4, z: 4, core: 2. Of those that a mesh axis runs over, the one named last changes fastest.
Arguments:
- spectra: bfloat16 [1792, 32, 16, 2, 256], P('tm', None, 'chan'), may hold values from -6 to 6
- partner: int32 [3, 16], replicated, may hold values from 0 to 15, as said below
Outputs:
- stacks: float32 [3, 16, 16, 2, 256, 256], P(None, 'chan', 'tm')
Inputs may be any that keep to these rules, and one draw needn't show every extreme that they name: `partner`: each of the 3 rows pairs the 16 blocks off: entry i is j exactly when entry j is i, and never i; no two rows pair the same two blocks.
All inputs are finite; a program needn't handle non-finite values.
Results may differ from a plain program's by a relative error of at most 0.0003.
Values may be sent and summed in bfloat16 or wider, within the bound.
No kernel may reach another device: no remote copies, remote signals or barrier semaphores. Data moves between devices by JAX's collectives and lax.ppermute only.
A program may use at most 128 MiB of HBM per device.

v0:
```python
import math

import jax
import jax.numpy as jnp
from jax import lax
from jax.sharding import PartitionSpec as P


def cross_terms(own_half, partner_half, width):
    product = jnp.einsum("wfa,wfb->fab", own_half, partner_half, preferred_element_type=jnp.float32)
    real_part = product[:, :width, :width] + product[:, width:, width:]
    imag_part = product[:, width:, :width] - product[:, :width, width:]
    return jnp.stack([real_part, imag_part], axis=1)


def bin_terms(own_half, partner_half, width):
    return cross_terms(own_half, partner_half, width)


def per_device(spectra, partner):
    window_count, bins, _, _, width = spectra.shape
    blocks = lax.axis_size("chan")
    groups = lax.axis_size("tm")
    position = lax.axis_index("chan")
    rounds = partner.shape[0]
    half_bins = bins // 2
    halves = (jnp.arange(blocks, dtype=jnp.int32)[None, :] > partner).astype(jnp.int32)
    flat = spectra.reshape(window_count, bins, 2 * width)
    arranged = flat.reshape(window_count, 2, half_bins, 2 * width)
    pieces = arranged.reshape(blocks, window_count // blocks, 2, half_bins, 2 * width)
    holdings = lax.all_to_all(pieces, "chan", split_axis=0, concat_axis=0, tiled=True)
    fetched = []
    for round_index in range(rounds):
        outgoing = holdings[partner[round_index], :, halves[round_index]]
        incoming = lax.all_to_all(outgoing, "chan", split_axis=0, concat_axis=0, tiled=True)
        fetched.append(incoming.reshape(window_count, half_bins, 2 * width))
    scale = 1.0 / math.sqrt(window_count * groups)
    results = []
    for round_index in range(rounds):
        mine = halves[round_index][position]
        own_half = lax.dynamic_index_in_dim(arranged, mine, 1, keepdims=False)
        term = lax.psum_scatter(
            bin_terms(own_half, fetched[round_index], width), "tm", scatter_dimension=0, tiled=True
        )
        results.append(term * scale)
    return jnp.stack(results)[:, None]


def solution(mesh):
    placed = (P("tm", None, "chan", None, None), P())
    return jax.shard_map(
        per_device,
        mesh=mesh,
        in_specs=placed,
        out_specs=P(None, "chan", "tm", None, None, None),
        check_vma=False,
    )
```

profile of v0, /device:TPU:1, one launch (start us, length us, event | category | flops | bytes accessed | tf_op | source)
XLA Modules:
  0.0 917.8 jit_solution(16056532042234771094)
XLA Ops:
  6.5 12.5 %reshape_reshape_reshape.3 = bf16[16,14,2,16,512]{4,3,2,1,0:T(8,128)(2,1)} reshape(bf16[224,32,1,2,256]{4,3,2,1,0:T(2,128)(2,1)} %param.2) | data formatting | bytes 14680064 | tf_op jit(solution)/shard_map/reshape;reshape;reshape | solution.py:30
  19.0 9.4 %all-to-all-start = ((bf16[16,14,2,16,512]{4,3,2,1,0:T(8,128)(2,1)}), bf16[16,14,2,16,512]{4,3,2,1,0:T(8,128)(2,1)}, u32[]{:S(2)}, u32[]{:S(2)}) async-start(bf16[16,14,2,16,512]{4,3,2,1,0:T(8,128)(2,1)} %reshape_reshape_reshape.3), calls=%async_computation | async-start | bytes 14680064 | tf_op jit(solution)/shard_map/all_to_all | solution.py:31
  28.5 103.5 %all-to-all-done = bf16[16,14,2,16,512]{4,3,2,1,0:T(8,128)(2,1)} async-done(((bf16[16,14,2,16,512]{4,3,2,1,0:T(8,128)(2,1)}), bf16[16,14,2,16,512]{4,3,2,1,0:T(8,128)(2,1)}, u32[]{:S(2)}, u32[]{:S(2)}) %all-to-all-start) | async-done | bytes 7340064 | tf_op jit(solution)/shard_map/all_to_all | solution.py:31
  132.0 5.8 gather_fusion
  137.8 14.4 %all-to-all-start.1 = ((bf16[16,14,16,512]{3,2,1,0:T(8,128)(2,1)}), bf16[16,14,16,512]{3,2,1,0:T(8,128)(2,1)}, u32[]{:S(2)}, u32[]{:S(2)}) async-start(bf16[16,14,16,512]{3,2,1,0:T(8,128)(2,1)} %gather_fusion), calls=%async_computation.1 | async-start | bytes 7340032 | tf_op jit(solution)/shard_map/all_to_all | solution.py:35
  152.1 5.8 gather_fusion.1
  157.9 42.0 %all-to-all-done.1 = bf16[16,14,16,512]{3,2,1,0:T(8,128)(2,1)} async-done(((bf16[16,14,16,512]{3,2,1,0:T(8,128)(2,1)}), bf16[16,14,16,512]{3,2,1,0:T(8,128)(2,1)}, u32[]{:S(2)}, u32[]{:S(2)}) %all-to-all-start.1) | async-done | bytes 3670048 | tf_op jit(solution)/shard_map/all_to_all | solution.py:35
  199.9 12.4 %all-to-all-start.2 = ((bf16[16,14,16,512]{3,2,1,0:T(8,128)(2,1)}), bf16[16,14,16,512]{3,2,1,0:T(8,128)(2,1)}, u32[]{:S(2)}, u32[]{:S(2)}) async-start(bf16[16,14,16,512]{3,2,1,0:T(8,128)(2,1)} %gather_fusion.1), calls=%async_computation.2 | async-start | bytes 7340032 | tf_op jit(solution)/shard_map/all_to_all | solution.py:35
  212.3 5.7 gather_fusion.2
  218.0 42.0 %all-to-all-done.2 = bf16[16,14,16,512]{3,2,1,0:T(8,128)(2,1)} async-done(((bf16[16,14,16,512]{3,2,1,0:T(8,128)(2,1)}), bf16[16,14,16,512]{3,2,1,0:T(8,128)(2,1)}, u32[]{:S(2)}, u32[]{:S(2)}) %all-to-all-start.2) | async-done | bytes 3670048 | tf_op jit(solution)/shard_map/all_to_all | solution.py:35
  260.0 12.4 %all-to-all-start.3 = ((bf16[16,14,16,512]{3,2,1,0:T(8,128)(2,1)}), bf16[16,14,16,512]{3,2,1,0:T(8,128)(2,1)}, u32[]{:S(2)}, u32[]{:S(2)}) async-start(bf16[16,14,16,512]{3,2,1,0:T(8,128)(2,1)} %gather_fusion.2), calls=%async_computation.3 | async-start | bytes 7340032 | tf_op jit(solution)/shard_map/all_to_all | solution.py:35
  272.5 0.6 constant_dynamic-slice_fusion.1
  275.5 0.6 constant_dynamic-slice_fusion.5
  277.4 12.9 %reshape_reshape.3 = bf16[224,2,16,512]{3,2,1,0:T(8,128)(2,1)} reshape(bf16[224,32,1,2,256]{4,3,2,1,0:T(2,128)(2,1)} %param.2) | data formatting | bytes 14680064 | tf_op jit(solution)/shard_map/reshape;reshape | solution.py:29
  292.1 8.6 constant_dynamic-slice_fusion.4
  300.7 18.2 %fusion.8 = f32[16,512,512]{2,1,0:T(8,128)} fusion(bf16[224,1,16,512]{3,2,1,0:T(8,128)(2,1)} %get-tuple-element.14, bf16[224,16,512]{2,1,0:T(8,128)(2,1)} %bitcast.5), kind=kOutput, calls=%fused_computation.23 | convolution fusion | flops 1879048192 | bytes 24117248 | tf_op jit(solution)/shard_map/wfa,wfb->fab/dot_general | solution.py:10
  319.0 10.6 %fusion.5 = (f32[16,1,256,256]{3,2,0,1:T(8,128)}, f32[16,1,256,256]{3,2,0,1:T(8,128)}) fusion(f32[16,512,512]{2,1,0:T(8,128)} %fusion.8), kind=kLoop, calls=%fused_computation.17 | loop fusion | flops 2097152 | bytes 25165824 | tf_op jit(solution)/shard_map/stack | solution.py:13
  329.6 17.7 %fusion.7 = f32[16,512,512]{2,1,0:T(8,128)} fusion(bf16[224,1,16,512]{3,2,1,0:T(8,128)(2,1)S(1)} %get-tuple-element.15, bf16[224,16,512]{2,1,0:T(8,128)(2,1)} %bitcast.14), kind=kOutput, calls=%fused_computation.21 | convolution fusion | flops 1879048192 | bytes 24117248 | tf_op jit(solution)/shard_map/wfa,wfb->fab/dot_general | solution.py:10
  347.3 10.6 %fusion.3 = (f32[16,1,256,256]{3,2,0,1:T(8,128)}, f32[16,1,256,256]{3,2,0,1:T(8,128)}) fusion(f32[16,512,512]{2,1,0:T(8,128)} %fusion.7), kind=kLoop, calls=%fused_computation.13 | loop fusion | flops 2097152 | bytes 25165824 | tf_op jit(solution)/shard_map/stack | solution.py:13
  357.9 18.4 %fusion.6 = f32[16,512,512]{2,1,0:T(8,128)} fusion(bf16[224,1,16,512]{3,2,1,0:T(8,128)(2,1)} %get-tuple-element.16, bf16[224,16,512]{2,1,0:T(8,128)(2,1)} %bitcast.23), kind=kOutput, calls=%fused_computation.19 | convolution fusion | flops 1879048192 | bytes 24117248 | tf_op jit(solution)/shard_map/wfa,wfb->fab/dot_general | solution.py:10
  376.3 10.8 %fusion.1 = (f32[16,1,256,256]{3,2,0,1:T(8,128)}, f32[16,1,256,256]{3,2,0,1:T(8,128)}) fusion(f32[16,512,512]{2,1,0:T(8,128)} %fusion.6), kind=kLoop, calls=%fused_computation.9 | loop fusion | flops 2097152 | bytes 25165824 | tf_op jit(solution)/shard_map/stack | solution.py:13
  387.1 6.6 pad_maximum_fusion
  393.7 4.8 pad_maximum_fusion.1
  398.5 1.7 copy-done.4
  400.2 3.8 pad_maximum_fusion.2
  404.0 0.6 copy-done.6
  404.6 0.6 dynamic-slice.3
  405.9 498.6 %all-reduce.6.cloned.1.call-done = (f32[16,2,256,256]{3,2,0,1:T(8,128)}, f32[16,2,256,256]{3,2,0,1:T(8,128)}, f32[16,2,256,256]{3,2,0,1:T(8,128)}) async-done(((f32[16,2,256,256]{3,2,0,1:T(8,128)}, f32[16,2,256,256]{3,2,0,1:T(8,128)}, f32[16,2,256,256]{3,2,0,1:T(8,128)}), (f32[16,2,256,256]{3,2,0,1:T(8,128)}, f32[16,2,256,256]{3,2,0,1:T(8,128)}, f32[16,2,256,256]{3,2,0,1:T(8,128)})) %all-reduce.6.cloned.1.call-update) | async-done | bytes 25165840
  904.4 1.3 fusion.12
  905.8 1.3 fusion.13
  907.1 1.3 fusion.14
  908.7 2.1 copy.20
  (19 shorter events, 0.3 us)
Async XLA Ops:
  19.0 9.4 %copy-start.5 = (s32[3,16]{1,0:T(4,128)S(1)}, s32[3,16]{1,0:T(4,128)}, u32[]{:S(2)}) copy-start(s32[3,16]{1,0:T(4,128)} %param.3) | copy-start | bytes 580
  19.0 113.0 %all-to-all-start = ((bf16[16,14,2,16,512]{4,3,2,1,0:T(8,128)(2,1)}), bf16[16,14,2,16,512]{4,3,2,1,0:T(8,128)(2,1)}, u32[]{:S(2)}, u32[]{:S(2)}) async-start(bf16[16,14,2,16,512]{4,3,2,1,0:T(8,128)(2,1)} %reshape_reshape_reshape.3), calls=%async_computation | async-start | bytes 14680064 | tf_op jit(solution)/shard_map/all_to_all | solution.py:31
  137.8 62.1 %all-to-all-start.1 = ((bf16[16,14,16,512]{3,2,1,0:T(8,128)(2,1)}), bf16[16,14,16,512]{3,2,1,0:T(8,128)(2,1)}, u32[]{:S(2)}, u32[]{:S(2)}) async-start(bf16[16,14,16,512]{3,2,1,0:T(8,128)(2,1)} %gather_fusion), calls=%async_computation.1 | async-start | bytes 7340032 | tf_op jit(solution)/shard_map/all_to_all | solution.py:35
  199.9 60.1 %all-to-all-start.2 = ((bf16[16,14,16,512]{3,2,1,0:T(8,128)(2,1)}), bf16[16,14,16,512]{3,2,1,0:T(8,128)(2,1)}, u32[]{:S(2)}, u32[]{:S(2)}) async-start(bf16[16,14,16,512]{3,2,1,0:T(8,128)(2,1)} %gather_fusion.1), calls=%async_computation.2 | async-start | bytes 7340032 | tf_op jit(solution)/shard_map/all_to_all | solution.py:35
  260.0 97.9 %all-to-all-start.3 = ((bf16[16,14,16,512]{3,2,1,0:T(8,128)(2,1)}), bf16[16,14,16,512]{3,2,1,0:T(8,128)(2,1)}, u32[]{:S(2)}, u32[]{:S(2)}) async-start(bf16[16,14,16,512]{3,2,1,0:T(8,128)(2,1)} %gather_fusion.2), calls=%async_computation.3 | async-start | bytes 7340032 | tf_op jit(solution)/shard_map/all_to_all | solution.py:35
  272.4 632.0 %all-reduce.6.cloned.1.call-start = ((), (), s32[]{:S(2)}) async-start(), calls=%async_computation.4 | async-start | bytes 50331648
  376.3 10.8 %copy-start = (f32[16,1,256,256]{3,2,0,1:T(8,128)S(1)}, f32[16,1,256,256]{3,2,0,1:T(8,128)}, u32[]{:S(2)}) copy-start(f32[16,1,256,256]{3,2,0,1:T(8,128)} %get-tuple-element.8) | copy-start | bytes 12582916
  387.1 6.6 copy-start.1
  387.1 6.6 copy-start.2
  393.7 4.8 copy-start.3
  393.7 6.5 copy-start.4
  404.0 0.7 copy-start.6
Sparse Core Ops, SparseCore 0:
  404.1 500.2 all-reduce.5
where the time goes:
time: 922 us; the launch traced here: 918 us
  waiting for transfers between devices  686 us (74%)
  local copies, waits for them, and re-layouts  57.4 us (6%)
  matrix products  54.3 us (6%)
  other arithmetic  51.4 us (6%)
  starting transfers between devices  48.5 us (5%)
  between operations  19.9 us (2%)
    unnamed x2, waiting for transfers between devices  499 us
    all_to_all x1, waiting for transfers between devices, per_device(): lax.all_to_all(pieces, 'chan', split_axis=0, concat_axis=0, tiled=True)  104 us
    all_to_all x3, waiting for transfers between devices, per_device(): lax.all_to_all(outgoing, 'chan', split_axis=0, concat_axis=0, tiled=True)  84 us
    dot_general x3, matrix products, cross_terms(): jnp.einsum('wfa,wfb->fab', own_half, partner_half, preferred_element_type...  54.3 us
    another operation x6, other arithmetic, cross_terms(): return jnp.stack([real_part, imag_part], axis=1)  47.2 us
    all_to_all x3, starting transfers between devices, per_device(): lax.all_to_all(outgoing, 'chan', split_axis=0, concat_axis=0, tiled=True)  39.1 us
  transfers between devices with their start and end apart: 5, of which 4 were waited for; matrix products, arithmetic and copies ran while one was open for 10% of the time, Pallas kernels for 0%

commit v1 on v0

v1 whole, which is shorter than its diff:
```python
import math

import jax
import jax.numpy as jnp
from jax import lax
from jax.sharding import PartitionSpec as P


def per_device(spectra, partner):
    window_count, bins, _, _, width = spectra.shape
    blocks = lax.axis_size("chan")
    groups = lax.axis_size("tm")
    position = lax.axis_index("chan")
    rounds = partner.shape[0]
    half_bins = bins // 2
    mine_bins = half_bins // groups
    halves = (jnp.arange(blocks, dtype=jnp.int32)[None, :] > partner).astype(jnp.int32)
    arranged = spectra.reshape(window_count, 2, groups, mine_bins, 2 * width)
    arranged = arranged.transpose(2, 1, 3, 0, 4)
    gathered = lax.all_to_all(arranged, "tm", split_axis=0, concat_axis=0, tiled=True)
    share = window_count * groups // blocks
    shares = gathered.reshape(groups, 2, mine_bins, blocks // groups, share, 2 * width)
    shares = shares.transpose(0, 3, 1, 2, 4, 5).reshape(blocks, 2, mine_bins, share, 2 * width)
    holdings = lax.all_to_all(shares, "chan", split_axis=0, concat_axis=0, tiled=True)
    scale = 1.0 / math.sqrt(window_count * groups)
    results = []
    for r in range(rounds):
        outgoing = holdings[partner[r], halves[r]]
        incoming = lax.all_to_all(outgoing, "chan", split_axis=0, concat_axis=0, tiled=True)
        own = lax.dynamic_index_in_dim(shares, halves[r][position], 1, keepdims=False)
        product = jnp.einsum("jfwa,jfwb->fab", own, incoming, preferred_element_type=jnp.float32)
        real_part = product[:, :width, :width] + product[:, width:, width:]
        imag_part = product[:, width:, :width] - product[:, :width, width:]
        results.append(jnp.stack([real_part, imag_part], axis=1) * scale)
    return jnp.stack(results)[:, None]


def solution(mesh):
    placed = (P("tm", None, "chan", None, None), P())
    return jax.shard_map(
        per_device,
        mesh=mesh,
        in_specs=placed,
        out_specs=P(None, "chan", "tm", None, None, None),
        check_vma=False,
    )
```

time: 922 us -> 437 us (0.47)
  waiting for transfers between devices: 686 us -> 210 us
  blocking collectives: 0 us -> 88.4 us
  other arithmetic: 51.4 us -> 6.54 us
  matrix products: 54.3 us -> 14.7 us
  between operations: 19.9 us -> 5.97 us
    unnamed x2 -> x0, waiting for transfers between devices: 499 us -> none
    all_to_all x0 -> x1, blocking collectives: none -> 88.4 us  [per_device(): lax.all_to_all(arranged, 'tm', split_axis=0, concat_axis=0, tiled=True)]
    another operation x9 -> x3, other arithmetic: 51.2 us -> 0.4 us  [per_device(): results.append(jnp.stack([real_part, imag_part], axis=1) * scale)]
    dot_general x3, matrix products: 54.3 us -> 14.7 us  [per_device(): jnp.einsum('jfwa,jfwb->fab', own, incoming, preferred_element_type=jnp.fl...]
    another operation x2 -> x0, local copies, waits for them, and re-layouts: 25.3 us -> none  [the longest x1 12.9 us: per_device(): arranged = flat.reshape(window_count, 2, half_bins, 2 * width)]
    all_to_all x3, waiting for transfers between devices: 84 us -> 107 us  [per_device(): lax.all_to_all(outgoing, 'chan', split_axis=0, concat_axis=0, tiled=True)]
    reshape x0 -> x1, local copies, waits for them, and re-layouts: none -> 19.1 us  [per_device(): arranged = spectra.reshape(window_count, 2, groups, mine_bins, 2 * width)]
  transfers between devices with their start and end apart: 5 -> 4, of which waited for: 4 -> 4; matrix products, arithmetic and copies ran while one was open for 10% -> 7% of each run, Pallas kernels for 0% -> 0%
where the time goes in v1:
time: 437 us; the launch traced here: 432 us
  waiting for transfers between devices  210 us (48%)
  blocking collectives  88.4 us (20%)
  local copies, waits for them, and re-layouts  57.6 us (13%)
  starting transfers between devices  49.2 us (11%)
  matrix products  14.7 us (3%)
  other arithmetic  6.54 us (1%)
  between operations  5.97 us (1%)
    all_to_all x3, waiting for transfers between devices, per_device(): lax.all_to_all(outgoing, 'chan', split_axis=0, concat_axis=0, tiled=True)  107 us
    all_to_all x1, waiting for transfers between devices, per_device(): lax.all_to_all(shares, 'chan', split_axis=0, concat_axis=0, tiled=True)  104 us
    all_to_all x1, blocking collectives, per_device(): lax.all_to_all(arranged, 'tm', split_axis=0, concat_axis=0, tiled=True)  88.4 us
    all_to_all x3, starting transfers between devices, per_device(): lax.all_to_all(outgoing, 'chan', split_axis=0, concat_axis=0, tiled=True)  39.1 us
    reshape x1, local copies, waits for them, and re-layouts, per_device(): arranged = spectra.reshape(window_count, 2, groups, mine_bins, 2 * width)  19.1 us
    gather x3, local copies, waits for them, and re-layouts, per_device(): outgoing = holdings[partner[r], halves[r]]  17.1 us
    dot_general x3, matrix products, per_device(): jnp.einsum('jfwa,jfwb->fab', own, incoming, preferred_element_type=jnp.fl...  14.7 us
    all_to_all x1, starting transfers between devices, per_device(): lax.all_to_all(shares, 'chan', split_axis=0, concat_axis=0, tiled=True)  10.1 us
  transfers between devices with their start and end apart: 4, of which 4 were waited for; matrix products, arithmetic and copies ran while one was open for 7% of the time, Pallas kernels for 0%

profile of v1, /device:TPU:1, one launch (start us, length us, event | category | flops | bytes accessed | tf_op | source)
XLA Modules:
  0.0 432.4 jit_solution(15354527521994183342)
XLA Ops:
  0.0 19.1 %reshape.297 = bf16[224,2,8,2,512]{4,3,2,1,0:T(2,128)(2,1)} reshape(bf16[224,32,1,2,256]{4,3,2,1,0:T(2,128)(2,1)} %param.2) | data formatting | bytes 14680064 | tf_op jit(solution)/shard_map/reshape | solution.py:18
  19.1 7.2 %copy.65 = bf16[224,2,8,2,512]{4,0,3,1,2:T(8,128)(2,1)S(1)} copy(bf16[224,2,8,2,512]{4,3,2,1,0:T(2,128)(2,1)} %reshape.297) | data formatting | bytes 14680064 | tf_op jit(solution)/shard_map/transpose | solution.py:19
  26.3 88.4 %all_to_all.25 = bf16[8,2,2,224,512]{4,3,2,1,0:T(8,128)(2,1)S(1)} all-to-all(bf16[8,2,2,224,512]{4,3,2,1,0:T(8,128)(2,1)S(1)} %bitcast.78), channel_id=1, replica_groups=mesh['chan'=16,'tm'=8] {'tm'}, dimensions={0} | all-to-all | bytes 14680064 | tf_op jit(solution)/shard_map/all_to_all | solution.py:20
  114.8 2.4 fusion.52
  117.1 5.6 %pad_maximum_fusion = bf16[8,4,2,112,512]{4,3,2,1,0:T(8,128)(2,1)} fusion(bf16[8,2,2,112,512]{4,3,2,1,0:T(8,128)(2,1)} %get-tuple-element.9, bf16[8,2,2,112,512]{4,3,2,1,0:T(8,128)(2,1)S(1)} %get-tuple-element.8), kind=kLoop, calls=%fused_computation.3 | loop fusion | flops 3670016 | bytes 14680064 | tf_op jit(solution)/shard_map/concatenate
  122.7 0.0 copy-start
  122.7 10.1 %all-to-all-start.1 = ((bf16[16,2,2,112,512]{4,3,2,1,0:T(8,128)(2,1)}), bf16[16,2,2,112,512]{4,3,2,1,0:T(8,128)(2,1)}, u32[]{:S(2)}, u32[]{:S(2)}) async-start(bf16[16,2,2,112,512]{4,3,2,1,0:T(8,128)(2,1)} %bitcast.76), calls=%async_computation.1 | async-start | bytes 14680064 | tf_op jit(solution)/shard_map/all_to_all | solution.py:24
  132.8 0.0 copy-done
  132.9 103.5 %all-to-all-done.1 = bf16[16,2,2,112,512]{4,3,2,1,0:T(8,128)(2,1)} async-done(((bf16[16,2,2,112,512]{4,3,2,1,0:T(8,128)(2,1)}), bf16[16,2,2,112,512]{4,3,2,1,0:T(8,128)(2,1)}, u32[]{:S(2)}, u32[]{:S(2)}) %all-to-all-start.1) | async-done | bytes 7340064 | tf_op jit(solution)/shard_map/all_to_all | solution.py:24
  236.4 5.7 %gather_fusion = bf16[16,2,112,512]{3,2,1,0:T(8,128)(2,1)} fusion(bf16[16,2,2,112,512]{4,3,2,1,0:T(8,128)(2,1)} %all-to-all-done.1, s32[16]{0:T(128)S(1)} %get-tuple-element.16), kind=kCustom, calls=%fused_computation | custom fusion | bytes 7340160 | tf_op jit(solution)/shard_map/gather | solution.py:28
  242.1 14.4 %all-to-all-start.2 = ((bf16[16,2,112,512]{3,2,1,0:T(8,128)(2,1)}), bf16[16,2,112,512]{3,2,1,0:T(8,128)(2,1)}, u32[]{:S(2)}, u32[]{:S(2)}) async-start(bf16[16,2,112,512]{3,2,1,0:T(8,128)(2,1)} %gather_fusion), calls=%async_computation.2 | async-start | bytes 7340032 | tf_op jit(solution)/shard_map/all_to_all | solution.py:29
  256.4 5.7 %gather_fusion.1 = bf16[16,2,112,512]{3,2,1,0:T(8,128)(2,1)} fusion(bf16[16,2,2,112,512]{4,3,2,1,0:T(8,128)(2,1)} %all-to-all-done.1, s32[16]{0:T(128)S(1)} %get-tuple-element.18), kind=kCustom, calls=%fused_computation.1 | custom fusion | bytes 7340160 | tf_op jit(solution)/shard_map/gather | solution.py:28
  262.1 42.1 %all-to-all-done.2 = bf16[16,2,112,512]{3,2,1,0:T(8,128)(2,1)} async-done(((bf16[16,2,112,512]{3,2,1,0:T(8,128)(2,1)}), bf16[16,2,112,512]{3,2,1,0:T(8,128)(2,1)}, u32[]{:S(2)}, u32[]{:S(2)}) %all-to-all-start.2) | async-done | bytes 3670048 | tf_op jit(solution)/shard_map/all_to_all | solution.py:29
  304.2 12.4 %all-to-all-start.3 = ((bf16[16,2,112,512]{3,2,1,0:T(8,128)(2,1)}), bf16[16,2,112,512]{3,2,1,0:T(8,128)(2,1)}, u32[]{:S(2)}, u32[]{:S(2)}) async-start(bf16[16,2,112,512]{3,2,1,0:T(8,128)(2,1)} %gather_fusion.1), calls=%async_computation.3 | async-start | bytes 7340032 | tf_op jit(solution)/shard_map/all_to_all | solution.py:29
  316.6 5.7 %gather_fusion.2 = bf16[16,2,112,512]{3,2,1,0:T(8,128)(2,1)} fusion(bf16[16,2,2,112,512]{4,3,2,1,0:T(8,128)(2,1)} %all-to-all-done.1, s32[16]{0:T(128)S(1)} %get-tuple-element.17), kind=kCustom, calls=%fused_computation.2 | custom fusion | bytes 7340160 | tf_op jit(solution)/shard_map/gather | solution.py:28
  322.3 42.0 %all-to-all-done.3 = bf16[16,2,112,512]{3,2,1,0:T(8,128)(2,1)} async-done(((bf16[16,2,112,512]{3,2,1,0:T(8,128)(2,1)}), bf16[16,2,112,512]{3,2,1,0:T(8,128)(2,1)}, u32[]{:S(2)}, u32[]{:S(2)}) %all-to-all-start.3) | async-done | bytes 3670048 | tf_op jit(solution)/shard_map/all_to_all | solution.py:29
  364.3 12.4 %all-to-all-start.4 = ((bf16[16,2,112,512]{3,2,1,0:T(8,128)(2,1)}), bf16[16,2,112,512]{3,2,1,0:T(8,128)(2,1)}, u32[]{:S(2)}, u32[]{:S(2)}) async-start(bf16[16,2,112,512]{3,2,1,0:T(8,128)(2,1)} %gather_fusion.2), calls=%async_computation.4 | async-start | bytes 7340032 | tf_op jit(solution)/shard_map/all_to_all | solution.py:29
  376.7 0.7 constant_dynamic-slice_fusion.1
  380.0 0.6 constant_dynamic-slice_fusion.5
  383.8 8.5 %constant_dynamic-slice_fusion.4 = (bf16[16,1,2,112,512]{4,3,2,1,0:T(8,128)(2,1)}, bf16[16,1,2,112,512]{4,3,2,1,0:T(8,128)(2,1)}, bf16[16,1,2,112,512]{4,3,2,1,0:T(8,128)(2,1)S(1)}) fusion(bf16[16,2,2,112,512]{4,3,2,1,0:T(8,128)(2,1)} %bitcast.77, s32[]{:T(128)S(6)} %select_n.76, s32[]{:T(128)S(6)} %select_n.82, s32[]{:T(128)S(6)} %select_n.79), kind=kLoop, calls=%fused_computation.48 | loop fusion | bytes 22020108 | tf_op jit(solution)/shard_map/jit(dynamic_index_in_dim)/dynamic_slice | solution.py:30
  392.3 5.3 %fusion.12 = f32[2,512,512]{2,1,0:T(8,128)S(1)} fusion(bf16[16,2,112,512]{3,2,1,0:T(8,128)(2,1)} %all-to-all-done.2, bf16[16,1,2,112,512]{4,3,2,1,0:T(8,128)(2,1)} %get-tuple-element.5), kind=kOutput, calls=%fused_computation.18 | convolution fusion | flops 1879048192 | bytes 9437184 | tf_op jit(solution)/shard_map/jfwa,jfwb->fab/dot_general | solution.py:31
  397.6 0.1 fusion.32
  397.7 4.2 fusion.17
  401.9 0.1 fusion.30
  402.0 22.4 %all-to-all-done.4 = bf16[16,2,112,512]{3,2,1,0:T(8,128)(2,1)} async-done(((bf16[16,2,112,512]{3,2,1,0:T(8,128)(2,1)}), bf16[16,2,112,512]{3,2,1,0:T(8,128)(2,1)}, u32[]{:S(2)}, u32[]{:S(2)}) %all-to-all-start.4) | async-done | bytes 3670048 | tf_op jit(solution)/shard_map/all_to_all | solution.py:29
  424.4 5.3 %fusion.22 = f32[2,512,512]{2,1,0:T(8,128)S(1)} fusion(bf16[16,2,112,512]{3,2,1,0:T(8,128)(2,1)} %all-to-all-done.4, bf16[16,1,2,112,512]{4,3,2,1,0:T(8,128)(2,1)} %get-tuple-element.6), kind=kOutput, calls=%fused_computation.20 | convolution fusion | flops 1879048192 | bytes 9437184 | tf_op jit(solution)/shard_map/jfwa,jfwb->fab/dot_general | solution.py:31
  429.7 0.1 fusion.28
  429.8 0.1 maximum_multiply_fusion
  429.9 0.1 maximum_multiply_fusion.1
  430.1 0.1 maximum_multiply_fusion.2
  430.2 0.2 maximum_bitcast_fusion
  430.4 2.1 copy.28
  (3 shorter events, 0.0 us)
Async XLA Ops:
  122.7 10.1 %copy-start = (s32[3,16]{1,0:T(4,128)S(1)}, s32[3,16]{1,0:T(4,128)}, u32[]{:S(2)}) copy-start(s32[3,16]{1,0:T(4,128)} %param.3) | copy-start | bytes 580
  122.7 113.7 %all-to-all-start.1 = ((bf16[16,2,2,112,512]{4,3,2,1,0:T(8,128)(2,1)}), bf16[16,2,2,112,512]{4,3,2,1,0:T(8,128)(2,1)}, u32[]{:S(2)}, u32[]{:S(2)}) async-start(bf16[16,2,2,112,512]{4,3,2,1,0:T(8,128)(2,1)} %bitcast.76), calls=%async_computation.1 | async-start | bytes 14680064 | tf_op jit(solution)/shard_map/all_to_all | solution.py:24
  242.1 62.1 %all-to-all-start.2 = ((bf16[16,2,112,512]{3,2,1,0:T(8,128)(2,1)}), bf16[16,2,112,512]{3,2,1,0:T(8,128)(2,1)}, u32[]{:S(2)}, u32[]{:S(2)}) async-start(bf16[16,2,112,512]{3,2,1,0:T(8,128)(2,1)} %gather_fusion), calls=%async_computation.2 | async-start | bytes 7340032 | tf_op jit(solution)/shard_map/all_to_all | solution.py:29
  304.2 60.1 %all-to-all-start.3 = ((bf16[16,2,112,512]{3,2,1,0:T(8,128)(2,1)}), bf16[16,2,112,512]{3,2,1,0:T(8,128)(2,1)}, u32[]{:S(2)}, u32[]{:S(2)}) async-start(bf16[16,2,112,512]{3,2,1,0:T(8,128)(2,1)} %gather_fusion.1), calls=%async_computation.3 | async-start | bytes 7340032 | tf_op jit(solution)/shard_map/all_to_all | solution.py:29
  364.3 60.1 %all-to-all-start.4 = ((bf16[16,2,112,512]{3,2,1,0:T(8,128)(2,1)}), bf16[16,2,112,512]{3,2,1,0:T(8,128)(2,1)}, u32[]{:S(2)}, u32[]{:S(2)}) async-start(bf16[16,2,112,512]{3,2,1,0:T(8,128)(2,1)} %gather_fusion.2), calls=%async_computation.4 | async-start | bytes 7340032 | tf_op jit(solution)/shard_map/all_to_all | solution.py:29

commit v2 on v1

v2 whole, which is shorter than its diff:
```python
import functools
import math

import jax
import jax.numpy as jnp
from jax import lax
from jax.experimental import pallas as pl
from jax.experimental.pallas import tpu as pltpu
from jax.sharding import Mesh, PartitionSpec as P


ALL = ("xh", "z", "core", "xl", "y")
ZC = ("z", "core")
XY = ("xh", "xl", "y")
LANES = 128


def pack_kernel(groups, src, dst, buf, in_sem, out_sem):
    quarters, quarter, bins = buf.shape[:3]
    per = bins // 2 // groups

    def load(s):
        return pltpu.make_async_copy(src.at[pl.ds(s * quarter, quarter), :, 0], buf.at[s], in_sem.at[s])

    for s in range(quarters):
        load(s).start()
    for s in range(quarters):
        load(s).wait()
        for b in range(bins):
            h, rest = b // (bins // 2), b % (bins // 2)
            u, e = rest // per, rest % per
            for lh in range(buf.shape[-1] // LANES):
                pltpu.make_async_copy(
                    buf.at[s, :, b, :, pl.ds(lh * LANES, LANES)],
                    dst.at[s // 2, s % 2, e, lh, u, h],
                    out_sem.at[s],
                ).start()
    for s in range(quarters):
        pltpu.make_async_copy(src.at[pl.ds(s * quarter, quarter), :, 0], buf.at[s], out_sem.at[s]).wait()


def pack(spectra, groups):
    windows, bins, _, parts, width = spectra.shape
    quarter = windows // 4
    per, sides = bins // 2 // groups, width // LANES
    return pl.pallas_call(
        functools.partial(pack_kernel, groups),
        out_shape=jax.ShapeDtypeStruct((2, 2, per, sides, groups, 2, quarter, parts, LANES), spectra.dtype),
        in_specs=[pl.BlockSpec(memory_space=pl.ANY)],
        out_specs=pl.BlockSpec(memory_space=pl.ANY),
        scratch_shapes=[
            pltpu.VMEM((4, quarter, bins, parts, width), spectra.dtype),
            pltpu.SemaphoreType.DMA((4,)),
            pltpu.SemaphoreType.DMA((4,)),
        ],
        cost_estimate=pl.CostEstimate(flops=0, transcendentals=0, bytes_accessed=4 * spectra.size),
        name="pack",
    )(spectra)


def pick_kernel(blocks_ref, halves_ref, src, dst, buf, in_sem, out_sem):
    count = buf.shape[0]

    def load(i):
        return pltpu.make_async_copy(src.at[blocks_ref[i], :, halves_ref[i]], buf.at[i], in_sem.at[i])

    def store(i):
        return pltpu.make_async_copy(buf.at[i], dst.at[i], out_sem.at[i])

    for i in range(count):
        load(i).start()
    for i in range(count):
        load(i).wait()
        store(i).start()
    for i in range(count):
        store(i).wait()


def pick(holdings, chosen, halves):
    _, groups, _, rows, lanes = holdings.shape
    count = chosen.shape[0]
    shape = (count, groups, rows, lanes)
    return pl.pallas_call(
        pick_kernel,
        out_shape=jax.ShapeDtypeStruct(shape, holdings.dtype),
        grid_spec=pltpu.PrefetchScalarGridSpec(
            num_scalar_prefetch=2,
            grid=(),
            in_specs=[pl.BlockSpec(memory_space=pl.ANY)],
            out_specs=pl.BlockSpec(memory_space=pl.ANY),
            scratch_shapes=[
                pltpu.VMEM(shape, holdings.dtype),
                pltpu.SemaphoreType.DMA((count,)),
                pltpu.SemaphoreType.DMA((count,)),
            ],
        ),
        cost_estimate=pl.CostEstimate(flops=0, transcendentals=0, bytes_accessed=4 * math.prod(shape)),
        name="pick",
    )(chosen, halves, holdings)


def cross_kernel(where_ref, own_ref, other_ref, out_ref):
    groups, quarters, sides, rows, lanes = own_ref.shape
    depth = groups * rows
    odd = lax.broadcasted_iota(jnp.int32, (depth // 8, 8, lanes * sides), 1) % 2 == 1
    real = None
    for q in range(quarters):
        a = jnp.concatenate([own_ref[:, q, s].reshape(depth, lanes) for s in range(sides)], axis=1)
        b = jnp.concatenate([other_ref[q, s].reshape(depth, lanes) for s in range(sides)], axis=1)
        tall = b.astype(jnp.float32).reshape(depth // 8, 8, lanes * sides)
        turned = jnp.where(odd, pltpu.roll(tall, 1, 1), -pltpu.roll(tall, 7, 1))
        turned = turned.reshape(depth, lanes * sides).astype(b.dtype)
        dims = (((0,), (0,)), ((), ()))
        re = lax.dot_general(a, b, dims, preferred_element_type=jnp.float32)
        im = lax.dot_general(a, turned, dims, preferred_element_type=jnp.float32)
        real, imag = (re, im) if real is None else (real + re, imag + im)
    out_ref[0, 0] = real
    out_ref[0, 1] = imag


def cross(own, other, half, turn):
    groups, quarters, mine, sides, _, rows, lanes = own.shape
    width = sides * lanes
    read = groups * quarters * mine * sides * rows * lanes * 2
    return pl.pallas_call(
        cross_kernel,
        out_shape=jax.ShapeDtypeStruct((mine, 2, width, width), jnp.float32),
        grid_spec=pltpu.PrefetchScalarGridSpec(
            num_scalar_prefetch=1,
            grid=(mine,),
            in_specs=[
                pl.BlockSpec(
                    (groups, quarters, None, sides, None, rows, lanes),
                    lambda e, w: (0, 0, e, 0, w[0], 0, 0),
                ),
                pl.BlockSpec(
                    (quarters, None, sides, None, groups, rows, lanes), lambda e, w: (0, e, 0, w[1], 0, 0, 0)
                ),
            ],
            out_specs=pl.BlockSpec((1, 2, width, width), lambda e, w: (e, 0, 0, 0)),
        ),
        cost_estimate=pl.CostEstimate(
            flops=4 * groups * quarters * rows * width * width * mine,
            transcendentals=0,
            bytes_accessed=2 * read + mine * 2 * width * width * 4,
        ),
        name="cross",
    )(jnp.stack([half, jnp.int32(turn)]), own, other)


HOPS = [(1, 0, 0), (1, 1, 0), (1, 1, 1), (1, 1, 3), (1, 0, 1), (1, 0, 3), (1, 1, 2), (1, 0, 2)]
HOPS += [(0, 1, 0), (0, 0, 1), (0, 0, 3), (0, 1, 1), (0, 1, 3), (0, 0, 2), (0, 1, 2)]


def per_device(spectra, partner):
    windows, bins, _, parts, width = spectra.shape
    nl, ny = lax.axis_size("xl"), lax.axis_size("y")
    groups = nl * ny
    lanes, sides = LANES, width // LANES
    inner = lax.axis_size("z") * lax.axis_size("core")
    blocks = 2 * inner
    plane, xl, y = lax.axis_index("xh"), lax.axis_index("xl"), lax.axis_index("y")
    column = lax.axis_index(ZC)
    rounds = partner.shape[0]
    mine = bins // 2 // groups
    rows = windows // 4 * parts
    halves = (jnp.arange(blocks, dtype=jnp.int32)[None, :] > partner).astype(jnp.int32)

    joint = pack(spectra, groups).reshape(blocks * groups, 2, rows, lanes)
    holdings = lax.all_to_all(joint, ALL, split_axis=0, concat_axis=0, tiled=True)
    holdings = holdings.reshape(blocks, groups, 2, rows, lanes)

    def fetch(side):
        first = side * inner
        chosen = lax.dynamic_slice_in_dim(partner, first, inner, 1).T.reshape(-1)
        wanted = lax.dynamic_slice_in_dim(halves, first, inner, 1).T.reshape(-1)
        outgoing = pick(holdings, chosen, wanted).reshape(inner, rounds, groups, rows, lanes)
        incoming = lax.all_to_all(outgoing, ZC, split_axis=0, concat_axis=0, tiled=True)
        return incoming.reshape(2, mine, sides, rounds, groups, rows, lanes)

    away_other = fetch(1 - plane)
    kept_other = fetch(plane)

    by_plane = joint.reshape(2, inner, groups, 2, rows, lanes)
    own = [jnp.zeros((groups, inner, 2, rows, lanes), spectra.dtype) for _ in range(2)]

    def piece(fx, fl, dy):
        start = (plane ^ fx, 0, (xl ^ fl) * ny + (y + dy) % ny, 0, 0, 0)
        return lax.dynamic_slice(by_plane, start, (1, inner, 1, 2, rows, lanes)).reshape(1, inner, 2, rows, lanes)

    def put(part, fx, fl, dy):
        slot = (xl ^ fl) * ny + (y - dy) % ny
        own[fx] = lax.dynamic_update_slice(own[fx], part, (slot, 0, 0, 0, 0))

    put(piece(0, 0, 0), 0, 0, 0)
    for fx, fl, dy in HOPS:
        table = [
            ((cx * nl + cl) * ny + cy, ((cx ^ fx) * nl + (cl ^ fl)) * ny + (cy + dy) % ny)
            for cx in range(2)
            for cl in range(nl)
            for cy in range(ny)
        ]
        part = piece(fx, fl, dy)
        part = lax.ppermute(part, XY, table)
        put(part, fx, fl, dy)
    kept_own, away_own = (o.reshape(groups, 2, mine, sides, 2, rows, lanes) for o in own)

    scale = 1.0 / math.sqrt(windows * groups)
    backs = []
    for r in range(rounds):
        away = cross(away_own, away_other, halves[r][(1 - plane) * inner + column], r)
        backs.append(lax.ppermute(away, "xh", [(0, 1), (1, 0)]))
    results = []
    for r in range(rounds):
        kept = cross(kept_own, kept_other, halves[r][plane * inner + column], r)
        results.append((kept + backs[r]) * scale)
    return jnp.stack(results)[:, None]


def solution(mesh):
    fine = Mesh(mesh.devices.reshape(2, 4, 2, 2, 4), ALL)
    chan, tm = ("xh", "z", "core"), ("xl", "y")

    return jax.shard_map(
        per_device,
        mesh=fine,
        in_specs=(P(tm, None, chan, None, None), P()),
        out_specs=P(None, chan, tm, None, None, None),
        check_vma=False,
    )
```

time: 437 us -> 385 us (0.88)
  blocking collectives: 88.4 us -> 0 us
  Pallas kernels: 0 us -> 44.7 us
  waiting for transfers between devices: 210 us -> 242 us
  local copies, waits for them, and re-layouts: 57.6 us -> 30.3 us
  matrix products: 14.7 us -> 0 us
  between operations: 5.97 us -> 0.13 us
  starting transfers between devices: 49.2 us -> 53.9 us
    ppermute x0 -> x18, waiting for transfers between devices: none -> 97 us  [the longest x15 50.3 us: per_device(): part = lax.ppermute(part, XY, table)]
    all_to_all x1 -> x0, blocking collectives: 88.4 us -> none  [per_device(): lax.all_to_all(arranged, 'tm', split_axis=0, concat_axis=0, tiled=True)]
    all_to_all x4 -> x3, waiting for transfers between devices: 210 us -> 145 us  [the longest x1 89.2 us: per_device(): lax.all_to_all(joint, ALL, split_axis=0, concat_axis=0, tiled=True)]
    pallas_call x0 -> x9, Pallas kernels: none -> 44.7 us  [the longest x6 26.8 us: cross(): pl.pallas_call(cross_kernel, out_shape=jax.ShapeDtypeStruct((mine, 2, wid...]
    ppermute x0 -> x18, starting transfers between devices: none -> 29.9 us  [the longest x15 25.8 us: per_device(): part = lax.ppermute(part, XY, table)]
    all_to_all x4 -> x3, starting transfers between devices: 49.2 us -> 23.9 us  [the longest x2 12 us: fetch(): lax.all_to_all(outgoing, ZC, split_axis=0, concat_axis=0, tiled=True)]
    gather x3 -> x0, local copies, waits for them, and re-layouts: 17.1 us -> none  [per_device(): outgoing = holdings[partner[r], halves[r]]]
    dynamic_update_slice x0 -> x16, local copies, waits for them, and re-layouts: none -> 15 us  [put(): own[fx] = lax.dynamic_update_slice(own[fx], part, (slot, 0, 0, 0, 0))]
  transfers between devices with their start and end apart: 4 -> 21, of which waited for: 4 -> 10; matrix products, arithmetic and copies ran while one was open for 7% -> 10% of each run, Pallas kernels for 0% -> 9%
where the time goes in v2:
time: 385 us; the launch traced here: 381 us
  waiting for transfers between devices  242 us (63%)
  starting transfers between devices  53.9 us (14%)
  Pallas kernels  44.7 us (12%)
  local copies, waits for them, and re-layouts  30.3 us (8%)
  other arithmetic  10.7 us (3%)
    all_to_all x1, waiting for transfers between devices, per_device(): lax.all_to_all(joint, ALL, split_axis=0, concat_axis=0, tiled=True)  89.2 us
    all_to_all x2, waiting for transfers between devices, fetch(): lax.all_to_all(outgoing, ZC, split_axis=0, concat_axis=0, tiled=True)  55.6 us
    ppermute x15, waiting for transfers between devices, per_device(): part = lax.ppermute(part, XY, table)  50.3 us
    ppermute x3, waiting for transfers between devices, per_device(): backs.append(lax.ppermute(away, 'xh', [(0, 1), (1, 0)]))  46.7 us
    pallas_call x6, Pallas kernels, cross(): pl.pallas_call(cross_kernel, out_shape=jax.ShapeDtypeStruct((mine, 2, wid...  26.8 us
    ppermute x15, starting transfers between devices, per_device(): part = lax.ppermute(part, XY, table)  25.8 us
    dynamic_update_slice x16, local copies, waits for them, and re-layouts, put(): own[fx] = lax.dynamic_update_slice(own[fx], part, (slot, 0, 0, 0, 0))  15 us
    all_to_all x2, starting transfers between devices, fetch(): lax.all_to_all(outgoing, ZC, split_axis=0, concat_axis=0, tiled=True)  12 us
  transfers between devices with their start and end apart: 21, of which 10 were waited for; matrix products, arithmetic and copies ran while one was open for 10% of the time, Pallas kernels for 9%

profile of v2, /device:TPU:1, one launch (start us, length us, event | category | flops | bytes accessed | tf_op | source)
XLA Modules:
  0.0 381.3 jit_solution(5796772912311694357)
XLA Ops:
  0.0 6.1 %pack.1 = bf16[2,2,2,2,8,2,56,2,128]{8,7,6,5,4,3,2,1,0:T(2,128)(2,1)} custom-call(bf16[224,32,1,2,256]{4,3,2,1,0:T(2,128)(2,1)} %src.1), custom_call_target="tpu_custom_call" | custom-call | bytes 14680064 | tf_op jit(solution)/shard_map/pack/pallas_call | solution.py:46
  6.2 11.9 %all-to-all-start = ((bf16[128,2,112,128]{3,2,1,0:T(8,128)(2,1)}), bf16[128,2,112,128]{3,2,1,0:T(8,128)(2,1)}, u32[]{:S(2)}, u32[]{:S(2)}) async-start(bf16[128,2,112,128]{3,2,1,0:T(8,128)(2,1)} %bitcast.65), calls=%async_computation | async-start | bytes 14680064 | tf_op jit(solution)/shard_map/all_to_all | solution.py:170
  19.6 89.2 %all-to-all-done = bf16[128,2,112,128]{3,2,1,0:T(8,128)(2,1)} async-done(((bf16[128,2,112,128]{3,2,1,0:T(8,128)(2,1)}), bf16[128,2,112,128]{3,2,1,0:T(8,128)(2,1)}, u32[]{:S(2)}, u32[]{:S(2)}) %all-to-all-start) | async-done | bytes 7340064 | tf_op jit(solution)/shard_map/all_to_all | solution.py:170
  108.8 5.9 %pick.3 = bf16[24,8,112,128]{3,2,1,0:T(8,128)(2,1)} custom-call(s32[24]{0:T(128)} %reshape.114.blocks_ref, s32[24]{0:T(128)} %reshape.115.halves_ref, bf16[16,8,2,112,128]{4,3,2,1,0:T(8,128)(2,1)} %bitcast.14.src), custom_call_target="tpu_custom_call" | custom-call | bytes 11010048 | tf_op jit(solution)/shard_map/pick/pallas_call | solution.py:83
  114.7 6.5 %all-to-all-start.2 = ((bf16[8,3,8,112,128]{4,3,2,1,0:T(8,128)(2,1)}), bf16[8,3,8,112,128]{4,3,2,1,0:T(8,128)(2,1)}, u32[]{:S(2)}, u32[]{:S(2)}) async-start(bf16[8,3,8,112,128]{4,3,2,1,0:T(8,128)(2,1)} %bitcast.69), calls=%async_computation.2 | async-start | bytes 11010048 | tf_op jit(solution)/shard_map/all_to_all | solution.py:178
  122.5 5.9 %pick.2 = bf16[24,8,112,128]{3,2,1,0:T(8,128)(2,1)} custom-call(s32[24]{0:T(128)} %reshape.99.blocks_ref, s32[24]{0:T(128)} %reshape.100.halves_ref, bf16[16,8,2,112,128]{4,3,2,1,0:T(8,128)(2,1)} %bitcast.14.src), custom_call_target="tpu_custom_call" | custom-call | bytes 11010048 | tf_op jit(solution)/shard_map/pick/pallas_call | solution.py:83
  128.4 55.5 %all-to-all-done.2 = bf16[8,3,8,112,128]{4,3,2,1,0:T(8,128)(2,1)} async-done(((bf16[8,3,8,112,128]{4,3,2,1,0:T(8,128)(2,1)}), bf16[8,3,8,112,128]{4,3,2,1,0:T(8,128)(2,1)}, u32[]{:S(2)}, u32[]{:S(2)}) %all-to-all-start.2) | async-done | bytes 5505056 | tf_op jit(solution)/shard_map/all_to_all | solution.py:178
  184.0 5.6 %all-to-all-start.1 = ((bf16[8,3,8,112,128]{4,3,2,1,0:T(8,128)(2,1)}), bf16[8,3,8,112,128]{4,3,2,1,0:T(8,128)(2,1)}, u32[]{:S(2)}, u32[]{:S(2)}) async-start(bf16[8,3,8,112,128]{4,3,2,1,0:T(8,128)(2,1)} %bitcast.68), calls=%async_computation.1 | async-start | bytes 11010048 | tf_op jit(solution)/shard_map/all_to_all | solution.py:178
  189.5 5.6 %dynamic-slice_bitcast_fusion = (bf16[1,8,2,112,128]{4,3,2,1,0:T(8,128)(2,1)S(1)}, bf16[1,8,2,112,128]{4,3,2,1,0:T(8,128)(2,1)}, bf16[1,8,2,112,128]{4,3,2,1,0:T...) fusion(bf16[2,8,8,2,112,128]{5,4,3,2,1,0:T(8,128)(2,1)} %bitcas, ...), kind=kLoop, calls=%fused_computation.5 | loop fusion | bytes 13762600 | tf_op jit(solution)/shard_map/reshape | solution.py:189
  195.1 2.1 collective-permute-start
  197.2 2.7 collective-permute-start.2
  199.9 3.0 collective-permute-start.7
  206.1 2.0 pad_add_fusion
  208.1 2.4 broadcast.13.clone
  218.1 2.6 collective-permute-done.7
  221.7 2.4 broadcast.13.clone.1
  227.2 3.7 collective-permute-start.12
  231.7 22.7 %collective-permute-done.9 = bf16[1,8,2,112,128]{4,3,2,1,0:T(8,128)(2,1)S(1)} collective-permute-done((bf16[1,8,2,112,128]{4,3,2,1,0:T(8,128)(2,1)S(1)}, bf16[1,8,2,112,128]{4,3,2,1,0:T(8,128)(2,1)S(1)}, u32[]{:S(2)}, u32[]{:S(2)}) %collective-permute-start.9) | collective-permute-done | bytes 458784 | tf_op jit(solution)/shard_map/ppermute | solution.py:204
  255.7 7.3 %collective-permute-done.10 = bf16[1,8,2,112,128]{4,3,2,1,0:T(8,128)(2,1)S(1)} collective-permute-done((bf16[1,8,2,112,128]{4,3,2,1,0:T(8,128)(2,1)S(1)}, bf16[1,8,2,112,128]{4,3,2,1,0:T(8,128)(2,1)S(1)}, u32[]{:S(2)}, u32[]{:S(2)}) %collective-permute-start.10) | collective-permute-done | bytes 458784 | tf_op jit(solution)/shard_map/ppermute | solution.py:204
  264.5 4.1 %collective-permute-start.3 = (bf16[1,8,2,112,128]{4,3,2,1,0:T(8,128)(2,1)}, bf16[1,8,2,112,128]{4,3,2,1,0:T(8,128)(2,1)S(1)}, u32[]{:S(2)}, u32[]{:S(2)}) collective-permute-start(bf16[1,8,2,112,128]{4,3,2,1,0:T(8,128)(2,1)} %get-tuple-element.16), channel_id=1, source_target_pairs={{0,5},{1,6},{2,7},{3,4},{4,1},{5,2},{6,3},{7,0},{64,69},{65,70},{6... | collective-permute-start | bytes 1376264 | tf_op jit(solution)/shard_map/ppermute | solution.py:204
  270.3 17.6 %collective-permute-done.13 = bf16[1,8,2,112,128]{4,3,2,1,0:T(8,128)(2,1)S(1)} collective-permute-done((bf16[1,8,2,112,128]{4,3,2,1,0:T(8,128)(2,1)}, bf16[1,8,2,112,128]{4,3,2,1,0:T(8,128)(2,1)S(1)}, u32[]{:S(2)}, u32[]{:S(2)}) %collective-permute-start.13) | collective-permute-done | bytes 458784 | tf_op jit(solution)/shard_map/ppermute | solution.py:204
  287.9 5.5 %collective-permute-start.5 = (bf16[1,8,2,112,128]{4,3,2,1,0:T(8,128)(2,1)}, bf16[1,8,2,112,128]{4,3,2,1,0:T(8,128)(2,1)S(1)}, u32[]{:S(2)}, u32[]{:S(2)}) collective-permute-start(bf16[1,8,2,112,128]{4,3,2,1,0:T(8,128)(2,1)} %get-tuple-element.14), channel_id=1, source_target_pairs={{0,2},{1,3},{2,0},{3,1},{4,6},{5,7},{6,4},{7,5},{64,66},{65,67},{6... | collective-permute-start | bytes 1376264 | tf_op jit(solution)/shard_map/ppermute | solution.py:204
  295.0 4.4 %cross.11 = f32[2,2,256,256]{3,2,1,0:T(8,128)} custom-call(s32[2]{0:T(128)} %pad_add_fusion.4.where_ref, bf16[8,2,2,2,2,112,128]{6,5,4,3,2,1,0:T(8,128)(2,1)} %bitcast.26.own_ref, bf16[2,2,2,3,8,112,128]{6,5,4,3,2,1,0:T(8,128)(2,1)} %bitcast.30.other_ref), custom_call_target="tpu_custom_call" | custom-call | flops 939524096 | bytes 4718592 | tf_op jit(solution)/shard_map/cross/pallas_call | solution.py:125
  301.3 4.4 %cross.9 = f32[2,2,256,256]{3,2,1,0:T(8,128)} custom-call(s32[2]{0:T(128)} %get-tuple-element.34.where_ref, bf16[8,2,2,2,2,112,128]{6,5,4,3,2,1,0:T(8,128)(2,1)} %bitcast.26.own_ref, bf16[2,2,2,3,8,112,128]{6,5,4,3,2,1,0:T(8,128)(2,1)} %bitcast.30.other_ref), custom_call_target="tpu_custom_call" | custom-call | flops 939524096 | bytes 4718592 | tf_op jit(solution)/shard_map/cross/pallas_call | solution.py:125
  310.3 4.4 %cross.7 = f32[2,2,256,256]{3,2,1,0:T(8,128)} custom-call(s32[2]{0:T(128)} %get-tuple-element.33.where_ref, bf16[8,2,2,2,2,112,128]{6,5,4,3,2,1,0:T(8,128)(2,1)} %bitcast.26.own_ref, bf16[2,2,2,3,8,112,128]{6,5,4,3,2,1,0:T(8,128)(2,1)} %bitcast.30.other_ref), custom_call_target="tpu_custom_call" | custom-call | flops 939524096 | bytes 4718592 | tf_op jit(solution)/shard_map/cross/pallas_call | solution.py:125
  317.5 4.4 %cross.10 = f32[2,2,256,256]{3,2,1,0:T(8,128)} custom-call(s32[2]{0:T(128)} %pad_add_fusion.5.where_ref, bf16[8,2,2,2,2,112,128]{6,5,4,3,2,1,0:T(8,128)(2,1)} %bitcast.10.own_ref, bf16[2,2,2,3,8,112,128]{6,5,4,3,2,1,0:T(8,128)(2,1)} %bitcast.16.other_ref), custom_call_target="tpu_custom_call" | custom-call | flops 939524096 | bytes 4718592 | tf_op jit(solution)/shard_map/cross/pallas_call | solution.py:125
  321.9 4.4 %cross.8 = f32[2,2,256,256]{3,2,1,0:T(8,128)} custom-call(s32[2]{0:T(128)} %pad_add_fusion.3.where_ref, bf16[8,2,2,2,2,112,128]{6,5,4,3,2,1,0:T(8,128)(2,1)} %bitcast.10.own_ref, bf16[2,2,2,3,8,112,128]{6,5,4,3,2,1,0:T(8,128)(2,1)} %bitcast.16.other_ref), custom_call_target="tpu_custom_call" | custom-call | flops 939524096 | bytes 4718592 | tf_op jit(solution)/shard_map/cross/pallas_call | solution.py:125
  326.4 4.6 %cross.6 = f32[2,2,256,256]{3,2,1,0:T(8,128)} custom-call(s32[2]{0:T(128)} %pad_add_fusion.1.where_ref, bf16[8,2,2,2,2,112,128]{6,5,4,3,2,1,0:T(8,128)(2,1)} %bitcast.10.own_ref, bf16[2,2,2,3,8,112,128]{6,5,4,3,2,1,0:T(8,128)(2,1)} %bitcast.16.other_ref), custom_call_target="tpu_custom_call" | custom-call | flops 939524096 | bytes 4718592 | tf_op jit(solution)/shard_map/cross/pallas_call | solution.py:125
  330.9 1.9 collective-permute-done.17
  333.0 22.3 %collective-permute-done.16 = f32[2,2,256,256]{3,2,1,0:T(8,128)S(1)} collective-permute-done((f32[2,2,256,256]{3,2,1,0:T(8,128)}, f32[2,2,256,256]{3,2,1,0:T(8,128)S(1)}, u32[]{:S(2)}, u32[]{:S(2)}) %collective-permute-start.16) | collective-permute-done | bytes 1048608 | tf_op jit(solution)/shard_map/ppermute | solution.py:212
  355.4 22.4 %collective-permute-done.15 = f32[2,2,256,256]{3,2,1,0:T(8,128)} collective-permute-done((f32[2,2,256,256]{3,2,1,0:T(8,128)}, f32[2,2,256,256]{3,2,1,0:T(8,128)}, u32[]{:S(2)}, u32[]{:S(2)}) %collective-permute-start.15) | collective-permute-done | bytes 1048608 | tf_op jit(solution)/shard_map/ppermute | solution.py:212
  379.2 2.1 maximum_bitcast_fusion
  (73 shorter events, 35.5 us)
Async XLA Ops:
  6.1 11.9 %copy-start.5 = (s32[3,16]{1,0:T(4,128)S(1)}, s32[3,16]{1,0:T(4,128)}, u32[]{:S(2)}) copy-start(s32[3,16]{1,0:T(4,128)} %param.3) | copy-start | bytes 580
  6.2 102.6 %all-to-all-start = ((bf16[128,2,112,128]{3,2,1,0:T(8,128)(2,1)}), bf16[128,2,112,128]{3,2,1,0:T(8,128)(2,1)}, u32[]{:S(2)}, u32[]{:S(2)}) async-start(bf16[128,2,112,128]{3,2,1,0:T(8,128)(2,1)} %bitcast.65), calls=%async_computation | async-start | bytes 14680064 | tf_op jit(solution)/shard_map/all_to_all | solution.py:170
  114.7 69.3 %all-to-all-start.2 = ((bf16[8,3,8,112,128]{4,3,2,1,0:T(8,128)(2,1)}), bf16[8,3,8,112,128]{4,3,2,1,0:T(8,128)(2,1)}, u32[]{:S(2)}, u32[]{:S(2)}) async-start(bf16[8,3,8,112,128]{4,3,2,1,0:T(8,128)(2,1)} %bitcast.69), calls=%async_computation.2 | async-start | bytes 11010048 | tf_op jit(solution)/shard_map/all_to_all | solution.py:178
  184.0 133.5 %all-to-all-start.1 = ((bf16[8,3,8,112,128]{4,3,2,1,0:T(8,128)(2,1)}), bf16[8,3,8,112,128]{4,3,2,1,0:T(8,128)(2,1)}, u32[]{:S(2)}, u32[]{:S(2)}) async-start(bf16[8,3,8,112,128]{4,3,2,1,0:T(8,128)(2,1)} %bitcast.68), calls=%async_computation.1 | async-start | bytes 11010048 | tf_op jit(solution)/shard_map/all_to_all | solution.py:178
  195.1 21.0 %collective-permute-start = (bf16[1,8,2,112,128]{4,3,2,1,0:T(8,128)(2,1)}, bf16[1,8,2,112,128]{4,3,2,1,0:T(8,128)(2,1)S(1)}, u32[]{:S(2)}, u32[]{:S(2)}) collective-permute-start(bf16[1,8,2,112,128]{4,3,2,1,0:T(8,128)(2,1)} %get-tuple-element.19), channel_id=1, source_target_pairs={{0,4},{1,5},{2,6},{3,7},{4,0},{5,1},{6,2},{7,3},{64,68},{65,69},{6... | collective-permute-start | bytes 1376264 | tf_op jit(solution)/shard_map/ppermute | solution.py:204
  197.2 29.9 %collective-permute-start.1 = (bf16[1,8,2,112,128]{4,3,2,1,0:T(8,128)(2,1)}, bf16[1,8,2,112,128]{4,3,2,1,0:T(8,128)(2,1)S(1)}, u32[]{:S(2)}, u32[]{:S(2)}) collective-permute-start(bf16[1,8,2,112,128]{4,3,2,1,0:T(8,128)(2,1)} %get-tuple-element.18), channel_id=1, source_target_pairs={{0,1},{1,2},{2,3},{3,0},{4,5},{5,6},{6,7},{7,4},{64,65},{65,66},{6... | collective-permute-start | bytes 1376264 | tf_op jit(solution)/shard_map/ppermute | solution.py:204
  197.2 102.2 %collective-permute-start.2 = (bf16[1,8,2,112,128]{4,3,2,1,0:T(8,128)(2,1)}, bf16[1,8,2,112,128]{4,3,2,1,0:T(8,128)(2,1)S(1)}, u32[]{:S(2)}, u32[]{:S(2)}) collective-permute-start(bf16[1,8,2,112,128]{4,3,2,1,0:T(8,128)(2,1)} %get-tuple-element.17), channel_id=1, source_target_pairs={{0,3},{1,0},{2,1},{3,2},{4,7},{5,4},{6,5},{7,6},{64,67},{65,64},{6... | collective-permute-start | bytes 1376264 | tf_op jit(solution)/shard_map/ppermute | solution.py:204
  199.9 20.8 %collective-permute-start.7 = (bf16[1,8,2,112,128]{4,3,2,1,0:T(8,128)(2,1)}, bf16[1,8,2,112,128]{4,3,2,1,0:T(8,128)(2,1)S(1)}, u32[]{:S(2)}, u32[]{:S(2)}) collective-permute-start(bf16[1,8,2,112,128]{4,3,2,1,0:T(8,128)(2,1)} %get-tuple-element.12), channel_id=1, source_target_pairs={{0,64},{1,65},{2,66},{3,67},{4,68},{5,69},{6,70},{7,71},{64,0},{65... | collective-permute-start | bytes 1376264 | tf_op jit(solution)/shard_map/ppermute | solution.py:204
  202.9 22.1 %collective-permute-start.8 = (bf16[1,8,2,112,128]{4,3,2,1,0:T(8,128)(2,1)}, bf16[1,8,2,112,128]{4,3,2,1,0:T(8,128)(2,1)S(1)}, u32[]{:S(2)}, u32[]{:S(2)}) collective-permute-start(bf16[1,8,2,112,128]{4,3,2,1,0:T(8,128)(2,1)} %get-tuple-element.11), channel_id=1, source_target_pairs={{0,68},{1,69},{2,70},{3,71},{4,64},{5,65},{6,66},{7,67},{64,4},{65... | collective-permute-start | bytes 1376264 | tf_op jit(solution)/shard_map/ppermute | solution.py:204
  202.9 13.2 %copy-start.4 = (bf16[1,8,2,112,128]{4,3,2,1,0:T(8,128)(2,1)S(1)}, bf16[1,8,2,112,128]{4,3,2,1,0:T(8,128)(2,1)}, u32[]{:S(2)}) copy-start(bf16[1,8,2,112,128]{4,3,2,1,0:T(8,128)(2,1)} %get-tuple-element.10) | copy-start | bytes 1376260
  202.9 17.8 %copy-start.3 = (bf16[1,8,2,112,128]{4,3,2,1,0:T(8,128)(2,1)S(1)}, bf16[1,8,2,112,128]{4,3,2,1,0:T(8,128)(2,1)}, u32[]{:S(2)}) copy-start(bf16[1,8,2,112,128]{4,3,2,1,0:T(8,128)(2,1)} %get-tuple-element.9) | copy-start | bytes 1376260
  216.1 38.3 %collective-permute-start.9 = (bf16[1,8,2,112,128]{4,3,2,1,0:T(8,128)(2,1)S(1)}, bf16[1,8,2,112,128]{4,3,2,1,0:T(8,128)(2,1)S(1)}, u32[]{:S(2)}, u32[]{:S(2)}) collective-permute-start(bf16[1,8,2,112,128]{4,3,2,1,0:T(8,128)(2,1)S(1)} %copy-done.4), channel_id=1, source_target_pairs={{0,69},{1,70},{2,71},{3,68},{4,65},{5,66},{6,67},{7,64},{64,5},{65... | collective-permute-start | bytes 1376264 | tf_op jit(solution)/shard_map/ppermute | solution.py:204
  220.7 42.3 %collective-permute-start.10 = (bf16[1,8,2,112,128]{4,3,2,1,0:T(8,128)(2,1)S(1)}, bf16[1,8,2,112,128]{4,3,2,1,0:T(8,128)(2,1)S(1)}, u32[]{:S(2)}, u32[]{:S(2)}) collective-permute-start(bf16[1,8,2,112,128]{4,3,2,1,0:T(8,128)(2,1)S(1)} %copy-done.3), channel_id=1, source_target_pairs={{0,71},{1,68},{2,69},{3,70},{4,67},{5,64},{6,65},{7,66},{64,7},{65... | collective-permute-start | bytes 1376264 | tf_op jit(solution)/shard_map/ppermute | solution.py:204
  225.0 39.6 %collective-permute-start.11 = (bf16[1,8,2,112,128]{4,3,2,1,0:T(8,128)(2,1)S(1)}, bf16[1,8,2,112,128]{4,3,2,1,0:T(8,128)(2,1)S(1)}, u32[]{:S(2)}, u32[]{:S(2)}) collective-permute-start(bf16[1,8,2,112,128]{4,3,2,1,0:T(8,128)(2,1)S(1)} %get-tuple-element.8), channel_id=1, source_target_pairs={{0,65},{1,66},{2,67},{3,64},{4,69},{5,70},{6,71},{7,68},{64,1},{65... | collective-permute-start | bytes 1376264 | tf_op jit(solution)/shard_map/ppermute | solution.py:204
  227.2 42.3 %collective-permute-start.12 = (bf16[1,8,2,112,128]{4,3,2,1,0:T(8,128)(2,1)}, bf16[1,8,2,112,128]{4,3,2,1,0:T(8,128)(2,1)S(1)}, u32[]{:S(2)}, u32[]{:S(2)}) collective-permute-start(bf16[1,8,2,112,128]{4,3,2,1,0:T(8,128)(2,1)} %get-tuple-element.7), channel_id=1, source_target_pairs={{0,67},{1,64},{2,65},{3,66},{4,71},{5,68},{6,69},{7,70},{64,3},{65... | collective-permute-start | bytes 1376264 | tf_op jit(solution)/shard_map/ppermute | solution.py:204
  254.4 33.5 %collective-permute-start.13 = (bf16[1,8,2,112,128]{4,3,2,1,0:T(8,128)(2,1)}, bf16[1,8,2,112,128]{4,3,2,1,0:T(8,128)(2,1)S(1)}, u32[]{:S(2)}, u32[]{:S(2)}) collective-permute-start(bf16[1,8,2,112,128]{4,3,2,1,0:T(8,128)(2,1)} %get-tuple-element.6), channel_id=1, source_target_pairs={{0,70},{1,71},{2,68},{3,69},{4,66},{5,67},{6,64},{7,65},{64,6},{65... | collective-permute-start | bytes 1376264 | tf_op jit(solution)/shard_map/ppermute | solution.py:204
  263.0 31.2 %collective-permute-start.14 = (bf16[1,8,2,112,128]{4,3,2,1,0:T(8,128)(2,1)S(1)}, bf16[1,8,2,112,128]{4,3,2,1,0:T(8,128)(2,1)S(1)}, u32[]{:S(2)}, u32[]{:S(2)}) collective-permute-start(bf16[1,8,2,112,128]{4,3,2,1,0:T(8,128)(2,1)S(1)} %get-tuple-element.5), channel_id=1, source_target_pairs={{0,66},{1,67},{2,64},{3,65},{4,70},{5,71},{6,68},{7,69},{64,2},{65... | collective-permute-start | bytes 1376264 | tf_op jit(solution)/shard_map/ppermute | solution.py:204
  264.5 41.2 %collective-permute-start.3 = (bf16[1,8,2,112,128]{4,3,2,1,0:T(8,128)(2,1)}, bf16[1,8,2,112,128]{4,3,2,1,0:T(8,128)(2,1)S(1)}, u32[]{:S(2)}, u32[]{:S(2)}) collective-permute-start(bf16[1,8,2,112,128]{4,3,2,1,0:T(8,128)(2,1)} %get-tuple-element.16), channel_id=1, source_target_pairs={{0,5},{1,6},{2,7},{3,4},{4,1},{5,2},{6,3},{7,0},{64,69},{65,70},{6... | collective-permute-start | bytes 1376264 | tf_op jit(solution)/shard_map/ppermute | solution.py:204
  269.5 39.0 %collective-permute-start.4 = (bf16[1,8,2,112,128]{4,3,2,1,0:T(8,128)(2,1)}, bf16[1,8,2,112,128]{4,3,2,1,0:T(8,128)(2,1)}, u32[]{:S(2)}, u32[]{:S(2)}) collective-permute-start(bf16[1,8,2,112,128]{4,3,2,1,0:T(8,128)(2,1)} %get-tuple-element.15), channel_id=1, source_target_pairs={{0,7},{1,4},{2,5},{3,6},{4,3},{5,0},{6,1},{7,2},{64,71},{65,68},{6... | collective-permute-start | bytes 1376264 | tf_op jit(solution)/shard_map/ppermute | solution.py:204
  287.9 28.0 %collective-permute-start.5 = (bf16[1,8,2,112,128]{4,3,2,1,0:T(8,128)(2,1)}, bf16[1,8,2,112,128]{4,3,2,1,0:T(8,128)(2,1)S(1)}, u32[]{:S(2)}, u32[]{:S(2)}) collective-permute-start(bf16[1,8,2,112,128]{4,3,2,1,0:T(8,128)(2,1)} %get-tuple-element.14), channel_id=1, source_target_pairs={{0,2},{1,3},{2,0},{3,1},{4,6},{5,7},{6,4},{7,5},{64,66},{65,67},{6... | collective-permute-start | bytes 1376264 | tf_op jit(solution)/shard_map/ppermute | solution.py:204
  294.2 22.5 %collective-permute-start.6 = (bf16[1,8,2,112,128]{4,3,2,1,0:T(8,128)(2,1)}, bf16[1,8,2,112,128]{4,3,2,1,0:T(8,128)(2,1)S(1)}, u32[]{:S(2)}, u32[]{:S(2)}) collective-permute-start(bf16[1,8,2,112,128]{4,3,2,1,0:T(8,128)(2,1)} %get-tuple-element.13), channel_id=1, source_target_pairs={{0,6},{1,7},{2,4},{3,5},{4,2},{5,3},{6,0},{7,1},{64,70},{65,71},{6... | collective-permute-start | bytes 1376264 | tf_op jit(solution)/shard_map/ppermute | solution.py:204
  299.4 33.4 %collective-permute-start.17 = (f32[2,2,256,256]{3,2,1,0:T(8,128)}, f32[2,2,256,256]{3,2,1,0:T(8,128)S(1)}, u32[]{:S(2)}, u32[]{:S(2)}) collective-permute-start(f32[2,2,256,256]{3,2,1,0:T(8,128)} %cross.11), channel_id=1, source_target_pairs={{0,64},{64,0},{1,65},{65,1},{2,66},{66,2},{3,67},{67,3},{4,68},{68... | collective-permute-start | bytes 3145736 | tf_op jit(solution)/shard_map/ppermute | solution.py:212
  305.8 49.5 %collective-permute-start.16 = (f32[2,2,256,256]{3,2,1,0:T(8,128)}, f32[2,2,256,256]{3,2,1,0:T(8,128)S(1)}, u32[]{:S(2)}, u32[]{:S(2)}) collective-permute-start(f32[2,2,256,256]{3,2,1,0:T(8,128)} %cross.9), channel_id=1, source_target_pairs={{0,64},{64,0},{1,65},{65,1},{2,66},{66,2},{3,67},{67,3},{4,68},{68... | collective-permute-start | bytes 3145736 | tf_op jit(solution)/shard_map/ppermute | solution.py:212
  314.7 63.2 %collective-permute-start.15 = (f32[2,2,256,256]{3,2,1,0:T(8,128)}, f32[2,2,256,256]{3,2,1,0:T(8,128)}, u32[]{:S(2)}, u32[]{:S(2)}) collective-permute-start(f32[2,2,256,256]{3,2,1,0:T(8,128)} %cross.7), channel_id=1, source_target_pairs={{0,64},{64,0},{1,65},{65,1},{2,66},{66,2},{3,67},{67,3},{4,68},{68... | collective-permute-start | bytes 3145736 | tf_op jit(solution)/shard_map/ppermute | solution.py:212
  326.4 6.5 %copy-start.2 = (f32[2,2,256,256]{3,2,1,0:T(8,128)S(1)}, f32[2,2,256,256]{3,2,1,0:T(8,128)}, u32[]{:S(2)}) copy-start(f32[2,2,256,256]{3,2,1,0:T(8,128)} %cross.10) | copy-start | bytes 3145732
  330.9 24.4 %copy-start.1 = (f32[2,2,256,256]{3,2,1,0:T(8,128)S(1)}, f32[2,2,256,256]{3,2,1,0:T(8,128)}, u32[]{:S(2)}) copy-start(f32[2,2,256,256]{3,2,1,0:T(8,128)} %cross.8) | copy-start | bytes 3145732
  330.9 47.0 %copy-start = (f32[2,2,256,256]{3,2,1,0:T(8,128)S(1)}, f32[2,2,256,256]{3,2,1,0:T(8,128)}, u32[]{:S(2)}) copy-start(f32[2,2,256,256]{3,2,1,0:T(8,128)} %cross.6) | copy-start | bytes 3145732

commit v3 on v2

--- a/solution.py
+++ b/solution.py
@@ -99,8 +99,13 @@
     )(chosen, halves, holdings)
 
 
-def cross_kernel(where_ref, own_ref, other_ref, out_ref):
+def cross_kernel(fused, scale, slots_ref, wanted_ref, *refs):
+    count = slots_ref.shape[0]
+    pieces, other_ref = refs[:count], refs[count]
+    out_ref, own_ref = refs[-2:]
     groups, quarters, sides, rows, lanes = own_ref.shape
+    for k in range(count):
+        own_ref[slots_ref[k]] = pieces[k][...]
     depth = groups * rows
     odd = lax.broadcasted_iota(jnp.int32, (depth // 8, 8, lanes * sides), 1) % 2 == 1
     real = None
@@ -114,38 +119,71 @@
         re = lax.dot_general(a, b, dims, preferred_element_type=jnp.float32)
         im = lax.dot_general(a, turned, dims, preferred_element_type=jnp.float32)
         real, imag = (re, im) if real is None else (real + re, imag + im)
+    if fused:
+        back_ref = refs[count + 1]
+        real, imag = (real + back_ref[0, 0]) * scale, (imag + back_ref[0, 1]) * scale
     out_ref[0, 0] = real
     out_ref[0, 1] = imag
 
 
-def cross(own, other, half, turn):
-    groups, quarters, mine, sides, _, rows, lanes = own.shape
+def cross(pieces, slots, wanted, other, turn, back=None, scale=None, out=None):
+    groups = len(pieces)
+    quarters, mine, sides, _, rows, lanes = pieces[0].shape
+    rounds = other.shape[3]
     width = sides * lanes
     read = groups * quarters * mine * sides * rows * lanes * 2
-    return pl.pallas_call(
-        cross_kernel,
-        out_shape=jax.ShapeDtypeStruct((mine, 2, width, width), jnp.float32),
+    piece = pl.BlockSpec((quarters, None, sides, None, rows, lanes), lambda e, n, w: (0, e, 0, w[turn], 0, 0))
+    in_specs = [piece] * groups
+    in_specs += [pl.BlockSpec((quarters, None, sides, None, groups, rows, lanes), lambda e, n, w: (0, e, 0, turn, 0, 0, 0))]
+    one = pl.BlockSpec((1, 2, width, width), lambda e, n, w: (e, 0, 0, 0))
+    operands = [slots, wanted, *pieces, other]
+    out_spec, shape, aliases = one, (mine, 2, width, width), {}
+    if back is not None:
+        operands.append(back)
+        in_specs.append(one)
+        out_spec = pl.BlockSpec((None, None, 1, 2, width, width), lambda e, n, w: (turn, 0, e, 0, 0, 0))
+        shape = (rounds, 1, mine, 2, width, width)
+        if out is not None:
+            aliases = {len(operands): 0}
+            operands.append(out)
+            in_specs.append(pl.BlockSpec(memory_space=pl.ANY))
+    return pl.pallas_call(
+        functools.partial(cross_kernel, back is not None, scale),
+        out_shape=jax.ShapeDtypeStruct(shape, jnp.float32),
         grid_spec=pltpu.PrefetchScalarGridSpec(
-            num_scalar_prefetch=1,
+            num_scalar_prefetch=2,
             grid=(mine,),
-            in_specs=[
-                pl.BlockSpec(
-                    (groups, quarters, None, sides, None, rows, lanes),
-                    lambda e, w: (0, 0, e, 0, w[0], 0, 0),
-                ),
-                pl.BlockSpec(
-                    (quarters, None, sides, None, groups, rows, lanes), lambda e, w: (0, e, 0, w[1], 0, 0, 0)
-                ),
-            ],
-            out_specs=pl.BlockSpec((1, 2, width, width), lambda e, w: (e, 0, 0, 0)),
+            in_specs=in_specs,
+            out_specs=out_spec,
+            scratch_shapes=[pltpu.VMEM((groups, quarters, sides, rows, lanes), pieces[0].dtype)],
         ),
+        input_output_aliases=aliases,
         cost_estimate=pl.CostEstimate(
             flops=4 * groups * quarters * rows * width * width * mine,
             transcendentals=0,
             bytes_accessed=2 * read + mine * 2 * width * width * 4,
         ),
         name="cross",
-    )(jnp.stack([half, jnp.int32(turn)]), own, other)
+    )(*operands)
+
+
+def settle_kernel(scale, kept_ref, back_ref, before_ref, out_ref):
+    out_ref[...] = (kept_ref[...] + back_ref[...]) * scale
+
+
+def settle(kept, back, out, turn, scale):
+    mine, _, width, _ = kept.shape
+    one = pl.BlockSpec((1, 2, width, width), lambda e: (e, 0, 0, 0))
+    return pl.pallas_call(
+        functools.partial(settle_kernel, scale),
+        out_shape=jax.ShapeDtypeStruct(out.shape, out.dtype),
+        grid=(mine,),
+        in_specs=[one, one, pl.BlockSpec(memory_space=pl.ANY)],
+        out_specs=pl.BlockSpec((None, None, 1, 2, width, width), lambda e: (turn, 0, e, 0, 0, 0)),
+        input_output_aliases={2: 0},
+        cost_estimate=pl.CostEstimate(flops=2 * kept.size, transcendentals=0, bytes_accessed=12 * kept.size),
+        name="settle",
+    )(kept, back, out)
 
 
 HOPS = [(1, 0, 0), (1, 1, 0), (1, 1, 1), (1, 1, 3), (1, 0, 1), (1, 0, 3), (1, 1, 2), (1, 0, 2)]
@@ -182,17 +220,14 @@
     kept_other = fetch(plane)
 
     by_plane = joint.reshape(2, inner, groups, 2, rows, lanes)
-    own = [jnp.zeros((groups, inner, 2, rows, lanes), spectra.dtype) for _ in range(2)]
+    shape = (2, mine, sides, 2, rows, lanes)
 
     def piece(fx, fl, dy):
         start = (plane ^ fx, 0, (xl ^ fl) * ny + (y + dy) % ny, 0, 0, 0)
-        return lax.dynamic_slice(by_plane, start, (1, inner, 1, 2, rows, lanes)).reshape(1, inner, 2, rows, lanes)
-
-    def put(part, fx, fl, dy):
-        slot = (xl ^ fl) * ny + (y - dy) % ny
-        own[fx] = lax.dynamic_update_slice(own[fx], part, (slot, 0, 0, 0, 0))
-
-    put(piece(0, 0, 0), 0, 0, 0)
+        part = lax.dynamic_slice(by_plane, start, (1, inner, 1, 2, rows, lanes))
+        return part.reshape(inner, 2, rows, lanes)
+
+    own = [[piece(0, 0, 0).reshape(shape)], []]
     for fx, fl, dy in HOPS:
         table = [
             ((cx * nl + cl) * ny + cy, ((cx ^ fx) * nl + (cl ^ fl)) * ny + (cy + dy) % ny)
@@ -202,19 +237,22 @@
         ]
         part = piece(fx, fl, dy)
         part = lax.ppermute(part, XY, table)
-        put(part, fx, fl, dy)
-    kept_own, away_own = (o.reshape(groups, 2, mine, sides, 2, rows, lanes) for o in own)
+        own[fx].append(part.reshape(shape))
+    places = [jnp.array([fl * ny for g, fl, _ in order if g == fx]) for fx, order in ((0, [(0, 0, 0)] + HOPS), (1, HOPS))]
+    steps = [jnp.array([dy for g, _, dy in order if g == fx]) for fx, order in ((0, [(0, 0, 0)] + HOPS), (1, HOPS))]
+    slots = [((xl * ny) ^ p) + (y - s) % ny for p, s in zip(places, steps)]
+    wanted = [lax.dynamic_index_in_dim(halves, (plane ^ fx) * inner + column, 1, keepdims=False) for fx in range(2)]
 
     scale = 1.0 / math.sqrt(windows * groups)
     backs = []
     for r in range(rounds):
-        away = cross(away_own, away_other, halves[r][(1 - plane) * inner + column], r)
+        away = cross(own[1], slots[1], wanted[1], away_other, r)
         backs.append(lax.ppermute(away, "xh", [(0, 1), (1, 0)]))
-    results = []
-    for r in range(rounds):
-        kept = cross(kept_own, kept_other, halves[r][plane * inner + column], r)
-        results.append((kept + backs[r]) * scale)
-    return jnp.stack(results)[:, None]
+    last = cross(own[0], slots[0], wanted[0], kept_other, rounds - 1)
+    out = None
+    for r in range(rounds - 1):
+        out = cross(own[0], slots[0], wanted[0], kept_other, r, backs[r], scale, out)
+    return settle(last, backs[-1], out, rounds - 1, scale)
 
 
 def solution(mesh):

time: 385 us -> 395 us (1.026)
  waiting for transfers between devices: 242 us -> 276 us
  local copies, waits for them, and re-layouts: 30.3 us -> 13.3 us
  other arithmetic: 10.7 us -> 1.17 us
  Pallas kernels: 44.7 us -> 49.7 us
    ppermute x15, waiting for transfers between devices: 50.3 us -> 131 us  [per_device(): part = lax.ppermute(part, XY, table)]
    ppermute x3, waiting for transfers between devices: 46.7 us -> 0.01 us  [per_device(): backs.append(lax.ppermute(away, 'xh', [(0, 1), (1, 0)]))]
    dynamic_update_slice x16 -> x0, local copies, waits for them, and re-layouts: 15 us -> none  [put(): own[fx] = lax.dynamic_update_slice(own[fx], part, (slot, 0, 0, 0, 0))]
    another operation x8 -> x0, other arithmetic: 8.6 us -> none  [the longest x5 6.96 us: cross(): jnp.stack([half, jnp.int32(turn)])]
    pallas_call x6 -> x7, Pallas kernels: 26.8 us -> 31.9 us  [the longest x6 29.5 us: cross(): pl.pallas_call(functools.partial(cross_kernel, back is not None, scale),...]
    another operation x2 -> x0, local copies, waits for them, and re-layouts: 4.81 us -> none
  transfers between devices with their start and end apart: 21 -> 21, of which waited for: 10 -> 9; matrix products, arithmetic and copies ran while one was open for 10% -> 3% of each run, Pallas kernels for 9% -> 9%
where the time goes in v3:
time: 395 us
  waiting for transfers between devices  276 us (70%)
  starting transfers between devices  54 us (14%)
  Pallas kernels  49.7 us (13%)
  local copies, waits for them, and re-layouts  13.3 us (3%)
    ppermute x15, waiting for transfers between devices, per_device(): part = lax.ppermute(part, XY, table)  131 us
    all_to_all x1, waiting for transfers between devices, per_device(): lax.all_to_all(joint, ALL, split_axis=0, concat_axis=0, tiled=True)  89.2 us
    all_to_all x2, waiting for transfers between devices, fetch(): lax.all_to_all(outgoing, ZC, split_axis=0, concat_axis=0, tiled=True)  55.6 us
    pallas_call x6, Pallas kernels, cross(): pl.pallas_call(functools.partial(cross_kernel, back is not None, scale),...  29.5 us
    ppermute x15, starting transfers between devices, per_device(): part = lax.ppermute(part, XY, table)  26.6 us
    all_to_all x2, starting transfers between devices, fetch(): lax.all_to_all(outgoing, ZC, split_axis=0, concat_axis=0, tiled=True)  12.1 us
    all_to_all x1, starting transfers between devices, per_device(): lax.all_to_all(joint, ALL, split_axis=0, concat_axis=0, tiled=True)  11.9 us
    pallas_call x2, Pallas kernels, pick(): pl.pallas_call(pick_kernel, out_shape=jax.ShapeDtypeStruct(shape, holding...  11.7 us
  transfers between devices with their start and end apart: 21, of which 9 were waited for; matrix products, arithmetic and copies ran while one was open for 3% of the time, Pallas kernels for 9%

profile of v3, /device:TPU:1, one launch (start us, length us, event | category | flops | bytes accessed | tf_op | source)
XLA Modules:
  0.0 394.5 jit_solution(885306586032690087)
XLA Ops:
  0.0 6.1 %pack.1 = bf16[2,2,2,2,8,2,56,2,128]{8,7,6,5,4,3,2,1,0:T(2,128)(2,1)} custom-call(bf16[224,32,1,2,256]{4,3,2,1,0:T(2,128)(2,1)} %src.1), custom_call_target="tpu_custom_call" | custom-call | bytes 14680064 | tf_op jit(solution)/shard_map/pack/pallas_call | solution.py:46
  6.1 11.9 %all-to-all-start = ((bf16[128,2,112,128]{3,2,1,0:T(8,128)(2,1)}), bf16[128,2,112,128]{3,2,1,0:T(8,128)(2,1)}, u32[]{:S(2)}, u32[]{:S(2)}) async-start(bf16[128,2,112,128]{3,2,1,0:T(8,128)(2,1)} %bitcast.63), calls=%async_computation | async-start | bytes 14680064 | tf_op jit(solution)/shard_map/all_to_all | solution.py:208
  19.5 89.2 %all-to-all-done = bf16[128,2,112,128]{3,2,1,0:T(8,128)(2,1)} async-done(((bf16[128,2,112,128]{3,2,1,0:T(8,128)(2,1)}), bf16[128,2,112,128]{3,2,1,0:T(8,128)(2,1)}, u32[]{:S(2)}, u32[]{:S(2)}) %all-to-all-start) | async-done | bytes 7340064 | tf_op jit(solution)/shard_map/all_to_all | solution.py:208
  108.7 5.9 %pick.3 = bf16[24,8,112,128]{3,2,1,0:T(8,128)(2,1)} custom-call(s32[24]{0:T(128)} %reshape.156.blocks_ref, s32[24]{0:T(128)} %reshape.157.halves_ref, bf16[16,8,2,112,128]{4,3,2,1,0:T(8,128)(2,1)} %bitcast.19.src), custom_call_target="tpu_custom_call" | custom-call | bytes 11010048 | tf_op jit(solution)/shard_map/pick/pallas_call | solution.py:83
  114.6 6.5 %all-to-all-start.2 = ((bf16[8,3,8,112,128]{4,3,2,1,0:T(8,128)(2,1)}), bf16[8,3,8,112,128]{4,3,2,1,0:T(8,128)(2,1)}, u32[]{:S(2)}, u32[]{:S(2)}) async-start(bf16[8,3,8,112,128]{4,3,2,1,0:T(8,128)(2,1)} %bitcast.66), calls=%async_computation.2 | async-start | bytes 11010048 | tf_op jit(solution)/shard_map/all_to_all | solution.py:216
  122.4 5.9 %pick.2 = bf16[24,8,112,128]{3,2,1,0:T(8,128)(2,1)} custom-call(s32[24]{0:T(128)} %reshape.134.blocks_ref, s32[24]{0:T(128)} %reshape.135.halves_ref, bf16[16,8,2,112,128]{4,3,2,1,0:T(8,128)(2,1)} %bitcast.19.src), custom_call_target="tpu_custom_call" | custom-call | bytes 11010048 | tf_op jit(solution)/shard_map/pick/pallas_call | solution.py:83
  128.3 55.6 %all-to-all-done.2 = bf16[8,3,8,112,128]{4,3,2,1,0:T(8,128)(2,1)} async-done(((bf16[8,3,8,112,128]{4,3,2,1,0:T(8,128)(2,1)}), bf16[8,3,8,112,128]{4,3,2,1,0:T(8,128)(2,1)}, u32[]{:S(2)}, u32[]{:S(2)}) %all-to-all-start.2) | async-done | bytes 5505056 | tf_op jit(solution)/shard_map/all_to_all | solution.py:216
  183.9 5.6 %all-to-all-start.1 = ((bf16[8,3,8,112,128]{4,3,2,1,0:T(8,128)(2,1)}), bf16[8,3,8,112,128]{4,3,2,1,0:T(8,128)(2,1)}, u32[]{:S(2)}, u32[]{:S(2)}) async-start(bf16[8,3,8,112,128]{4,3,2,1,0:T(8,128)(2,1)} %bitcast.65), calls=%async_computation.1 | async-start | bytes 11010048 | tf_op jit(solution)/shard_map/all_to_all | solution.py:216
  189.5 5.8 %dynamic-slice_bitcast_fusion = (bf16[8,2,112,128]{3,2,1,0:T(8,128)(2,1)S(1)}, bf16[8,2,112,128]{3,2,1,0:T(8,128)(2,1)S(1)}, bf16[8,2,112,128]{3,2,1,0:T(8,128)(...) fusion(bf16[2,8,8,2,112,128]{5,4,3,2,1,0:T(8,128)(2,1)} %bitcas, ...), kind=kLoop, calls=%fused_computation | loop fusion | bytes 14680104 | tf_op jit(solution)/shard_map/reshape | solution.py:228
  195.3 2.3 collective-permute-start.14
  197.6 4.6 %collective-permute-start.13 = (bf16[8,2,112,128]{3,2,1,0:T(8,128)(2,1)S(1)}, bf16[8,2,112,128]{3,2,1,0:T(8,128)(2,1)S(1)}, u32[]{:S(2)}, u32[]{:S(2)}) collective-permute-start(bf16[8,2,112,128]{3,2,1,0:T(8,128)(2,1)S(1)} %get-tuple-element.10), channel_id=1, source_target_pairs={{0,70},{1,71},{2,68},{3,69},{4,66},{5,67},{6,64},{7,65},{64,6},{65... | collective-permute-start | bytes 1376264 | tf_op jit(solution)/shard_map/ppermute | solution.py:239
  202.6 3.4 collective-permute-start.11
  206.0 3.1 collective-permute-start.10
  209.1 2.0 collective-permute-done.14
  211.8 29.4 %collective-permute-done.13 = bf16[8,2,112,128]{3,2,1,0:T(8,128)(2,1)S(1)} collective-permute-done((bf16[8,2,112,128]{3,2,1,0:T(8,128)(2,1)S(1)}, bf16[8,2,112,128]{3,2,1,0:T(8,128)(2,1)S(1)}, u32[]{:S(2)}, u32[]{:S(2)}) %collective-permute-start.13) | collective-permute-done | bytes 458784 | tf_op jit(solution)/shard_map/ppermute | solution.py:239
  241.1 3.5 collective-permute-start.8
  244.6 2.7 collective-permute-start.6
  247.3 13.3 %collective-permute-done.10 = bf16[8,2,112,128]{3,2,1,0:T(8,128)(2,1)S(1)} collective-permute-done((bf16[8,2,112,128]{3,2,1,0:T(8,128)(2,1)S(1)}, bf16[8,2,112,128]{3,2,1,0:T(8,128)(2,1)S(1)}, u32[]{:S(2)}, u32[]{:S(2)}) %collective-permute-start.10) | collective-permute-done | bytes 458784 | tf_op jit(solution)/shard_map/ppermute | solution.py:239
  262.7 13.5 %collective-permute-done.9 = bf16[8,2,112,128]{3,2,1,0:T(8,128)(2,1)S(1)} collective-permute-done((bf16[8,2,112,128]{3,2,1,0:T(8,128)(2,1)}, bf16[8,2,112,128]{3,2,1,0:T(8,128)(2,1)S(1)}, u32[]{:S(2)}, u32[]{:S(2)}) %collective-permute-start.9) | collective-permute-done | bytes 458784 | tf_op jit(solution)/shard_map/ppermute | solution.py:239
  277.8 8.2 %collective-permute-done.8 = bf16[8,2,112,128]{3,2,1,0:T(8,128)(2,1)S(1)} collective-permute-done((bf16[8,2,112,128]{3,2,1,0:T(8,128)(2,1)}, bf16[8,2,112,128]{3,2,1,0:T(8,128)(2,1)S(1)}, u32[]{:S(2)}, u32[]{:S(2)}) %collective-permute-start.8) | collective-permute-done | bytes 458784 | tf_op jit(solution)/shard_map/ppermute | solution.py:239
  288.7 2.3 collective-permute-start.2
  291.0 4.8 %cross.9 = f32[2,2,256,256]{3,2,1,0:T(8,128)} custom-call(s32[8]{0:T(128)} %get-tuple-element.7.slots_ref, s32[3]{0:T(128)} %get-tuple-element.5.wanted_ref, bf16[2,2,2,2,112,128]{5,4,3,2,1,0:T(8,128)(2,1)} %bitcast.112, bf16[2,2,2,2,112,128]{5,4,3,2,1,0:T(8,128)(2,1)} %bitcast.109, bf16[2,2,2,2,112,128]{5,4,3,2,1,0:T(8,128)(2,1)} %bitcast.106, ...), custom_call_target="tpu_custom_call" | custom-call | flops 939524096 | bytes 4718592 | tf_op jit(solution)/shard_map/cross/pallas_call | solution.py:150
  296.2 4.9 %cross.8 = f32[2,2,256,256]{3,2,1,0:T(8,128)} custom-call(s32[8]{0:T(128)} %get-tuple-element.7.slots_ref, s32[3]{0:T(128)} %get-tuple-element.5.wanted_ref, bf16[2,2,2,2,112,128]{5,4,3,2,1,0:T(8,128)(2,1)} %bitcast.113, bf16[2,2,2,2,112,128]{5,4,3,2,1,0:T(8,128)(2,1)} %bitcast.110, bf16[2,2,2,2,112,128]{5,4,3,2,1,0:T(8,128)(2,1)} %bitcast.107, ...), custom_call_target="tpu_custom_call" | custom-call | flops 939524096 | bytes 4718592 | tf_op jit(solution)/shard_map/cross/pallas_call | solution.py:150
  301.1 2.8 collective-permute-start.16
  303.9 4.9 %cross.7 = f32[2,2,256,256]{3,2,1,0:T(8,128)} custom-call(s32[8]{0:T(128)} %get-tuple-element.7.slots_ref, s32[3]{0:T(128)} %get-tuple-element.5.wanted_ref, bf16[2,2,2,2,112,128]{5,4,3,2,1,0:T(8,128)(2,1)} %bitcast.114, bf16[2,2,2,2,112,128]{5,4,3,2,1,0:T(8,128)(2,1)} %bitcast.111, bf16[2,2,2,2,112,128]{5,4,3,2,1,0:T(8,128)(2,1)} %bitcast.108, ...), custom_call_target="tpu_custom_call" | custom-call | flops 939524096 | bytes 4718592 | tf_op jit(solution)/shard_map/cross/pallas_call | solution.py:150
  309.1 1.8 collective-permute-start
  311.5 9.3 %collective-permute-done.1 = bf16[8,2,112,128]{3,2,1,0:T(8,128)(2,1)S(1)} collective-permute-done((bf16[8,2,112,128]{3,2,1,0:T(8,128)(2,1)}, bf16[8,2,112,128]{3,2,1,0:T(8,128)(2,1)S(1)}, u32[]{:S(2)}, u32[]{:S(2)}) %collective-permute-start.1) | collective-permute-done | bytes 458784 | tf_op jit(solution)/shard_map/ppermute | solution.py:239
  320.8 55.6 %collective-permute-done = bf16[8,2,112,128]{3,2,1,0:T(8,128)(2,1)S(1)} collective-permute-done((bf16[8,2,112,128]{3,2,1,0:T(8,128)(2,1)}, bf16[8,2,112,128]{3,2,1,0:T(8,128)(2,1)S(1)}, u32[]{:S(2)}, u32[]{:S(2)}) %collective-permute-start) | collective-permute-done | bytes 458784 | tf_op jit(solution)/shard_map/ppermute | solution.py:239
  377.2 4.9 %cross.6.kept_ref = f32[2,2,256,256]{3,2,1,0:T(8,128)} custom-call(s32[8]{0:T(128)} %xor_add_fusion.1.slots_ref, s32[3]{0:T(128)} %get-tuple-element.6.wanted_ref, bf16[2,2,2,2,112,128]{5,4,3,2,1,0:T(8,128)(2,1)} %bitcast.67, bf16[2,2,2,2,112,128]{5,4,3,2,1,0:T(8,128)(2,1)} %bitcast.88, bf16[2,2,2,2,112,128]{5,4,3,2,1,0:T(8,128)(2,1)} %bitcast.85, ...), custom_call_target="tpu_custom_call" | custom-call | flops 939524096 | bytes 4718592 | tf_op jit(solution)/shard_map/cross/pallas_call | solution.py:150
  382.1 5.0 %cross.10.refs_10_ = f32[3,1,2,2,256,256]{5,4,3,2,1,0:T(8,128)} custom-call(s32[8]{0:T(128)} %xor_add_fusion.1.slots_ref, s32[3]{0:T(128)} %get-tuple-element.6.wanted_ref, bf16[2,2,2,2,112,128]{5,4,3,2,1,0:T(8,128)(2,1)} %bitcast.68, bf16[2,2,2,2,112,128]{5,4,3,2,1,0:T(8,128)(2,1)} %bitcast.89, bf16[2,2,2,2,112,128]{5,4,3,2,1,0:T(8,128)(2,1)} %bitcast.86, ...), custom_call_target="tpu_custom_call" | custom-call | flops 939524096 | bytes 4718592 | tf_op jit(solution)/shard_map/cross/pallas_call | solution.py:150
  387.1 5.0 %cross.11.before_ref = f32[3,1,2,2,256,256]{5,4,3,2,1,0:T(8,128)} custom-call(s32[8]{0:T(128)} %xor_add_fusion.1.slots_ref, s32[3]{0:T(128)} %get-tuple-element.6.wanted_ref, bf16[2,2,2,2,112,128]{5,4,3,2,1,0:T(8,128)(2,1)} %bitcast.69, bf16[2,2,2,2,112,128]{5,4,3,2,1,0:T(8,128)(2,1)} %bitcast.90, ...), custom_call_target="tpu_custom_call", output_to_operand_aliasing={{}: (12, {})} | custom-call | flops 939524096 | bytes 4718592 | tf_op jit(solution)/shard_map/cross/pallas_call | solution.py:150
  392.1 2.4 settle.1
  (72 shorter events, 12.5 us)
Async XLA Ops:
  6.1 102.6 %all-to-all-start = ((bf16[128,2,112,128]{3,2,1,0:T(8,128)(2,1)}), bf16[128,2,112,128]{3,2,1,0:T(8,128)(2,1)}, u32[]{:S(2)}, u32[]{:S(2)}) async-start(bf16[128,2,112,128]{3,2,1,0:T(8,128)(2,1)} %bitcast.63), calls=%async_computation | async-start | bytes 14680064 | tf_op jit(solution)/shard_map/all_to_all | solution.py:208
  114.6 69.3 %all-to-all-start.2 = ((bf16[8,3,8,112,128]{4,3,2,1,0:T(8,128)(2,1)}), bf16[8,3,8,112,128]{4,3,2,1,0:T(8,128)(2,1)}, u32[]{:S(2)}, u32[]{:S(2)}) async-start(bf16[8,3,8,112,128]{4,3,2,1,0:T(8,128)(2,1)} %bitcast.66), calls=%async_computation.2 | async-start | bytes 11010048 | tf_op jit(solution)/shard_map/all_to_all | solution.py:216
  183.9 192.6 %all-to-all-start.1 = ((bf16[8,3,8,112,128]{4,3,2,1,0:T(8,128)(2,1)}), bf16[8,3,8,112,128]{4,3,2,1,0:T(8,128)(2,1)}, u32[]{:S(2)}, u32[]{:S(2)}) async-start(bf16[8,3,8,112,128]{4,3,2,1,0:T(8,128)(2,1)} %bitcast.65), calls=%async_computation.1 | async-start | bytes 11010048 | tf_op jit(solution)/shard_map/all_to_all | solution.py:216
  189.5 87.7 %copy-start.17 = (s32[8]{0:T(128)S(1)}, s32[8]{0:T(128)}, u32[]{:S(2)}) copy-start(s32[8]{0:T(128)} %constant.108) | copy-start | bytes 100
  189.5 87.7 %copy-start.18 = (s32[8]{0:T(128)S(1)}, s32[8]{0:T(128)}, u32[]{:S(2)}) copy-start(s32[8]{0:T(128)} %constant.105.clone) | copy-start | bytes 100
  195.3 15.8 %collective-permute-start.14 = (bf16[8,2,112,128]{3,2,1,0:T(8,128)(2,1)S(1)}, bf16[8,2,112,128]{3,2,1,0:T(8,128)(2,1)S(1)}, u32[]{:S(2)}, u32[]{:S(2)}) collective-permute-start(bf16[8,2,112,128]{3,2,1,0:T(8,128)(2,1)S(1)} %get-tuple-element.9), channel_id=1, source_target_pairs={{0,66},{1,67},{2,64},{3,65},{4,70},{5,71},{6,68},{7,69},{64,2},{65... | collective-permute-start | bytes 1376264 | tf_op jit(solution)/shard_map/ppermute | solution.py:239
  197.6 43.5 %collective-permute-start.13 = (bf16[8,2,112,128]{3,2,1,0:T(8,128)(2,1)S(1)}, bf16[8,2,112,128]{3,2,1,0:T(8,128)(2,1)S(1)}, u32[]{:S(2)}, u32[]{:S(2)}) collective-permute-start(bf16[8,2,112,128]{3,2,1,0:T(8,128)(2,1)S(1)} %get-tuple-element.10), channel_id=1, source_target_pairs={{0,70},{1,71},{2,68},{3,69},{4,66},{5,67},{6,64},{7,65},{64,6},{65... | collective-permute-start | bytes 1376264 | tf_op jit(solution)/shard_map/ppermute | solution.py:239
  202.2 42.4 %collective-permute-start.12 = (bf16[8,2,112,128]{3,2,1,0:T(8,128)(2,1)S(1)}, bf16[8,2,112,128]{3,2,1,0:T(8,128)(2,1)S(1)}, u32[]{:S(2)}, u32[]{:S(2)}) collective-permute-start(bf16[8,2,112,128]{3,2,1,0:T(8,128)(2,1)S(1)} %get-tuple-element.11), channel_id=1, source_target_pairs={{0,67},{1,64},{2,65},{3,66},{4,71},{5,68},{6,69},{7,70},{64,3},{65... | collective-permute-start | bytes 1376264 | tf_op jit(solution)/shard_map/ppermute | solution.py:239
  202.6 42.0 %collective-permute-start.11 = (bf16[8,2,112,128]{3,2,1,0:T(8,128)(2,1)S(1)}, bf16[8,2,112,128]{3,2,1,0:T(8,128)(2,1)S(1)}, u32[]{:S(2)}, u32[]{:S(2)}) collective-permute-start(bf16[8,2,112,128]{3,2,1,0:T(8,128)(2,1)S(1)} %get-tuple-element.12), channel_id=1, source_target_pairs={{0,65},{1,66},{2,67},{3,64},{4,69},{5,70},{6,71},{7,68},{64,1},{65... | collective-permute-start | bytes 1376264 | tf_op jit(solution)/shard_map/ppermute | solution.py:239
  206.0 54.6 %collective-permute-start.10 = (bf16[8,2,112,128]{3,2,1,0:T(8,128)(2,1)S(1)}, bf16[8,2,112,128]{3,2,1,0:T(8,128)(2,1)S(1)}, u32[]{:S(2)}, u32[]{:S(2)}) collective-permute-start(bf16[8,2,112,128]{3,2,1,0:T(8,128)(2,1)S(1)} %get-tuple-element.13), channel_id=1, source_target_pairs={{0,71},{1,68},{2,69},{3,70},{4,67},{5,64},{6,65},{7,66},{64,7},{65... | collective-permute-start | bytes 1376264 | tf_op jit(solution)/shard_map/ppermute | solution.py:239
  211.1 79.9 %copy-start.7 = (bf16[8,2,112,128]{3,2,1,0:T(8,128)(2,1)}, bf16[8,2,112,128]{3,2,1,0:T(8,128)(2,1)S(1)}, u32[]{:S(2)}) copy-start(bf16[8,2,112,128]{3,2,1,0:T(8,128)(2,1)S(1)} %collective-permute-done.14) | copy-start | bytes 1376260
  211.1 65.1 %collective-permute-start.9 = (bf16[8,2,112,128]{3,2,1,0:T(8,128)(2,1)}, bf16[8,2,112,128]{3,2,1,0:T(8,128)(2,1)S(1)}, u32[]{:S(2)}, u32[]{:S(2)}) collective-permute-start(bf16[8,2,112,128]{3,2,1,0:T(8,128)(2,1)} %get-tuple-element.14), channel_id=1, source_target_pairs={{0,69},{1,70},{2,71},{3,68},{4,65},{5,66},{6,67},{7,64},{64,5},{65... | collective-permute-start | bytes 1376264 | tf_op jit(solution)/shard_map/ppermute | solution.py:239
  241.1 49.9 %copy-start.8 = (bf16[8,2,112,128]{3,2,1,0:T(8,128)(2,1)}, bf16[8,2,112,128]{3,2,1,0:T(8,128)(2,1)S(1)}, u32[]{:S(2)}) copy-start(bf16[8,2,112,128]{3,2,1,0:T(8,128)(2,1)S(1)} %collective-permute-done.13) | copy-start | bytes 1376260
  241.1 44.8 %collective-permute-start.8 = (bf16[8,2,112,128]{3,2,1,0:T(8,128)(2,1)}, bf16[8,2,112,128]{3,2,1,0:T(8,128)(2,1)S(1)}, u32[]{:S(2)}, u32[]{:S(2)}) collective-permute-start(bf16[8,2,112,128]{3,2,1,0:T(8,128)(2,1)} %get-tuple-element.15), channel_id=1, source_target_pairs={{0,68},{1,69},{2,70},{3,71},{4,64},{5,65},{6,66},{7,67},{64,4},{65... | collective-permute-start | bytes 1376264 | tf_op jit(solution)/shard_map/ppermute | solution.py:239
  244.6 16.0 %copy-start.9 = (bf16[8,2,112,128]{3,2,1,0:T(8,128)(2,1)}, bf16[8,2,112,128]{3,2,1,0:T(8,128)(2,1)S(1)}, u32[]{:S(2)}) copy-start(bf16[8,2,112,128]{3,2,1,0:T(8,128)(2,1)S(1)} %collective-permute-done.12) | copy-start | bytes 1376260
  244.6 43.3 %collective-permute-start.7 = (bf16[8,2,112,128]{3,2,1,0:T(8,128)(2,1)}, bf16[8,2,112,128]{3,2,1,0:T(8,128)(2,1)S(1)}, u32[]{:S(2)}, u32[]{:S(2)}) collective-permute-start(bf16[8,2,112,128]{3,2,1,0:T(8,128)(2,1)} %get-tuple-element.16), channel_id=1, source_target_pairs={{0,64},{1,65},{2,66},{3,67},{4,68},{5,69},{6,70},{7,71},{64,0},{65... | collective-permute-start | bytes 1376264 | tf_op jit(solution)/shard_map/ppermute | solution.py:239
  244.6 16.8 %copy-start.10 = (bf16[8,2,112,128]{3,2,1,0:T(8,128)(2,1)}, bf16[8,2,112,128]{3,2,1,0:T(8,128)(2,1)S(1)}, u32[]{:S(2)}) copy-start(bf16[8,2,112,128]{3,2,1,0:T(8,128)(2,1)S(1)} %collective-permute-done.11) | copy-start | bytes 1376260
  244.6 51.2 %collective-permute-start.6 = (bf16[8,2,112,128]{3,2,1,0:T(8,128)(2,1)}, bf16[8,2,112,128]{3,2,1,0:T(8,128)(2,1)S(1)}, u32[]{:S(2)}, u32[]{:S(2)}) collective-permute-start(bf16[8,2,112,128]{3,2,1,0:T(8,128)(2,1)} %get-tuple-element.17), channel_id=1, source_target_pairs={{0,6},{1,7},{2,4},{3,5},{4,2},{5,3},{6,0},{7,1},{64,70},{65,71},{6... | collective-permute-start | bytes 1376264 | tf_op jit(solution)/shard_map/ppermute | solution.py:239
  261.4 39.7 %collective-permute-start.5 = (bf16[8,2,112,128]{3,2,1,0:T(8,128)(2,1)}, bf16[8,2,112,128]{3,2,1,0:T(8,128)(2,1)S(1)}, u32[]{:S(2)}, u32[]{:S(2)}) collective-permute-start(bf16[8,2,112,128]{3,2,1,0:T(8,128)(2,1)} %get-tuple-element.18), channel_id=1, source_target_pairs={{0,2},{1,3},{2,0},{3,1},{4,6},{5,7},{6,4},{7,5},{64,66},{65,67},{6... | collective-permute-start | bytes 1376264 | tf_op jit(solution)/shard_map/ppermute | solution.py:239
  277.0 31.7 %collective-permute-start.4 = (bf16[8,2,112,128]{3,2,1,0:T(8,128)(2,1)}, bf16[8,2,112,128]{3,2,1,0:T(8,128)(2,1)S(1)}, u32[]{:S(2)}, u32[]{:S(2)}) collective-permute-start(bf16[8,2,112,128]{3,2,1,0:T(8,128)(2,1)} %get-tuple-element.19), channel_id=1, source_target_pairs={{0,7},{1,4},{2,5},{3,6},{4,3},{5,0},{6,1},{7,2},{64,71},{65,68},{6... | collective-permute-start | bytes 1376264 | tf_op jit(solution)/shard_map/ppermute | solution.py:239
  286.7 22.4 %collective-permute-start.3 = (bf16[8,2,112,128]{3,2,1,0:T(8,128)(2,1)}, bf16[8,2,112,128]{3,2,1,0:T(8,128)(2,1)S(1)}, u32[]{:S(2)}, u32[]{:S(2)}) collective-permute-start(bf16[8,2,112,128]{3,2,1,0:T(8,128)(2,1)} %get-tuple-element.20), channel_id=1, source_target_pairs={{0,5},{1,6},{2,7},{3,4},{4,1},{5,2},{6,3},{7,0},{64,69},{65,70},{6... | collective-permute-start | bytes 1376264 | tf_op jit(solution)/shard_map/ppermute | solution.py:239
  288.7 20.5 %collective-permute-start.2 = (bf16[8,2,112,128]{3,2,1,0:T(8,128)(2,1)}, bf16[8,2,112,128]{3,2,1,0:T(8,128)(2,1)S(1)}, u32[]{:S(2)}, u32[]{:S(2)}) collective-permute-start(bf16[8,2,112,128]{3,2,1,0:T(8,128)(2,1)} %get-tuple-element.21), channel_id=1, source_target_pairs={{0,3},{1,0},{2,1},{3,2},{4,7},{5,4},{6,5},{7,6},{64,67},{65,64},{6... | collective-permute-start | bytes 1376264 | tf_op jit(solution)/shard_map/ppermute | solution.py:239
  295.9 86.2 %collective-permute-start.17 = (f32[2,2,256,256]{3,2,1,0:T(8,128)}, f32[2,2,256,256]{3,2,1,0:T(8,128)}, u32[]{:S(2)}, u32[]{:S(2)}) collective-permute-start(f32[2,2,256,256]{3,2,1,0:T(8,128)} %cross.9), channel_id=1, source_target_pairs={{0,64},{64,0},{1,65},{65,1},{2,66},{66,2},{3,67},{67,3},{4,68},{68... | collective-permute-start | bytes 3145736 | tf_op jit(solution)/shard_map/ppermute | solution.py:250
  301.1 75.4 %copy-start.1 = (bf16[8,2,112,128]{3,2,1,0:T(8,128)(2,1)}, bf16[8,2,112,128]{3,2,1,0:T(8,128)(2,1)S(1)}, u32[]{:S(2)}) copy-start(bf16[8,2,112,128]{3,2,1,0:T(8,128)(2,1)S(1)} %collective-permute-done.5) | copy-start | bytes 1376260
  301.1 86.0 %collective-permute-start.16 = (f32[2,2,256,256]{3,2,1,0:T(8,128)}, f32[2,2,256,256]{3,2,1,0:T(8,128)}, u32[]{:S(2)}, u32[]{:S(2)}) collective-permute-start(f32[2,2,256,256]{3,2,1,0:T(8,128)} %cross.8), channel_id=1, source_target_pairs={{0,64},{64,0},{1,65},{65,1},{2,66},{66,2},{3,67},{67,3},{4,68},{68... | collective-permute-start | bytes 3145736 | tf_op jit(solution)/shard_map/ppermute | solution.py:250
  308.7 67.7 %copy-start.2 = (bf16[8,2,112,128]{3,2,1,0:T(8,128)(2,1)}, bf16[8,2,112,128]{3,2,1,0:T(8,128)(2,1)S(1)}, u32[]{:S(2)}) copy-start(bf16[8,2,112,128]{3,2,1,0:T(8,128)(2,1)S(1)} %collective-permute-done.4) | copy-start | bytes 1376260
  308.8 83.4 %collective-permute-start.15 = (f32[2,2,256,256]{3,2,1,0:T(8,128)}, f32[2,2,256,256]{3,2,1,0:T(8,128)}, u32[]{:S(2)}, u32[]{:S(2)}) collective-permute-start(f32[2,2,256,256]{3,2,1,0:T(8,128)} %cross.7), channel_id=1, source_target_pairs={{0,64},{64,0},{1,65},{65,1},{2,66},{66,2},{3,67},{67,3},{4,68},{68... | collective-permute-start | bytes 3145736 | tf_op jit(solution)/shard_map/ppermute | solution.py:250
  309.1 67.3 %copy-start.3 = (bf16[8,2,112,128]{3,2,1,0:T(8,128)(2,1)}, bf16[8,2,112,128]{3,2,1,0:T(8,128)(2,1)S(1)}, u32[]{:S(2)}) copy-start(bf16[8,2,112,128]{3,2,1,0:T(8,128)(2,1)S(1)} %collective-permute-done.3) | copy-start | bytes 1376260
  309.1 11.7 %collective-permute-start.1 = (bf16[8,2,112,128]{3,2,1,0:T(8,128)(2,1)}, bf16[8,2,112,128]{3,2,1,0:T(8,128)(2,1)S(1)}, u32[]{:S(2)}, u32[]{:S(2)}) collective-permute-start(bf16[8,2,112,128]{3,2,1,0:T(8,128)(2,1)} %get-tuple-element.22), channel_id=1, source_target_pairs={{0,1},{1,2},{2,3},{3,0},{4,5},{5,6},{6,7},{7,4},{64,65},{65,66},{6... | collective-permute-start | bytes 1376264 | tf_op jit(solution)/shard_map/ppermute | solution.py:239
  309.1 67.3 %copy-start.4 = (bf16[8,2,112,128]{3,2,1,0:T(8,128)(2,1)}, bf16[8,2,112,128]{3,2,1,0:T(8,128)(2,1)S(1)}, u32[]{:S(2)}) copy-start(bf16[8,2,112,128]{3,2,1,0:T(8,128)(2,1)S(1)} %collective-permute-done.2) | copy-start | bytes 1376260
  309.1 67.3 %collective-permute-start = (bf16[8,2,112,128]{3,2,1,0:T(8,128)(2,1)}, bf16[8,2,112,128]{3,2,1,0:T(8,128)(2,1)S(1)}, u32[]{:S(2)}, u32[]{:S(2)}) collective-permute-start(bf16[8,2,112,128]{3,2,1,0:T(8,128)(2,1)} %get-tuple-element.23), channel_id=1, source_target_pairs={{0,4},{1,5},{2,6},{3,7},{4,0},{5,1},{6,2},{7,3},{64,68},{65,69},{6... | collective-permute-start | bytes 1376264 | tf_op jit(solution)/shard_map/ppermute | solution.py:239
  320.8 55.7 %copy-start.5 = (bf16[8,2,112,128]{3,2,1,0:T(8,128)(2,1)}, bf16[8,2,112,128]{3,2,1,0:T(8,128)(2,1)S(1)}, u32[]{:S(2)}) copy-start(bf16[8,2,112,128]{3,2,1,0:T(8,128)(2,1)S(1)} %collective-permute-done.1) | copy-start | bytes 1376260
  (8 other events, 38.5 us)

commit v4 on v3

v4 whole, which is shorter than its diff:
```python
import functools
import math

import jax
import jax.numpy as jnp
from jax import lax
from jax.experimental import pallas as pl
from jax.experimental.pallas import tpu as pltpu
from jax.sharding import Mesh, PartitionSpec as P


ALL = ("xh", "z", "core", "xl", "y")
ZC = ("z", "core")
XY = ("xh", "xl", "y")
LANES = 128


def pack_kernel(groups, src, dst, buf, in_sem, out_sem):
    quarters, quarter, bins = buf.shape[:3]
    per = bins // 2 // groups

    def load(s):
        return pltpu.make_async_copy(src.at[pl.ds(s * quarter, quarter), :, 0], buf.at[s], in_sem.at[s])

    for s in range(quarters):
        load(s).start()
    for s in range(quarters):
        load(s).wait()
        for b in range(bins):
            h, rest = b // (bins // 2), b % (bins // 2)
            u, e = rest // per, rest % per
            for lh in range(buf.shape[-1] // LANES):
                pltpu.make_async_copy(
                    buf.at[s, :, b, :, pl.ds(lh * LANES, LANES)],
                    dst.at[s // 2, s % 2, e, lh, u, h],
                    out_sem.at[s],
                ).start()
    for s in range(quarters):
        pltpu.make_async_copy(src.at[pl.ds(s * quarter, quarter), :, 0], buf.at[s], out_sem.at[s]).wait()


def pack(spectra, groups):
    windows, bins, _, parts, width = spectra.shape
    quarter = windows // 4
    per, sides = bins // 2 // groups, width // LANES
    return pl.pallas_call(
        functools.partial(pack_kernel, groups),
        out_shape=jax.ShapeDtypeStruct((2, 2, per, sides, groups, 2, quarter, parts, LANES), spectra.dtype),
        in_specs=[pl.BlockSpec(memory_space=pl.ANY)],
        out_specs=pl.BlockSpec(memory_space=pl.ANY),
        scratch_shapes=[
            pltpu.VMEM((4, quarter, bins, parts, width), spectra.dtype),
            pltpu.SemaphoreType.DMA((4,)),
            pltpu.SemaphoreType.DMA((4,)),
        ],
        cost_estimate=pl.CostEstimate(flops=0, transcendentals=0, bytes_accessed=4 * spectra.size),
        name="pack",
    )(spectra)


def pick_kernel(entries, meta, src, *refs):
    outs, (buf, in_sem, out_sem) = refs[:-3], refs[-3:]
    targets, groups = buf.shape[0], src.shape[1]
    if len(outs) == 1:
        outs = [outs[0].at[k] for k in range(targets)]
    steps = (buf.shape[1] - entries * groups) // 2

    def loads(k):
        copies = []
        for i in range(entries):
            n = k * entries + i
            copies.append((src.at[meta[n], :, meta[targets * entries + n]], buf.at[k, pl.ds(i * groups, groups)]))
        for i in range(steps):
            block, group = meta[2 * targets * entries + k], meta[2 * targets * entries + targets + i]
            copies.append((src.at[block, group], buf.at[k, pl.ds(entries * groups + 2 * i, 2)]))
        return [pltpu.make_async_copy(x, y, in_sem.at[k, i]) for i, (x, y) in enumerate(copies)]

    for k in range(targets):
        for copy in loads(k):
            copy.start()
    for k in range(targets):
        for copy in loads(k):
            copy.wait()
        pltpu.make_async_copy(buf.at[k], outs[k], out_sem.at[k]).start()
    for k in range(targets):
        pltpu.make_async_copy(buf.at[k], outs[k], out_sem.at[k]).wait()


def pick(holdings, blocks, halves, own_blocks, own_groups, joined):
    _, groups, _, rows, lanes = holdings.shape
    targets, entries = blocks.shape
    steps = own_groups.shape[0]
    units = entries * groups + 2 * steps
    meta = jnp.concatenate([blocks.reshape(-1), halves.reshape(-1), own_blocks, own_groups])
    whole = pl.BlockSpec(memory_space=pl.ANY)
    shapes = [(targets, units, rows, lanes)] if joined else [(units, rows, lanes)] * targets
    return pl.pallas_call(
        functools.partial(pick_kernel, entries),
        out_shape=[jax.ShapeDtypeStruct(shape, holdings.dtype) for shape in shapes],
        grid_spec=pltpu.PrefetchScalarGridSpec(
            num_scalar_prefetch=1,
            grid=(),
            in_specs=[whole],
            out_specs=[whole] * len(shapes),
            scratch_shapes=[
                pltpu.VMEM((targets, units, rows, lanes), holdings.dtype),
                pltpu.SemaphoreType.DMA((targets, entries + steps)),
                pltpu.SemaphoreType.DMA((targets,)),
            ],
        ),
        cost_estimate=pl.CostEstimate(flops=0, transcendentals=0, bytes_accessed=4 * targets * units * rows * lanes),
        name="pick",
    )(meta, holdings)


def cross_kernel(counts, mine, fused, scale, wanted_ref, places_ref, *refs):
    whole, steps, shares = counts
    pieces, refs = refs[:whole], refs[whole:]
    single, refs = refs[: shares * steps], refs[shares * steps :]
    others, refs = refs[:shares], refs[shares:]
    out_ref, own_ref, other_ref = refs[-3:]
    _, groups, rows, lanes = own_ref.shape
    for k in range(whole):
        own_ref[:, places_ref[shares + k]] = pieces[k][...]
    for k in range(shares):
        other_ref[places_ref[k]] = others[k][...]
        for i in range(steps):
            own_ref[k, places_ref[shares + whole + i]] = single[k * steps + i][...]
    sides = 2
    quarters = shares // (mine * sides)
    depth = groups * rows
    odd = lax.broadcasted_iota(jnp.int32, (depth // 8, 8, lanes * sides), 1) % 2 == 1
    for e in range(mine):
        real = None
        for q in range(quarters):
            at = (q * mine + e) * sides
            a = jnp.concatenate([own_ref[at + s].reshape(depth, lanes) for s in range(sides)], axis=1)
            b = jnp.concatenate([other_ref[at + s].reshape(depth, lanes) for s in range(sides)], axis=1)
            tall = b.astype(jnp.float32).reshape(depth // 8, 8, lanes * sides)
            turned = jnp.where(odd, pltpu.roll(tall, 1, 1), -pltpu.roll(tall, 7, 1))
            turned = turned.reshape(depth, lanes * sides).astype(b.dtype)
            dims = (((0,), (0,)), ((), ()))
            re = lax.dot_general(a, b, dims, preferred_element_type=jnp.float32)
            im = lax.dot_general(a, turned, dims, preferred_element_type=jnp.float32)
            real, imag = (re, im) if real is None else (real + re, imag + im)
        if fused:
            back_ref = refs[0]
            real, imag = (real + back_ref[e, 0]) * scale, (imag + back_ref[e, 1]) * scale
        out_ref[e, 0] = real
        out_ref[e, 1] = imag


def cross(pieces, single, others, entry, first, places, wanted, mine, turn, rounds, back=None, scale=None, out=None):
    shares, _, rows, lanes = pieces[0].shape
    width = 2 * lanes
    steps = 0 if single is None else places.shape[0] - shares - len(pieces)
    groups = len(pieces) + steps
    in_specs = [pl.BlockSpec((shares, None, rows, lanes), lambda i, w, p: (0, w[turn], 0, 0))] * len(pieces)
    operands = [wanted, places, *pieces]
    for k in range(shares):
        for i in range(steps):
            operands.append(single)
            in_specs.append(
                pl.BlockSpec((None, None, rows, lanes), lambda n, w, p, k=k, at=first + 2 * i: (k, at + w[turn], 0, 0))
            )
    if isinstance(others, list):
        operands += others
        in_specs += [pl.BlockSpec((groups, rows, lanes), lambda i, w, p: (entry, 0, 0))] * shares
    else:
        operands += [others] * shares
        in_specs += [
            pl.BlockSpec((None, groups, rows, lanes), lambda i, w, p, k=k: (k, entry, 0, 0)) for k in range(shares)
        ]
    one = pl.BlockSpec((mine, 2, width, width), lambda i, w, p: (0, 0, 0, 0))
    out_spec, shape, aliases = one, (mine, 2, width, width), {}
    if back is not None:
        operands.append(back)
        in_specs.append(one)
        out_spec = pl.BlockSpec((None, None, mine, 2, width, width), lambda i, w, p: (turn, 0, 0, 0, 0, 0))
        shape = (rounds, 1, mine, 2, width, width)
        if out is not None:
            aliases = {len(operands): 0}
            operands.append(out)
            in_specs.append(pl.BlockSpec(memory_space=pl.ANY))
    return pl.pallas_call(
        functools.partial(cross_kernel, (len(pieces), steps, shares), mine, back is not None, scale),
        out_shape=jax.ShapeDtypeStruct(shape, jnp.float32),
        grid_spec=pltpu.PrefetchScalarGridSpec(
            num_scalar_prefetch=2,
            grid=(1,),
            in_specs=in_specs,
            out_specs=out_spec,
            scratch_shapes=[pltpu.VMEM((shares, groups, rows, lanes), pieces[0].dtype)] * 2,
        ),
        input_output_aliases=aliases,
        cost_estimate=pl.CostEstimate(
            flops=2 * shares * groups * rows * width * width,
            transcendentals=0,
            bytes_accessed=4 * shares * groups * rows * lanes + mine * 2 * width * width * 4,
        ),
        name="cross",
    )(*operands)


HOPS = [(1, 1, 0), (0, 1, 0), (1, 1, 1), (1, 0, 0), (0, 1, 1), (1, 1, 3), (1, 0, 3), (0, 1, 3), (1, 1, 2), (0, 1, 2)]
HOPS += [(0, 0, 1), (0, 0, 3), (0, 0, 2)]
FETCHED = (1, 2)
TURNS = [(0, 0), (1, 0), (3, 0), (1, 1), (3, 1), (2, 0), (2, 1), (0, 1)]
PARTS = [[(0, 0), (0, 1)], [(0, 2), (1, 0)], [(1, 1), (1, 2)]]


def per_device(spectra, partner):
    windows, bins, _, parts, _ = spectra.shape
    nl, ny = lax.axis_size("xl"), lax.axis_size("y")
    nz, nc = lax.axis_size("z"), lax.axis_size("core")
    groups, inner = nl * ny, nz * nc
    lanes = LANES
    blocks = 2 * inner
    plane, xl, y = lax.axis_index("xh"), lax.axis_index("xl"), lax.axis_index("y")
    z, core = lax.axis_index("z"), lax.axis_index("core")
    rounds = partner.shape[0]
    mine = bins // 2 // groups
    rows = windows // 4 * parts

    joint = pack(spectra, groups).reshape(blocks * groups, 2, rows, lanes)
    holdings = lax.all_to_all(joint, ALL, split_axis=0, concat_axis=0, tiled=True)
    holdings = holdings.reshape(blocks, groups, 2, rows, lanes)

    dz, dc = jnp.array([t[0] for t in TURNS]), jnp.array([t[1] for t in TURNS])
    every = jnp.arange(inner, dtype=jnp.int32)
    turned = ((z + dz) % nz) * nc + (core + dc) % nc
    shares = ((z - dz) % nz) * nc + (core - dc) % nc
    planes = jnp.stack([1 - plane, plane])
    seat = planes[:, None] * inner + jnp.concatenate([every, turned])[None, :]
    mates = partner[:, seat]
    sides = (seat[None] > mates).astype(jnp.int32)
    fetched_groups = xl * ny + (y - jnp.array(FETCHED)) % ny

    def fetch(part):
        entries, joined = PARTS[part], part == 0
        at = slice(0, inner) if joined else slice(inner, None)
        chosen = jnp.stack([mates[r, side, at] for side, r in entries], axis=1)
        wanted = jnp.stack([sides[r, side, at] for side, r in entries], axis=1)
        extra = fetched_groups if joined else fetched_groups[:0]
        outs = pick(holdings, chosen, wanted, seat[0, at], extra, joined)
        if joined:
            return lax.all_to_all(outs[0], ZC, split_axis=0, concat_axis=0, tiled=True)
        arrived = [outs[0]]
        for k, (a, b) in enumerate(TURNS[1:]):
            table = [
                (cz * nc + cc, ((cz + a) % nz) * nc + (cc + b) % nc) for cz in range(nz) for cc in range(nc)
            ]
            arrived.append(lax.ppermute(outs[k + 1], ZC, table))
        return arrived

    others = [fetch(part) for part in range(len(PARTS))]

    by_plane = joint.reshape(2, inner, groups, 2, rows, lanes)

    def piece(fx, fl, dy):
        start = (plane ^ fx, 0, (xl ^ fl) * ny + (y + dy) % ny, 0, 0, 0)
        part = lax.dynamic_slice(by_plane, start, (1, inner, 1, 2, rows, lanes))
        return part.reshape(inner, 2, rows, lanes)

    own = [[piece(0, 0, 0)], []]
    for fx, fl, dy in HOPS:
        table = [
            ((cx * nl + cl) * ny + cy, ((cx ^ fx) * nl + (cl ^ fl)) * ny + (cy + dy) % ny)
            for cx in range(2)
            for cl in range(nl)
            for cy in range(ny)
        ]
        part = piece(fx, fl, dy)
        own[fx].append(lax.ppermute(part, XY, table))

    def places(order):
        flips, steps = jnp.array([fl for fl, _ in order]), jnp.array([dy for _, dy in order])
        slots = (xl ^ flips) * ny + (y - steps) % ny
        return [jnp.concatenate([every, slots]), jnp.concatenate([shares, slots])]

    away_places = places([(fl, dy) for fx, fl, dy in HOPS if fx == 1] + [(0, dy) for dy in FETCHED])
    kept_places = places([(0, 0)] + [(fl, dy) for fx, fl, dy in HOPS if fx == 0])
    wanted = (planes[:, None, None] * inner + z * nc + core)[:, :, 0]
    mine_half = [(wanted[i, 0] > lax.dynamic_index_in_dim(partner, wanted[i, 0], 1, False)).astype(jnp.int32) for i in range(2)]

    where = {pair: (p, i) for p, pairs in enumerate(PARTS) for i, pair in enumerate(pairs)}
    first = len(PARTS[0]) * groups
    scale = 1.0 / math.sqrt(windows * groups)
    backs = []
    for r in range(rounds):
        p, i = where[0, r]
        away = cross(own[1], others[0], others[p], i, first, away_places[p > 0], mine_half[0], mine, r, rounds)
        backs.append(lax.ppermute(away, "xh", [(0, 1), (1, 0)]))
    out = None
    for r in range(rounds):
        p, i = where[1, r]
        out = cross(own[0], None, others[p], i, 0, kept_places[p > 0], mine_half[1], mine, r, rounds, backs[r], scale, out)
    return out


def solution(mesh):
    fine = Mesh(mesh.devices.reshape(2, 4, 2, 2, 4), ALL)
    chan, tm = ("xh", "z", "core"), ("xl", "y")

    return jax.shard_map(
        per_device,
        mesh=fine,
        in_specs=(P(tm, None, chan, None, None), P()),
        out_specs=P(None, chan, tm, None, None, None),
        check_vma=False,
    )
```

time: 395 us -> 346 us (0.88)
  waiting for transfers between devices: 276 us -> 209 us
  starting transfers between devices: 54 us -> 66.8 us
  local copies, waits for them, and re-layouts: 13.3 us -> 8.66 us
  between operations: 0.23 us -> 4.28 us
    all_to_all x2 -> x1, waiting for transfers between devices: 55.6 us -> 0.01 us  [fetch(): return lax.all_to_all(outs[0], ZC, split_axis=0, concat_axis=0, tiled=True)]
    ppermute x15 -> x27, starting transfers between devices: 26.6 us -> 46.5 us  [the longest x13 25.8 us: per_device(): own[fx].append(lax.ppermute(part, XY, table))]
    ppermute x15 -> x27, waiting for transfers between devices: 131 us -> 121 us  [the longest x13 79.3 us: per_device(): own[fx].append(lax.ppermute(part, XY, table))]
    all_to_all x2 -> x1, starting transfers between devices: 12.1 us -> 6.47 us  [fetch(): return lax.all_to_all(outs[0], ZC, split_axis=0, concat_axis=0, tiled=True)]
  transfers between devices with their start and end apart: 21 -> 32, of which waited for: 9 -> 13; matrix products, arithmetic and copies ran while one was open for 3% -> 3% of each run, Pallas kernels for 9% -> 10%
where the time goes in v4:
time: 346 us; the launch traced here: 345 us
  waiting for transfers between devices  209 us (60%)
  starting transfers between devices  66.8 us (19%)
  Pallas kernels  52.6 us (15%)
  local copies, waits for them, and re-layouts  8.66 us (3%)
  between operations  4.28 us (1%)
  other arithmetic  4.23 us (1%)
    all_to_all x1, waiting for transfers between devices, per_device(): lax.all_to_all(joint, ALL, split_axis=0, concat_axis=0, tiled=True)  87.7 us
    ppermute x13, waiting for transfers between devices, per_device(): own[fx].append(lax.ppermute(part, XY, table))  79.3 us
    ppermute x14, waiting for transfers between devices, fetch(): arrived.append(lax.ppermute(outs[k + 1], ZC, table))  41.6 us
    pallas_call x6, Pallas kernels, cross(): pl.pallas_call(functools.partial(cross_kernel, (len(pieces), steps, share...  33 us
    ppermute x13, starting transfers between devices, per_device(): own[fx].append(lax.ppermute(part, XY, table))  25.8 us
    ppermute x14, starting transfers between devices, fetch(): arrived.append(lax.ppermute(outs[k + 1], ZC, table))  20.7 us
    pallas_call x3, Pallas kernels, pick(): pl.pallas_call(functools.partial(pick_kernel, entries), out_shape=[jax.Sh...  13.5 us
    all_to_all x1, starting transfers between devices, per_device(): lax.all_to_all(joint, ALL, split_axis=0, concat_axis=0, tiled=True)  11.9 us
  transfers between devices with their start and end apart: 32, of which 13 were waited for; matrix products, arithmetic and copies ran while one was open for 3% of the time, Pallas kernels for 10%

profile of v4, /device:TPU:1, one launch (start us, length us, event | category | flops | bytes accessed | tf_op | source)
XLA Modules:
  0.0 345.2 jit_solution(4401775987897939918)
XLA Ops:
  0.0 6.1 %pack.1 = bf16[2,2,2,2,8,2,56,2,128]{8,7,6,5,4,3,2,1,0:T(2,128)(2,1)} custom-call(bf16[224,32,1,2,256]{4,3,2,1,0:T(2,128)(2,1)} %src.1), custom_call_target="tpu_custom_call" | custom-call | bytes 14680064 | tf_op jit(solution)/shard_map/pack/pallas_call | solution.py:46
  6.2 11.9 %all-to-all-start = ((bf16[128,2,112,128]{3,2,1,0:T(8,128)(2,1)}), bf16[128,2,112,128]{3,2,1,0:T(8,128)(2,1)}, u32[]{:S(2)}, u32[]{:S(2)}) async-start(bf16[128,2,112,128]{3,2,1,0:T(8,128)(2,1)} %bitcast.98), calls=%async_computation | async-start | bytes 14680064 | tf_op jit(solution)/shard_map/all_to_all | solution.py:226
  21.2 87.7 %all-to-all-done = bf16[128,2,112,128]{3,2,1,0:T(8,128)(2,1)} async-done(((bf16[128,2,112,128]{3,2,1,0:T(8,128)(2,1)}), bf16[128,2,112,128]{3,2,1,0:T(8,128)(2,1)}, u32[]{:S(2)}, u32[]{:S(2)}) %all-to-all-start) | async-done | bytes 7340064 | tf_op jit(solution)/shard_map/all_to_all | solution.py:226
  108.8 5.1 %pick.4 = bf16[8,20,112,128]{3,2,1,0:T(8,128)(2,1)} custom-call(s32[42]{0:T(128)} %pad_add_fusion.8.meta, bf16[16,8,2,112,128]{4,3,2,1,0:T(8,128)(2,1)} %bitcast.22.src), custom_call_target="tpu_custom_call" | custom-call | bytes 9175040 | tf_op jit(solution)/shard_map/pick/pallas_call | solution.py:97
  114.0 6.5 %all-to-all-start.1 = ((bf16[8,20,112,128]{3,2,1,0:T(8,128)(2,1)}), bf16[8,20,112,128]{3,2,1,0:T(8,128)(2,1)}, u32[]{:S(2)}, u32[]{:S(2)}) async-start(bf16[8,20,112,128]{3,2,1,0:T(8,128)(2,1)} %pick.4), calls=%async_computation.1 | async-start | bytes 9175040 | tf_op jit(solution)/shard_map/all_to_all | solution.py:247
  120.4 5.2 %dynamic-slice_bitcast_fusion = (bf16[8,2,112,128]{3,2,1,0:T(8,128)(2,1)S(1)}, bf16[8,2,112,128]{3,2,1,0:T(8,128)(2,1)S(1)}, bf16[8,2,112,128]{3,2,1,0:T(8,128)(...) fusion(bf16[2,8,8,2,112,128]{5,4,3,2,1,0:T(8,128)(2,1)} %bitcas, ...), kind=kLoop, calls=%fused_computation.1 | loop fusion | bytes 12845096 | tf_op jit(solution)/shard_map/reshape | solution.py:263
  127.6 3.3 collective-permute-start.18
  133.1 4.9 %collective-permute-start.15 = (bf16[8,2,112,128]{3,2,1,0:T(8,128)(2,1)S(1)}, bf16[8,2,112,128]{3,2,1,0:T(8,128)(2,1)S(1)}, u32[]{:S(2)}, u32[]{:S(2)}) collective-permute-start(bf16[8,2,112,128]{3,2,1,0:T(8,128)(2,1)S(1)} %get-tuple-element.43), channel_id=1, source_target_pairs={{0,69},{1,70},{2,71},{3,68},{4,65},{5,66},{6,67},{7,64},{64,5},{65... | collective-permute-start | bytes 1376264 | tf_op jit(solution)/shard_map/ppermute | solution.py:274
  137.9 23.0 %collective-permute-done.19.refs_5_ = bf16[8,2,112,128]{3,2,1,0:T(8,128)(2,1)S(1)} collective-permute-done((bf16[8,2,112,128]{3,2,1,0:T(8,128)(2,1)S(1)}, bf16[8,2,112,128]{3,2,1,0:T(8,128)(2,1)S(1)}, u32[]{:S(2)}, u32[]{:S(2)}) %collective-permute-start.19) | collective-permute-done | bytes 458784 | tf_op jit(solution)/shard_map/ppermute | solution.py:274
  161.0 4.1 %collective-permute-start.14 = (bf16[8,2,112,128]{3,2,1,0:T(8,128)(2,1)}, bf16[8,2,112,128]{3,2,1,0:T(8,128)(2,1)S(1)}, u32[]{:S(2)}, u32[]{:S(2)}) collective-permute-start(bf16[8,2,112,128]{3,2,1,0:T(8,128)(2,1)} %get-tuple-element.44), channel_id=1, source_target_pairs={{0,68},{1,69},{2,70},{3,71},{4,64},{5,65},{6,66},{7,67},{64,4},{65... | collective-permute-start | bytes 1376264 | tf_op jit(solution)/shard_map/ppermute | solution.py:274
  165.0 6.4 %collective-permute-done.17.refs_3_ = bf16[8,2,112,128]{3,2,1,0:T(8,128)(2,1)S(1)} collective-permute-done((bf16[8,2,112,128]{3,2,1,0:T(8,128)(2,1)S(1)}, bf16[8,2,112,128]{3,2,1,0:T(8,128)(2,1)S(1)}, u32[]{:S(2)}, u32[]{:S(2)}) %collective-permute-start.17) | collective-permute-done | bytes 458784 | tf_op jit(solution)/shard_map/ppermute | solution.py:274
  174.2 8.0 %collective-permute-done.15.refs_1_ = bf16[8,2,112,128]{3,2,1,0:T(8,128)(2,1)S(1)} collective-permute-done((bf16[8,2,112,128]{3,2,1,0:T(8,128)(2,1)S(1)}, bf16[8,2,112,128]{3,2,1,0:T(8,128)(2,1)S(1)}, u32[]{:S(2)}, u32[]{:S(2)}) %collective-permute-start.15) | collective-permute-done | bytes 458784 | tf_op jit(solution)/shard_map/ppermute | solution.py:274
  183.3 7.9 %collective-permute-done.14.refs_0_ = bf16[8,2,112,128]{3,2,1,0:T(8,128)(2,1)S(1)} collective-permute-done((bf16[8,2,112,128]{3,2,1,0:T(8,128)(2,1)}, bf16[8,2,112,128]{3,2,1,0:T(8,128)(2,1)S(1)}, u32[]{:S(2)}, u32[]{:S(2)}) %collective-permute-start.14) | collective-permute-done | bytes 458784 | tf_op jit(solution)/shard_map/ppermute | solution.py:274
  192.3 4.2 %pick.5 = (bf16[16,112,128]{2,1,0:T(8,128)(2,1)}, bf16[16,112,128]{2,1,0:T(8,128)(2,1)}, bf16[16,112,128]{2,1,0:T(8,128)(2,1)}, bf16[16,112,128]{2,1,0:T(8,128)(...) custom-call(s32[40]{0:T(128)} %get-tuple-element.73.meta, ...), custom_call_target="tpu_custom_call" | custom-call | bytes 7340032 | tf_op jit(solution)/shard_map/pick/pallas_call | solution.py:97
  198.5 11.7 %collective-permute-done.5.refs_6_ = bf16[8,2,112,128]{3,2,1,0:T(8,128)(2,1)} collective-permute-done((bf16[8,2,112,128]{3,2,1,0:T(8,128)(2,1)}, bf16[8,2,112,128]{3,2,1,0:T(8,128)(2,1)}, u32[]{:S(2)}, u32[]{:S(2)}) %collective-permute-start.5) | collective-permute-done | bytes 458784 | tf_op jit(solution)/shard_map/ppermute | solution.py:274
  211.0 7.6 %collective-permute-done.4.refs_5_ = bf16[8,2,112,128]{3,2,1,0:T(8,128)(2,1)} collective-permute-done((bf16[8,2,112,128]{3,2,1,0:T(8,128)(2,1)}, bf16[8,2,112,128]{3,2,1,0:T(8,128)(2,1)}, u32[]{:S(2)}, u32[]{:S(2)}) %collective-permute-start.4) | collective-permute-done | bytes 458784 | tf_op jit(solution)/shard_map/ppermute | solution.py:274
  223.8 3.9 %collective-permute-start.25 = (bf16[16,112,128]{2,1,0:T(8,128)(2,1)}, bf16[16,112,128]{2,1,0:T(8,128)(2,1)}, u32[]{:S(2)}, u32[]{:S(2)}) collective-permute-start(bf16[16,112,128]{2,1,0:T(8,128)(2,1)} %get-tuple-element.35), channel_id=1, source_target_pairs={{0,40},{8,32},{16,56},{24,48},{32,8},{40,0},{48,24},{56,16},{1,41}... | collective-permute-start | bytes 1376264 | tf_op jit(solution)/shard_map/ppermute | solution.py:253
  234.2 5.3 %cross.8 = f32[2,2,256,256]{3,2,1,0:T(8,128)} custom-call(s32[3]{0:T(128)} %get-tuple-element.37.wanted_ref, s32[16]{0:T(128)} %get-tuple-element.69.places_ref, bf16[8,2,112,128]{3,2,1,0:T(8,128)(2,1)} %copy-done.5, bf16[8,2,112,128]{3,2,1,0:T(8,128)(2,1)} %copy-done.4, bf16[8,2,112,128]{3,2,1,0:T(8,128)(2,1)} %copy-done.3, ...), custom_call_target="tpu_custom_call" | custom-call | flops 939524096 | bytes 4718592 | tf_op jit(solution)/shard_map/cross/pallas_call | solution.py:185
  239.7 15.4 %collective-permute-done.22.refs_25_.refs_11_ = bf16[16,112,128]{2,1,0:T(8,128)(2,1)} collective-permute-done((bf16[16,112,128]{2,1,0:T(8,128)(2,1)}, bf16[16,112,128]{2,1,0:T(8,128)(2,1)}, u32[]{:S(2)}, u32[]{:S(2)}) %collective-permute-start.22) | collective-permute-done | bytes 458784 | tf_op jit(solution)/shard_map/ppermute | solution.py:253
  255.1 5.1 %collective-permute-start = (bf16[8,2,112,128]{3,2,1,0:T(8,128)(2,1)}, bf16[8,2,112,128]{3,2,1,0:T(8,128)(2,1)S(1)}, u32[]{:S(2)}, u32[]{:S(2)}) collective-permute-start(bf16[8,2,112,128]{3,2,1,0:T(8,128)(2,1)} %get-tuple-element.51), channel_id=1, source_target_pairs={{0,4},{1,5},{2,6},{3,7},{4,0},{5,1},{6,2},{7,3},{64,68},{65,69},{6... | collective-permute-start | bytes 1376264 | tf_op jit(solution)/shard_map/ppermute | solution.py:274
  260.2 4.2 %pick.3 = (bf16[16,112,128]{2,1,0:T(8,128)(2,1)}, bf16[16,112,128]{2,1,0:T(8,128)(2,1)}, bf16[16,112,128]{2,1,0:T(8,128)(2,1)}, bf16[16,112,128]{2,1,0:T(8,128)(...) custom-call(s32[40]{0:T(128)} %get-tuple-element.74.meta, ...), custom_call_target="tpu_custom_call" | custom-call | bytes 7340032 | tf_op jit(solution)/shard_map/pick/pallas_call | solution.py:97
  264.5 4.3 %collective-permute-start.8 = (bf16[16,112,128]{2,1,0:T(8,128)(2,1)}, bf16[16,112,128]{2,1,0:T(8,128)(2,1)S(1)}, u32[]{:S(2)}, u32[]{:S(2)}) collective-permute-start(bf16[16,112,128]{2,1,0:T(8,128)(2,1)} %get-tuple-element.23), channel_id=1, source_target_pairs={{0,48},{8,56},{16,0},{24,8},{32,16},{40,24},{48,32},{56,40},{1,49}... | collective-permute-start | bytes 1376264 | tf_op jit(solution)/shard_map/ppermute | solution.py:253
  268.8 5.3 %cross.7 = f32[2,2,256,256]{3,2,1,0:T(8,128)} custom-call(s32[3]{0:T(128)} %get-tuple-element.37.wanted_ref, s32[16]{0:T(128)} %get-tuple-element.69.places_ref, bf16[8,2,112,128]{3,2,1,0:T(8,128)(2,1)} %copy-done.5, bf16[8,2,112,128]{3,2,1,0:T(8,128)(2,1)} %copy-done.4, bf16[8,2,112,128]{3,2,1,0:T(8,128)(2,1)} %copy-done.3, ...), custom_call_target="tpu_custom_call" | custom-call | flops 939524096 | bytes 4718592 | tf_op jit(solution)/shard_map/cross/pallas_call | solution.py:185
  275.1 5.4 %cross.6 = f32[2,2,256,256]{3,2,1,0:T(8,128)} custom-call(s32[3]{0:T(128)} %get-tuple-element.37.wanted_ref, s32[16]{0:T(128)} %get-tuple-element.70.places_ref, bf16[8,2,112,128]{3,2,1,0:T(8,128)(2,1)} %copy-done.5, bf16[8,2,112,128]{3,2,1,0:T(8,128)(2,1)} %copy-done.4, bf16[8,2,112,128]{3,2,1,0:T(8,128)(2,1)} %copy-done.3, ...), custom_call_target="tpu_custom_call" | custom-call | flops 939524096 | bytes 4718592 | tf_op jit(solution)/shard_map/cross/pallas_call | solution.py:185
  280.6 13.3 %collective-permute-done.refs_1_ = bf16[8,2,112,128]{3,2,1,0:T(8,128)(2,1)S(1)} collective-permute-done((bf16[8,2,112,128]{3,2,1,0:T(8,128)(2,1)}, bf16[8,2,112,128]{3,2,1,0:T(8,128)(2,1)S(1)}, u32[]{:S(2)}, u32[]{:S(2)}) %collective-permute-start) | collective-permute-done | bytes 458784 | tf_op jit(solution)/shard_map/ppermute | solution.py:274
  297.8 11.1 %collective-permute-done.9.refs_11_ = bf16[16,112,128]{2,1,0:T(8,128)(2,1)S(1)} collective-permute-done((bf16[16,112,128]{2,1,0:T(8,128)(2,1)S(1)}, bf16[16,112,128]{2,1,0:T(8,128)(2,1)S(1)}, u32[]{:S(2)}, u32[]{:S(2)}) %collective-permute-start.9) | collective-permute-done | bytes 458784 | tf_op jit(solution)/shard_map/ppermute | solution.py:253
  308.9 3.1 collective-permute-start.12
  312.3 5.7 %cross.9.refs_17_ = f32[3,1,2,2,256,256]{5,4,3,2,1,0:T(8,128)} custom-call(s32[3]{0:T(128)} %get-tuple-element.38.wanted_ref, s32[16]{0:T(128)} %get-tuple-element.71.places_ref, bf16[8,2,112,128]{3,2,1,0:T(8,128)(2,1)} %get-tuple-element.52.refs_0_, bf16[8,2,112,128]{3,2,1,0:T(8,128)(2,1)} %copy-done.7, ...), custom_call_target="tpu_custom_call" | custom-call | flops 939524096 | bytes 4718592 | tf_op jit(solution)/shard_map/cross/pallas_call | solution.py:185
  318.0 4.8 %collective-permute-done.11.refs_13_ = bf16[16,112,128]{2,1,0:T(8,128)(2,1)S(1)} collective-permute-done((bf16[16,112,128]{2,1,0:T(8,128)(2,1)}, bf16[16,112,128]{2,1,0:T(8,128)(2,1)S(1)}, u32[]{:S(2)}, u32[]{:S(2)}) %collective-permute-start.11) | collective-permute-done | bytes 458784 | tf_op jit(solution)/shard_map/ppermute | solution.py:253
  322.8 10.3 %collective-permute-done.12.refs_14_ = bf16[16,112,128]{2,1,0:T(8,128)(2,1)S(1)} collective-permute-done((bf16[16,112,128]{2,1,0:T(8,128)(2,1)}, bf16[16,112,128]{2,1,0:T(8,128)(2,1)S(1)}, u32[]{:S(2)}, u32[]{:S(2)}) %collective-permute-start.12) | collective-permute-done | bytes 458784 | tf_op jit(solution)/shard_map/ppermute | solution.py:253
  333.9 5.6 %cross.10.refs_17_ = f32[3,1,2,2,256,256]{5,4,3,2,1,0:T(8,128)} custom-call(s32[3]{0:T(128)} %get-tuple-element.38.wanted_ref, s32[16]{0:T(128)} %get-tuple-element.71.places_ref, bf16[8,2,112,128]{3,2,1,0:T(8,128)(2,1)} %get-tuple-element.52.refs_0_, bf16[8,2,112,128]{3,2,1,0:T(8,128)(2,1)} %copy-done.7, ...), custom_call_target="tpu_custom_call", output_to_operand_aliasing={{}: (19, {})} | custom-call | flops 939524096 | bytes 4718592 | tf_op jit(solution)/shard_map/cross/pallas_call | solution.py:185
  339.5 5.7 %cross.11 = f32[3,1,2,2,256,256]{5,4,3,2,1,0:T(8,128)} custom-call(s32[3]{0:T(128)} %get-tuple-element.38.wanted_ref, s32[16]{0:T(128)} %get-tuple-element.71.places_ref, bf16[8,2,112,128]{3,2,1,0:T(8,128)(2,1)} %get-tuple-element.52.refs_0_, bf16[8,2,112,128]{3,2,1,0:T(8,128)(2,1)} %copy-done.7, ...), custom_call_target="tpu_custom_call", output_to_operand_aliasing={{}: (19, {})} | custom-call | flops 939524096 | bytes 4718592 | tf_op jit(solution)/shard_map/cross/pallas_call | solution.py:185
  (136 shorter events, 28.8 us)
Async XLA Ops:
  6.2 102.6 %all-to-all-start = ((bf16[128,2,112,128]{3,2,1,0:T(8,128)(2,1)}), bf16[128,2,112,128]{3,2,1,0:T(8,128)(2,1)}, u32[]{:S(2)}, u32[]{:S(2)}) async-start(bf16[128,2,112,128]{3,2,1,0:T(8,128)(2,1)} %bitcast.98), calls=%async_computation | async-start | bytes 14680064 | tf_op jit(solution)/shard_map/all_to_all | solution.py:226
  114.0 120.2 %all-to-all-start.1 = ((bf16[8,20,112,128]{3,2,1,0:T(8,128)(2,1)}), bf16[8,20,112,128]{3,2,1,0:T(8,128)(2,1)}, u32[]{:S(2)}, u32[]{:S(2)}) async-start(bf16[8,20,112,128]{3,2,1,0:T(8,128)(2,1)} %pick.4), calls=%async_computation.1 | async-start | bytes 9175040 | tf_op jit(solution)/shard_map/all_to_all | solution.py:247
  125.6 35.3 %collective-permute-start.19 = (bf16[8,2,112,128]{3,2,1,0:T(8,128)(2,1)S(1)}, bf16[8,2,112,128]{3,2,1,0:T(8,128)(2,1)S(1)}, u32[]{:S(2)}, u32[]{:S(2)}) collective-permute-start(bf16[8,2,112,128]{3,2,1,0:T(8,128)(2,1)S(1)} %get-tuple-element.39), channel_id=1, source_target_pairs={{0,70},{1,71},{2,68},{3,69},{4,66},{5,67},{6,64},{7,65},{64,6},{65... | collective-permute-start | bytes 1376264 | tf_op jit(solution)/shard_map/ppermute | solution.py:274
  127.6 37.5 %collective-permute-start.18 = (bf16[8,2,112,128]{3,2,1,0:T(8,128)(2,1)S(1)}, bf16[8,2,112,128]{3,2,1,0:T(8,128)(2,1)S(1)}, u32[]{:S(2)}, u32[]{:S(2)}) collective-permute-start(bf16[8,2,112,128]{3,2,1,0:T(8,128)(2,1)S(1)} %get-tuple-element.40), channel_id=1, source_target_pairs={{0,67},{1,64},{2,65},{3,66},{4,71},{5,68},{6,69},{7,70},{64,3},{65... | collective-permute-start | bytes 1376264 | tf_op jit(solution)/shard_map/ppermute | solution.py:274
  130.8 40.6 %collective-permute-start.17 = (bf16[8,2,112,128]{3,2,1,0:T(8,128)(2,1)S(1)}, bf16[8,2,112,128]{3,2,1,0:T(8,128)(2,1)S(1)}, u32[]{:S(2)}, u32[]{:S(2)}) collective-permute-start(bf16[8,2,112,128]{3,2,1,0:T(8,128)(2,1)S(1)} %get-tuple-element.41), channel_id=1, source_target_pairs={{0,71},{1,68},{2,69},{3,70},{4,67},{5,64},{6,65},{7,66},{64,7},{65... | collective-permute-start | bytes 1376264 | tf_op jit(solution)/shard_map/ppermute | solution.py:274
  132.5 41.6 %collective-permute-start.16 = (bf16[8,2,112,128]{3,2,1,0:T(8,128)(2,1)S(1)}, bf16[8,2,112,128]{3,2,1,0:T(8,128)(2,1)S(1)}, u32[]{:S(2)}, u32[]{:S(2)}) collective-permute-start(bf16[8,2,112,128]{3,2,1,0:T(8,128)(2,1)S(1)} %get-tuple-element.42), channel_id=1, source_target_pairs={{0,64},{1,65},{2,66},{3,67},{4,68},{5,69},{6,70},{7,71},{64,0},{65... | collective-permute-start | bytes 1376264 | tf_op jit(solution)/shard_map/ppermute | solution.py:274
  133.1 49.2 %collective-permute-start.15 = (bf16[8,2,112,128]{3,2,1,0:T(8,128)(2,1)S(1)}, bf16[8,2,112,128]{3,2,1,0:T(8,128)(2,1)S(1)}, u32[]{:S(2)}, u32[]{:S(2)}) collective-permute-start(bf16[8,2,112,128]{3,2,1,0:T(8,128)(2,1)S(1)} %get-tuple-element.43), channel_id=1, source_target_pairs={{0,69},{1,70},{2,71},{3,68},{4,65},{5,66},{6,67},{7,64},{64,5},{65... | collective-permute-start | bytes 1376264 | tf_op jit(solution)/shard_map/ppermute | solution.py:274
  161.0 30.2 %collective-permute-start.14 = (bf16[8,2,112,128]{3,2,1,0:T(8,128)(2,1)}, bf16[8,2,112,128]{3,2,1,0:T(8,128)(2,1)S(1)}, u32[]{:S(2)}, u32[]{:S(2)}) collective-permute-start(bf16[8,2,112,128]{3,2,1,0:T(8,128)(2,1)} %get-tuple-element.44), channel_id=1, source_target_pairs={{0,68},{1,69},{2,70},{3,71},{4,64},{5,65},{6,66},{7,67},{64,4},{65... | collective-permute-start | bytes 1376264 | tf_op jit(solution)/shard_map/ppermute | solution.py:274
  165.0 32.8 %collective-permute-start.6 = (bf16[8,2,112,128]{3,2,1,0:T(8,128)(2,1)}, bf16[8,2,112,128]{3,2,1,0:T(8,128)(2,1)S(1)}, u32[]{:S(2)}, u32[]{:S(2)}) collective-permute-start(bf16[8,2,112,128]{3,2,1,0:T(8,128)(2,1)} %get-tuple-element.45), channel_id=1, source_target_pairs={{0,2},{1,3},{2,0},{3,1},{4,6},{5,7},{6,4},{7,5},{64,66},{65,67},{6... | collective-permute-start | bytes 1376264 | tf_op jit(solution)/shard_map/ppermute | solution.py:274
  171.4 38.8 %collective-permute-start.5 = (bf16[8,2,112,128]{3,2,1,0:T(8,128)(2,1)}, bf16[8,2,112,128]{3,2,1,0:T(8,128)(2,1)}, u32[]{:S(2)}, u32[]{:S(2)}) collective-permute-start(bf16[8,2,112,128]{3,2,1,0:T(8,128)(2,1)} %get-tuple-element.46), channel_id=1, source_target_pairs={{0,3},{1,0},{2,1},{3,2},{4,7},{5,4},{6,5},{7,6},{64,67},{65,64},{6... | collective-permute-start | bytes 1376264 | tf_op jit(solution)/shard_map/ppermute | solution.py:274
  174.1 44.6 %collective-permute-start.4 = (bf16[8,2,112,128]{3,2,1,0:T(8,128)(2,1)}, bf16[8,2,112,128]{3,2,1,0:T(8,128)(2,1)}, u32[]{:S(2)}, u32[]{:S(2)}) collective-permute-start(bf16[8,2,112,128]{3,2,1,0:T(8,128)(2,1)} %get-tuple-element.47), channel_id=1, source_target_pairs={{0,1},{1,2},{2,3},{3,0},{4,5},{5,6},{6,7},{7,4},{64,65},{65,66},{6... | collective-permute-start | bytes 1376264 | tf_op jit(solution)/shard_map/ppermute | solution.py:274
  182.2 38.6 %collective-permute-start.3 = (bf16[8,2,112,128]{3,2,1,0:T(8,128)(2,1)}, bf16[8,2,112,128]{3,2,1,0:T(8,128)(2,1)}, u32[]{:S(2)}, u32[]{:S(2)}) collective-permute-start(bf16[8,2,112,128]{3,2,1,0:T(8,128)(2,1)} %get-tuple-element.48), channel_id=1, source_target_pairs={{0,6},{1,7},{2,4},{3,5},{4,2},{5,3},{6,0},{7,1},{64,70},{65,71},{6... | collective-permute-start | bytes 1376264 | tf_op jit(solution)/shard_map/ppermute | solution.py:274
  191.2 29.7 %collective-permute-start.2 = (bf16[8,2,112,128]{3,2,1,0:T(8,128)(2,1)}, bf16[8,2,112,128]{3,2,1,0:T(8,128)(2,1)}, u32[]{:S(2)}, u32[]{:S(2)}) collective-permute-start(bf16[8,2,112,128]{3,2,1,0:T(8,128)(2,1)} %get-tuple-element.49), channel_id=1, source_target_pairs={{0,7},{1,4},{2,5},{3,6},{4,3},{5,0},{6,1},{7,2},{64,71},{65,68},{6... | collective-permute-start | bytes 1376264 | tf_op jit(solution)/shard_map/ppermute | solution.py:274
  197.8 26.0 %collective-permute-start.1 = (bf16[8,2,112,128]{3,2,1,0:T(8,128)(2,1)}, bf16[8,2,112,128]{3,2,1,0:T(8,128)(2,1)}, u32[]{:S(2)}, u32[]{:S(2)}) collective-permute-start(bf16[8,2,112,128]{3,2,1,0:T(8,128)(2,1)} %get-tuple-element.50), channel_id=1, source_target_pairs={{0,5},{1,6},{2,7},{3,4},{4,1},{5,2},{6,3},{7,0},{64,69},{65,70},{6... | collective-permute-start | bytes 1376264 | tf_op jit(solution)/shard_map/ppermute | solution.py:274
  210.2 13.6 %collective-permute-start.20 = (bf16[16,112,128]{2,1,0:T(8,128)(2,1)}, bf16[16,112,128]{2,1,0:T(8,128)(2,1)}, u32[]{:S(2)}, u32[]{:S(2)}) collective-permute-start(bf16[16,112,128]{2,1,0:T(8,128)(2,1)} %get-tuple-element.30), channel_id=1, source_target_pairs={{0,16},{8,24},{16,32},{24,40},{32,48},{40,56},{48,0},{56,8},{1,17}... | collective-permute-start | bytes 1376264 | tf_op jit(solution)/shard_map/ppermute | solution.py:253
  218.7 20.9 %collective-permute-start.21 = (bf16[16,112,128]{2,1,0:T(8,128)(2,1)}, bf16[16,112,128]{2,1,0:T(8,128)(2,1)}, u32[]{:S(2)}, u32[]{:S(2)}) collective-permute-start(bf16[16,112,128]{2,1,0:T(8,128)(2,1)} %get-tuple-element.31), channel_id=1, source_target_pairs={{0,48},{8,56},{16,0},{24,8},{32,16},{40,24},{48,32},{56,40},{1,49}... | collective-permute-start | bytes 1376264 | tf_op jit(solution)/shard_map/ppermute | solution.py:253
  220.9 34.2 %collective-permute-start.22 = (bf16[16,112,128]{2,1,0:T(8,128)(2,1)}, bf16[16,112,128]{2,1,0:T(8,128)(2,1)}, u32[]{:S(2)}, u32[]{:S(2)}) collective-permute-start(bf16[16,112,128]{2,1,0:T(8,128)(2,1)} %get-tuple-element.32), channel_id=1, source_target_pairs={{0,24},{8,16},{16,40},{24,32},{32,56},{40,48},{48,8},{56,0},{1,25}... | collective-permute-start | bytes 1376264 | tf_op jit(solution)/shard_map/ppermute | solution.py:253
  220.9 34.2 %collective-permute-start.23 = (bf16[16,112,128]{2,1,0:T(8,128)(2,1)}, bf16[16,112,128]{2,1,0:T(8,128)(2,1)}, u32[]{:S(2)}, u32[]{:S(2)}) collective-permute-start(bf16[16,112,128]{2,1,0:T(8,128)(2,1)} %get-tuple-element.33), channel_id=1, source_target_pairs={{0,56},{8,48},{16,8},{24,0},{32,24},{40,16},{48,40},{56,32},{1,57}... | collective-permute-start | bytes 1376264 | tf_op jit(solution)/shard_map/ppermute | solution.py:253
  223.8 40.6 %collective-permute-start.24 = (bf16[16,112,128]{2,1,0:T(8,128)(2,1)}, bf16[16,112,128]{2,1,0:T(8,128)(2,1)}, u32[]{:S(2)}, u32[]{:S(2)}) collective-permute-start(bf16[16,112,128]{2,1,0:T(8,128)(2,1)} %get-tuple-element.34), channel_id=1, source_target_pairs={{0,32},{8,40},{16,48},{24,56},{32,0},{40,8},{48,16},{56,24},{1,33}... | collective-permute-start | bytes 1376264 | tf_op jit(solution)/shard_map/ppermute | solution.py:253
  223.8 40.6 %collective-permute-start.25 = (bf16[16,112,128]{2,1,0:T(8,128)(2,1)}, bf16[16,112,128]{2,1,0:T(8,128)(2,1)}, u32[]{:S(2)}, u32[]{:S(2)}) collective-permute-start(bf16[16,112,128]{2,1,0:T(8,128)(2,1)} %get-tuple-element.35), channel_id=1, source_target_pairs={{0,40},{8,32},{16,56},{24,48},{32,8},{40,0},{48,24},{56,16},{1,41}... | collective-permute-start | bytes 1376264 | tf_op jit(solution)/shard_map/ppermute | solution.py:253
  239.6 34.5 %collective-permute-start.26 = (bf16[16,112,128]{2,1,0:T(8,128)(2,1)}, bf16[16,112,128]{2,1,0:T(8,128)(2,1)S(1)}, u32[]{:S(2)}, u32[]{:S(2)}) collective-permute-start(bf16[16,112,128]{2,1,0:T(8,128)(2,1)} %get-tuple-element.36), channel_id=1, source_target_pairs={{0,8},{8,0},{16,24},{24,16},{32,40},{40,32},{48,56},{56,48},{1,9},... | collective-permute-start | bytes 1376264 | tf_op jit(solution)/shard_map/ppermute | solution.py:253
  255.1 57.0 %collective-permute-start.29 = (f32[2,2,256,256]{3,2,1,0:T(8,128)}, f32[2,2,256,256]{3,2,1,0:T(8,128)}, u32[]{:S(2)}, u32[]{:S(2)}) collective-permute-start(f32[2,2,256,256]{3,2,1,0:T(8,128)} %cross.8), channel_id=1, source_target_pairs={{0,64},{64,0},{1,65},{65,1},{2,66},{66,2},{3,67},{67,3},{4,68},{68... | collective-permute-start | bytes 3145736 | tf_op jit(solution)/shard_map/ppermute | solution.py:293
  255.1 38.8 %collective-permute-start = (bf16[8,2,112,128]{3,2,1,0:T(8,128)(2,1)}, bf16[8,2,112,128]{3,2,1,0:T(8,128)(2,1)S(1)}, u32[]{:S(2)}, u32[]{:S(2)}) collective-permute-start(bf16[8,2,112,128]{3,2,1,0:T(8,128)(2,1)} %get-tuple-element.51), channel_id=1, source_target_pairs={{0,4},{1,5},{2,6},{3,7},{4,0},{5,1},{6,2},{7,3},{64,68},{65,69},{6... | collective-permute-start | bytes 1376264 | tf_op jit(solution)/shard_map/ppermute | solution.py:274
  264.4 30.3 %collective-permute-start.7 = (bf16[16,112,128]{2,1,0:T(8,128)(2,1)}, bf16[16,112,128]{2,1,0:T(8,128)(2,1)S(1)}, u32[]{:S(2)}, u32[]{:S(2)}) collective-permute-start(bf16[16,112,128]{2,1,0:T(8,128)(2,1)} %get-tuple-element.22), channel_id=1, source_target_pairs={{0,16},{8,24},{16,32},{24,40},{32,48},{40,56},{48,0},{56,8},{1,17}... | collective-permute-start | bytes 1376264 | tf_op jit(solution)/shard_map/ppermute | solution.py:253
  264.5 30.3 %collective-permute-start.8 = (bf16[16,112,128]{2,1,0:T(8,128)(2,1)}, bf16[16,112,128]{2,1,0:T(8,128)(2,1)S(1)}, u32[]{:S(2)}, u32[]{:S(2)}) collective-permute-start(bf16[16,112,128]{2,1,0:T(8,128)(2,1)} %get-tuple-element.23), channel_id=1, source_target_pairs={{0,48},{8,56},{16,0},{24,8},{32,16},{40,24},{48,32},{56,40},{1,49}... | collective-permute-start | bytes 1376264 | tf_op jit(solution)/shard_map/ppermute | solution.py:253
  274.1 59.0 %collective-permute-start.28 = (f32[2,2,256,256]{3,2,1,0:T(8,128)}, f32[2,2,256,256]{3,2,1,0:T(8,128)}, u32[]{:S(2)}, u32[]{:S(2)}) collective-permute-start(f32[2,2,256,256]{3,2,1,0:T(8,128)} %cross.7), channel_id=1, source_target_pairs={{0,64},{64,0},{1,65},{65,1},{2,66},{66,2},{3,67},{67,3},{4,68},{68... | collective-permute-start | bytes 3145736 | tf_op jit(solution)/shard_map/ppermute | solution.py:293
  293.9 45.6 %collective-permute-start.27 = (f32[2,2,256,256]{3,2,1,0:T(8,128)}, f32[2,2,256,256]{3,2,1,0:T(8,128)}, u32[]{:S(2)}, u32[]{:S(2)}) collective-permute-start(f32[2,2,256,256]{3,2,1,0:T(8,128)} %cross.6), channel_id=1, source_target_pairs={{0,64},{64,0},{1,65},{65,1},{2,66},{66,2},{3,67},{67,3},{4,68},{68... | collective-permute-start | bytes 3145736 | tf_op jit(solution)/shard_map/ppermute | solution.py:293
  294.7 14.2 %collective-permute-start.9 = (bf16[16,112,128]{2,1,0:T(8,128)(2,1)S(1)}, bf16[16,112,128]{2,1,0:T(8,128)(2,1)S(1)}, u32[]{:S(2)}, u32[]{:S(2)}) collective-permute-start(bf16[16,112,128]{2,1,0:T(8,128)(2,1)S(1)} %copy-done.26), channel_id=1, source_target_pairs={{0,24},{8,16},{16,40},{24,32},{32,56},{40,48},{48,8},{56,0},{1,25}... | collective-permute-start | bytes 1376264 | tf_op jit(solution)/shard_map/ppermute | solution.py:253
  294.8 14.1 %collective-permute-start.10 = (bf16[16,112,128]{2,1,0:T(8,128)(2,1)S(1)}, bf16[16,112,128]{2,1,0:T(8,128)(2,1)S(1)}, u32[]{:S(2)}, u32[]{:S(2)}) collective-permute-start(bf16[16,112,128]{2,1,0:T(8,128)(2,1)S(1)} %copy-done.25), channel_id=1, source_target_pairs={{0,56},{8,48},{16,8},{24,0},{32,24},{40,16},{48,40},{56,32},{1,57}... | collective-permute-start | bytes 1376264 | tf_op jit(solution)/shard_map/ppermute | solution.py:253
  308.9 13.9 %collective-permute-start.11 = (bf16[16,112,128]{2,1,0:T(8,128)(2,1)}, bf16[16,112,128]{2,1,0:T(8,128)(2,1)S(1)}, u32[]{:S(2)}, u32[]{:S(2)}) collective-permute-start(bf16[16,112,128]{2,1,0:T(8,128)(2,1)} %get-tuple-element.26), channel_id=1, source_target_pairs={{0,32},{8,40},{16,48},{24,56},{32,0},{40,8},{48,16},{56,24},{1,33}... | collective-permute-start | bytes 1376264 | tf_op jit(solution)/shard_map/ppermute | solution.py:253
  308.9 24.2 %collective-permute-start.12 = (bf16[16,112,128]{2,1,0:T(8,128)(2,1)}, bf16[16,112,128]{2,1,0:T(8,128)(2,1)S(1)}, u32[]{:S(2)}, u32[]{:S(2)}) collective-permute-start(bf16[16,112,128]{2,1,0:T(8,128)(2,1)} %get-tuple-element.27), channel_id=1, source_target_pairs={{0,40},{8,32},{16,56},{24,48},{32,8},{40,0},{48,24},{56,16},{1,41}... | collective-permute-start | bytes 1376264 | tf_op jit(solution)/shard_map/ppermute | solution.py:253
  312.0 21.1 %collective-permute-start.13 = (bf16[16,112,128]{2,1,0:T(8,128)(2,1)}, bf16[16,112,128]{2,1,0:T(8,128)(2,1)}, u32[]{:S(2)}, u32[]{:S(2)}) collective-permute-start(bf16[16,112,128]{2,1,0:T(8,128)(2,1)} %get-tuple-element.28), channel_id=1, source_target_pairs={{0,8},{8,0},{16,24},{24,16},{32,40},{40,32},{48,56},{56,48},{1,9},... | collective-permute-start | bytes 1376264 | tf_op jit(solution)/shard_map/ppermute | solution.py:253
  (27 other events, 660.5 us)

commit v5 on v4

--- a/solution.py
+++ b/solution.py
@@ -129,20 +129,21 @@
     sides = 2
     quarters = shares // (mine * sides)
     depth = groups * rows
-    odd = lax.broadcasted_iota(jnp.int32, (depth // 8, 8, lanes * sides), 1) % 2 == 1
+    odd = lax.broadcasted_iota(jnp.int32, (quarters * depth // 8, 8, lanes * sides), 1) % 2 == 1
     for e in range(mine):
-        real = None
-        for q in range(quarters):
-            at = (q * mine + e) * sides
-            a = jnp.concatenate([own_ref[at + s].reshape(depth, lanes) for s in range(sides)], axis=1)
-            b = jnp.concatenate([other_ref[at + s].reshape(depth, lanes) for s in range(sides)], axis=1)
-            tall = b.astype(jnp.float32).reshape(depth // 8, 8, lanes * sides)
-            turned = jnp.where(odd, pltpu.roll(tall, 1, 1), -pltpu.roll(tall, 7, 1))
-            turned = turned.reshape(depth, lanes * sides).astype(b.dtype)
-            dims = (((0,), (0,)), ((), ()))
-            re = lax.dot_general(a, b, dims, preferred_element_type=jnp.float32)
-            im = lax.dot_general(a, turned, dims, preferred_element_type=jnp.float32)
-            real, imag = (re, im) if real is None else (real + re, imag + im)
+        at = [[(q * mine + e) * sides + s for q in range(quarters)] for s in range(sides)]
+        a = jnp.concatenate(
+            [jnp.concatenate([own_ref[n].reshape(depth, lanes) for n in rest], axis=0) for rest in at], axis=1
+        )
+        b = jnp.concatenate(
+            [jnp.concatenate([other_ref[n].reshape(depth, lanes) for n in rest], axis=0) for rest in at], axis=1
+        )
+        tall = b.astype(jnp.float32).reshape(quarters * depth // 8, 8, lanes * sides)
+        turned = jnp.where(odd, pltpu.roll(tall, 1, 1), -pltpu.roll(tall, 7, 1))
+        turned = turned.reshape(quarters * depth, lanes * sides).astype(b.dtype)
+        both = jnp.concatenate([b, turned], axis=1)
+        both = lax.dot_general(a, both, (((0,), (0,)), ((), ())), preferred_element_type=jnp.float32)
+        real, imag = both[:, : lanes * sides], both[:, lanes * sides :]
         if fused:
             back_ref = refs[0]
             real, imag = (real + back_ref[e, 0]) * scale, (imag + back_ref[e, 1]) * scale
@@ -206,7 +207,7 @@
 HOPS += [(0, 0, 1), (0, 0, 3), (0, 0, 2)]
 FETCHED = (1, 2)
 TURNS = [(0, 0), (1, 0), (3, 0), (1, 1), (3, 1), (2, 0), (2, 1), (0, 1)]
-PARTS = [[(0, 0), (0, 1)], [(0, 2), (1, 0)], [(1, 1), (1, 2)]]
+PARTS = [[(0, 0)], [(0, 1), (0, 2)], [(1, 0), (1, 1)], [(1, 2)]]
 
 
 def per_device(spectra, partner):

time: 346 us -> 359 us (1.038)
  starting transfers between devices: 66.8 us -> 93.2 us
  waiting for transfers between devices: 209 us -> 193 us
    ppermute x14 -> x21, starting transfers between devices: 20.7 us -> 43.6 us  [fetch(): arrived.append(lax.ppermute(outs[k + 1], ZC, table))]
    ppermute x13, waiting for transfers between devices: 79.3 us -> 63.3 us  [per_device(): own[fx].append(lax.ppermute(part, XY, table))]
    ppermute x3, starting transfers between devices: 1.86 us -> 9.65 us  [per_device(): backs.append(lax.ppermute(away, 'xh', [(0, 1), (1, 0)]))]
    ppermute x3, waiting for transfers between devices: 0.01 us -> 7.24 us  [per_device(): backs.append(lax.ppermute(away, 'xh', [(0, 1), (1, 0)]))]
    ppermute x14 -> x21, waiting for transfers between devices: 41.6 us -> 34.6 us  [fetch(): arrived.append(lax.ppermute(outs[k + 1], ZC, table))]
    ppermute x13, starting transfers between devices: 25.8 us -> 21.7 us  [per_device(): own[fx].append(lax.ppermute(part, XY, table))]
    pallas_call x3 -> x4, Pallas kernels: 13.5 us -> 15 us  [pick(): pl.pallas_call(functools.partial(pick_kernel, entries), out_shape=[jax.Sh...]
  transfers between devices with their start and end apart: 32 -> 39, of which waited for: 13 -> 13; matrix products, arithmetic and copies ran while one was open for 3% -> 3% of each run, Pallas kernels for 10% -> 11%
where the time goes in v5:
time: 359 us
  waiting for transfers between devices  193 us (54%)
  starting transfers between devices  93.2 us (26%)
  Pallas kernels  53.3 us (15%)
  local copies, waits for them, and re-layouts  10.1 us (3%)
  other arithmetic  4.82 us (1%)
  between operations  4.1 us (1%)
    all_to_all x1, waiting for transfers between devices, per_device(): lax.all_to_all(joint, ALL, split_axis=0, concat_axis=0, tiled=True)  87.9 us
    ppermute x13, waiting for transfers between devices, per_device(): own[fx].append(lax.ppermute(part, XY, table))  63.3 us
    ppermute x21, starting transfers between devices, fetch(): arrived.append(lax.ppermute(outs[k + 1], ZC, table))  43.6 us
    ppermute x21, waiting for transfers between devices, fetch(): arrived.append(lax.ppermute(outs[k + 1], ZC, table))  34.6 us
    pallas_call x6, Pallas kernels, cross(): pl.pallas_call(functools.partial(cross_kernel, (len(pieces), steps, share...  32.2 us
    ppermute x13, starting transfers between devices, per_device(): own[fx].append(lax.ppermute(part, XY, table))  21.7 us
    pallas_call x4, Pallas kernels, pick(): pl.pallas_call(functools.partial(pick_kernel, entries), out_shape=[jax.Sh...  15 us
    all_to_all x1, starting transfers between devices, per_device(): lax.all_to_all(joint, ALL, split_axis=0, concat_axis=0, tiled=True)  11.9 us
  transfers between devices with their start and end apart: 39, of which 13 were waited for; matrix products, arithmetic and copies ran while one was open for 3% of the time, Pallas kernels for 11%

profile of v5, /device:TPU:1, one launch (start us, length us, event | category | flops | bytes accessed | tf_op | source)
XLA Modules:
  0.0 358.6 jit_solution(1914448641332351072)
XLA Ops:
  0.0 6.1 %pack.1 = bf16[2,2,2,2,8,2,56,2,128]{8,7,6,5,4,3,2,1,0:T(2,128)(2,1)} custom-call(bf16[224,32,1,2,256]{4,3,2,1,0:T(2,128)(2,1)} %src.1), custom_call_target="tpu_custom_call" | custom-call | bytes 14680064 | tf_op jit(solution)/shard_map/pack/pallas_call | solution.py:46
  6.2 11.9 %all-to-all-start = ((bf16[128,2,112,128]{3,2,1,0:T(8,128)(2,1)}), bf16[128,2,112,128]{3,2,1,0:T(8,128)(2,1)}, u32[]{:S(2)}, u32[]{:S(2)}) async-start(bf16[128,2,112,128]{3,2,1,0:T(8,128)(2,1)} %bitcast.98), calls=%async_computation | async-start | bytes 14680064 | tf_op jit(solution)/shard_map/all_to_all | solution.py:227
  20.9 87.9 %all-to-all-done = bf16[128,2,112,128]{3,2,1,0:T(8,128)(2,1)} async-done(((bf16[128,2,112,128]{3,2,1,0:T(8,128)(2,1)}), bf16[128,2,112,128]{3,2,1,0:T(8,128)(2,1)}, u32[]{:S(2)}, u32[]{:S(2)}) %all-to-all-start) | async-done | bytes 7340064 | tf_op jit(solution)/shard_map/all_to_all | solution.py:227
  108.8 3.5 pick.5
  112.3 6.5 %all-to-all-start.1 = ((bf16[8,12,112,128]{3,2,1,0:T(8,128)(2,1)}), bf16[8,12,112,128]{3,2,1,0:T(8,128)(2,1)S(1)}, u32[]{:S(2)}, u32[]{:S(2)}) async-start(bf16[8,12,112,128]{3,2,1,0:T(8,128)(2,1)} %pick.5), calls=%async_computation.1 | async-start | bytes 5505024 | tf_op jit(solution)/shard_map/all_to_all | solution.py:248
  118.8 5.2 %dynamic-slice_bitcast_fusion = (bf16[8,2,112,128]{3,2,1,0:T(8,128)(2,1)S(1)}, bf16[8,2,112,128]{3,2,1,0:T(8,128)(2,1)S(1)}, bf16[8,2,112,128]{3,2,1,0:T(8,128)(...) fusion(bf16[2,8,8,2,112,128]{5,4,3,2,1,0:T(8,128)(2,1)} %bitcas, ...), kind=kLoop, calls=%fused_computation.1 | loop fusion | bytes 12845096 | tf_op jit(solution)/shard_map/reshape | solution.py:264
  125.9 3.1 collective-permute-start.18
  131.4 3.8 %collective-permute-start.15 = (bf16[8,2,112,128]{3,2,1,0:T(8,128)(2,1)S(1)}, bf16[8,2,112,128]{3,2,1,0:T(8,128)(2,1)}, u32[]{:S(2)}, u32[]{:S(2)}) collective-permute-start(bf16[8,2,112,128]{3,2,1,0:T(8,128)(2,1)S(1)} %get-tuple-element.59), channel_id=1, source_target_pairs={{0,69},{1,70},{2,71},{3,68},{4,65},{5,66},{6,67},{7,64},{64,5},{65... | collective-permute-start | bytes 1376264 | tf_op jit(solution)/shard_map/ppermute | solution.py:275
  135.2 24.1 %collective-permute-done.19.refs_5_ = bf16[8,2,112,128]{3,2,1,0:T(8,128)(2,1)S(1)} collective-permute-done((bf16[8,2,112,128]{3,2,1,0:T(8,128)(2,1)S(1)}, bf16[8,2,112,128]{3,2,1,0:T(8,128)(2,1)S(1)}, u32[]{:S(2)}, u32[]{:S(2)}) %collective-permute-start.19) | collective-permute-done | bytes 458784 | tf_op jit(solution)/shard_map/ppermute | solution.py:275
  162.6 6.8 %collective-permute-done.17.refs_3_ = bf16[8,2,112,128]{3,2,1,0:T(8,128)(2,1)} collective-permute-done((bf16[8,2,112,128]{3,2,1,0:T(8,128)(2,1)S(1)}, bf16[8,2,112,128]{3,2,1,0:T(8,128)(2,1)}, u32[]{:S(2)}, u32[]{:S(2)}) %collective-permute-start.17) | collective-permute-done | bytes 458784 | tf_op jit(solution)/shard_map/ppermute | solution.py:275
  172.8 6.5 %collective-permute-done.15.refs_1_ = bf16[8,2,112,128]{3,2,1,0:T(8,128)(2,1)} collective-permute-done((bf16[8,2,112,128]{3,2,1,0:T(8,128)(2,1)S(1)}, bf16[8,2,112,128]{3,2,1,0:T(8,128)(2,1)}, u32[]{:S(2)}, u32[]{:S(2)}) %collective-permute-start.15) | collective-permute-done | bytes 458784 | tf_op jit(solution)/shard_map/ppermute | solution.py:275
  180.6 9.0 %collective-permute-done.14.refs_0_ = bf16[8,2,112,128]{3,2,1,0:T(8,128)(2,1)} collective-permute-done((bf16[8,2,112,128]{3,2,1,0:T(8,128)(2,1)S(1)}, bf16[8,2,112,128]{3,2,1,0:T(8,128)(2,1)}, u32[]{:S(2)}, u32[]{:S(2)}) %collective-permute-start.14) | collective-permute-done | bytes 458784 | tf_op jit(solution)/shard_map/ppermute | solution.py:275
  192.5 16.9 %collective-permute-done.5.refs_6_ = bf16[8,2,112,128]{3,2,1,0:T(8,128)(2,1)} collective-permute-done((bf16[8,2,112,128]{3,2,1,0:T(8,128)(2,1)}, bf16[8,2,112,128]{3,2,1,0:T(8,128)(2,1)}, u32[]{:S(2)}, u32[]{:S(2)}) %collective-permute-start.5) | collective-permute-done | bytes 458784 | tf_op jit(solution)/shard_map/ppermute | solution.py:275
  210.2 4.2 %pick.6 = (bf16[16,112,128]{2,1,0:T(8,128)(2,1)}, bf16[16,112,128]{2,1,0:T(8,128)(2,1)}, bf16[16,112,128]{2,1,0:T(8,128)(2,1)}, bf16[16,112,128]{2,1,0:T(8,128)(...) custom-call(s32[40]{0:T(128)} %get-tuple-element.90.meta, ...), custom_call_target="tpu_custom_call" | custom-call | bytes 7340032 | tf_op jit(solution)/shard_map/pick/pallas_call | solution.py:97
  218.1 3.2 pick.4
  226.1 5.8 %collective-permute-done.7.refs_9_ = bf16[8,112,128]{2,1,0:T(8,128)(2,1)S(1)} collective-permute-done((bf16[8,112,128]{2,1,0:T(8,128)(2,1)}, bf16[8,112,128]{2,1,0:T(8,128)(2,1)S(1)}, u32[]{:S(2)}, u32[]{:S(2)}) %collective-permute-start.7) | collective-permute-done | bytes 229408 | tf_op jit(solution)/shard_map/ppermute | solution.py:254
  234.4 4.5 %collective-permute-start.25 = (bf16[16,112,128]{2,1,0:T(8,128)(2,1)}, bf16[16,112,128]{2,1,0:T(8,128)(2,1)}, u32[]{:S(2)}, u32[]{:S(2)}) collective-permute-start(bf16[16,112,128]{2,1,0:T(8,128)(2,1)} %get-tuple-element.43), channel_id=1, source_target_pairs={{0,40},{8,32},{16,56},{24,48},{32,8},{40,0},{48,24},{56,16},{1,41}... | collective-permute-start | bytes 1376264 | tf_op jit(solution)/shard_map/ppermute | solution.py:254
  238.9 4.2 %pick.7 = (bf16[16,112,128]{2,1,0:T(8,128)(2,1)}, bf16[16,112,128]{2,1,0:T(8,128)(2,1)}, bf16[16,112,128]{2,1,0:T(8,128)(2,1)}, bf16[16,112,128]{2,1,0:T(8,128)(...) custom-call(s32[40]{0:T(128)} %get-tuple-element.89.meta, ...), custom_call_target="tpu_custom_call" | custom-call | bytes 7340032 | tf_op jit(solution)/shard_map/pick/pallas_call | solution.py:97
  246.1 7.4 %collective-permute-done.24.refs_27_ = bf16[16,112,128]{2,1,0:T(8,128)(2,1)} collective-permute-done((bf16[16,112,128]{2,1,0:T(8,128)(2,1)}, bf16[16,112,128]{2,1,0:T(8,128)(2,1)}, u32[]{:S(2)}, u32[]{:S(2)}) %collective-permute-start.24) | collective-permute-done | bytes 458784 | tf_op jit(solution)/shard_map/ppermute | solution.py:254
  253.5 10.9 %collective-permute-start.29 = (bf16[16,112,128]{2,1,0:T(8,128)(2,1)}, bf16[16,112,128]{2,1,0:T(8,128)(2,1)}, u32[]{:S(2)}, u32[]{:S(2)}) collective-permute-start(bf16[16,112,128]{2,1,0:T(8,128)(2,1)} %get-tuple-element.47), channel_id=1, source_target_pairs={{0,48},{8,56},{16,0},{24,8},{32,16},{40,24},{48,32},{56,40},{1,49}... | collective-permute-start | bytes 1376264 | tf_op jit(solution)/shard_map/ppermute | solution.py:254
  273.4 5.2 %cross.7 = f32[2,2,256,256]{3,2,1,0:T(8,128)} custom-call(s32[3]{0:T(128)} %get-tuple-element.53.wanted_ref, s32[16]{0:T(128)} %get-tuple-element.86.places_ref, bf16[8,2,112,128]{3,2,1,0:T(8,128)(2,1)} %collective-permute-done.14.refs_0_, bf16[8,2,112,128]{3,2,1,0:T(8,128)(2,1)} %collective-permute-done.15.refs_1_, ...), custom_call_target="tpu_custom_call" | custom-call | flops 939524096 | bytes 4718592 | tf_op jit(solution)/shard_map/cross/pallas_call | solution.py:186
  278.6 6.5 %collective-permute-start.35 = (f32[2,2,256,256]{3,2,1,0:T(8,128)}, f32[2,2,256,256]{3,2,1,0:T(8,128)}, u32[]{:S(2)}, u32[]{:S(2)}) collective-permute-start(f32[2,2,256,256]{3,2,1,0:T(8,128)} %cross.7), channel_id=1, source_target_pairs={{0,64},{64,0},{1,65},{65,1},{2,66},{66,2},{3,67},{67,3},{4,68},{68... | collective-permute-start | bytes 3145736 | tf_op jit(solution)/shard_map/ppermute | solution.py:294
  285.0 5.3 %cross.8 = f32[2,2,256,256]{3,2,1,0:T(8,128)} custom-call(s32[3]{0:T(128)} %get-tuple-element.53.wanted_ref, s32[16]{0:T(128)} %get-tuple-element.85.places_ref, bf16[8,2,112,128]{3,2,1,0:T(8,128)(2,1)} %collective-permute-done.14.refs_0_, bf16[8,2,112,128]{3,2,1,0:T(8,128)(2,1)} %collective-permute-done.15.refs_1_, ...), custom_call_target="tpu_custom_call" | custom-call | flops 939524096 | bytes 4718592 | tf_op jit(solution)/shard_map/cross/pallas_call | solution.py:186
  292.9 5.2 %cross.6 = f32[2,2,256,256]{3,2,1,0:T(8,128)} custom-call(s32[3]{0:T(128)} %get-tuple-element.53.wanted_ref, s32[16]{0:T(128)} %get-tuple-element.86.places_ref, bf16[8,2,112,128]{3,2,1,0:T(8,128)(2,1)} %collective-permute-done.14.refs_0_, bf16[8,2,112,128]{3,2,1,0:T(8,128)(2,1)} %collective-permute-done.15.refs_1_, ...), custom_call_target="tpu_custom_call" | custom-call | flops 939524096 | bytes 4718592 | tf_op jit(solution)/shard_map/cross/pallas_call | solution.py:186
  301.2 10.2 %collective-permute-done.31.refs_12_ = bf16[16,112,128]{2,1,0:T(8,128)(2,1)S(1)} collective-permute-done((bf16[16,112,128]{2,1,0:T(8,128)(2,1)S(1)}, bf16[16,112,128]{2,1,0:T(8,128)(2,1)S(1)}, u32[]{:S(2)}, u32[]{:S(2)}) %collective-permute-start.31) | collective-permute-done | bytes 458784 | tf_op jit(solution)/shard_map/ppermute | solution.py:254
  311.5 9.9 %collective-permute-done.33.refs_14_ = bf16[16,112,128]{2,1,0:T(8,128)(2,1)S(1)} collective-permute-done((bf16[16,112,128]{2,1,0:T(8,128)(2,1)}, bf16[16,112,128]{2,1,0:T(8,128)(2,1)S(1)}, u32[]{:S(2)}, u32[]{:S(2)}) %collective-permute-start.33) | collective-permute-done | bytes 458784 | tf_op jit(solution)/shard_map/ppermute | solution.py:254
  321.4 7.9 %collective-permute-start.10 = (bf16[8,112,128]{2,1,0:T(8,128)(2,1)}, bf16[8,112,128]{2,1,0:T(8,128)(2,1)S(1)}, u32[]{:S(2)}, u32[]{:S(2)}) collective-permute-start(bf16[8,112,128]{2,1,0:T(8,128)(2,1)} %get-tuple-element.33), channel_id=1, source_target_pairs={{0,56},{8,48},{16,8},{24,0},{32,24},{40,16},{48,40},{56,32},{1,57}... | collective-permute-start | bytes 688136 | tf_op jit(solution)/shard_map/ppermute | solution.py:254
  329.4 3.0 collective-permute-start.12
  332.7 5.5 %cross.9.refs_17_ = f32[3,1,2,2,256,256]{5,4,3,2,1,0:T(8,128)} custom-call(s32[3]{0:T(128)} %get-tuple-element.54.wanted_ref, s32[16]{0:T(128)} %get-tuple-element.87.places_ref, bf16[8,2,112,128]{3,2,1,0:T(8,128)(2,1)} %get-tuple-element.68.refs_0_, bf16[8,2,112,128]{3,2,1,0:T(8,128)(2,1)} %collective-permute-done.refs_1_, ...), custom_call_target="tpu_custom_call" | custom-call | flops 939524096 | bytes 4718592 | tf_op jit(solution)/shard_map/cross/pallas_call | solution.py:186
  338.3 5.5 %cross.10.refs_17_ = f32[3,1,2,2,256,256]{5,4,3,2,1,0:T(8,128)} custom-call(s32[3]{0:T(128)} %get-tuple-element.54.wanted_ref, s32[16]{0:T(128)} %get-tuple-element.87.places_ref, bf16[8,2,112,128]{3,2,1,0:T(8,128)(2,1)} %get-tuple-element.68.refs_0_, bf16[8,2,112,128]{3,2,1,0:T(8,128)(2,1)} %collective-permute-done.refs_1_, ...), custom_call_target="tpu_custom_call", output_to_operand_aliasing={{}: (19, {})} | custom-call | flops 939524096 | bytes 4718592 | tf_op jit(solution)/shard_map/cross/pallas_call | solution.py:186
  344.8 7.2 %collective-permute-done.27.refs_16_ = f32[2,2,256,256]{3,2,1,0:T(8,128)S(1)} collective-permute-done((f32[2,2,256,256]{3,2,1,0:T(8,128)}, f32[2,2,256,256]{3,2,1,0:T(8,128)S(1)}, u32[]{:S(2)}, u32[]{:S(2)}) %collective-permute-start.27) | collective-permute-done | bytes 1048608 | tf_op jit(solution)/shard_map/ppermute | solution.py:294
  353.1 5.5 %cross.11 = f32[3,1,2,2,256,256]{5,4,3,2,1,0:T(8,128)} custom-call(s32[3]{0:T(128)} %get-tuple-element.54.wanted_ref, s32[16]{0:T(128)} %get-tuple-element.87.places_ref, bf16[8,2,112,128]{3,2,1,0:T(8,128)(2,1)} %get-tuple-element.68.refs_0_, bf16[8,2,112,128]{3,2,1,0:T(8,128)(2,1)} %collective-permute-done.refs_1_, ...), custom_call_target="tpu_custom_call", output_to_operand_aliasing={{}: (19, {})} | custom-call | flops 939524096 | bytes 4718592 | tf_op jit(solution)/shard_map/cross/pallas_call | solution.py:186
  (141 shorter events, 46.1 us)
Async XLA Ops:
  6.2 102.6 %all-to-all-start = ((bf16[128,2,112,128]{3,2,1,0:T(8,128)(2,1)}), bf16[128,2,112,128]{3,2,1,0:T(8,128)(2,1)}, u32[]{:S(2)}, u32[]{:S(2)}) async-start(bf16[128,2,112,128]{3,2,1,0:T(8,128)(2,1)} %bitcast.98), calls=%async_computation | async-start | bytes 14680064 | tf_op jit(solution)/shard_map/all_to_all | solution.py:227
  112.3 159.5 %all-to-all-start.1 = ((bf16[8,12,112,128]{3,2,1,0:T(8,128)(2,1)}), bf16[8,12,112,128]{3,2,1,0:T(8,128)(2,1)S(1)}, u32[]{:S(2)}, u32[]{:S(2)}) async-start(bf16[8,12,112,128]{3,2,1,0:T(8,128)(2,1)} %pick.5), calls=%async_computation.1 | async-start | bytes 5505024 | tf_op jit(solution)/shard_map/all_to_all | solution.py:248
  124.0 35.3 %collective-permute-start.19 = (bf16[8,2,112,128]{3,2,1,0:T(8,128)(2,1)S(1)}, bf16[8,2,112,128]{3,2,1,0:T(8,128)(2,1)S(1)}, u32[]{:S(2)}, u32[]{:S(2)}) collective-permute-start(bf16[8,2,112,128]{3,2,1,0:T(8,128)(2,1)S(1)} %get-tuple-element.55), channel_id=1, source_target_pairs={{0,70},{1,71},{2,68},{3,69},{4,66},{5,67},{6,64},{7,65},{64,6},{65... | collective-permute-start | bytes 1376264 | tf_op jit(solution)/shard_map/ppermute | solution.py:275
  125.9 36.1 %collective-permute-start.18 = (bf16[8,2,112,128]{3,2,1,0:T(8,128)(2,1)S(1)}, bf16[8,2,112,128]{3,2,1,0:T(8,128)(2,1)}, u32[]{:S(2)}, u32[]{:S(2)}) collective-permute-start(bf16[8,2,112,128]{3,2,1,0:T(8,128)(2,1)S(1)} %get-tuple-element.56), channel_id=1, source_target_pairs={{0,67},{1,64},{2,65},{3,66},{4,71},{5,68},{6,69},{7,70},{64,3},{65... | collective-permute-start | bytes 1376264 | tf_op jit(solution)/shard_map/ppermute | solution.py:275
  129.0 40.4 %collective-permute-start.17 = (bf16[8,2,112,128]{3,2,1,0:T(8,128)(2,1)S(1)}, bf16[8,2,112,128]{3,2,1,0:T(8,128)(2,1)}, u32[]{:S(2)}, u32[]{:S(2)}) collective-permute-start(bf16[8,2,112,128]{3,2,1,0:T(8,128)(2,1)S(1)} %get-tuple-element.57), channel_id=1, source_target_pairs={{0,71},{1,68},{2,69},{3,70},{4,67},{5,64},{6,65},{7,66},{64,7},{65... | collective-permute-start | bytes 1376264 | tf_op jit(solution)/shard_map/ppermute | solution.py:275
  129.9 42.2 %collective-permute-start.16 = (bf16[8,2,112,128]{3,2,1,0:T(8,128)(2,1)S(1)}, bf16[8,2,112,128]{3,2,1,0:T(8,128)(2,1)}, u32[]{:S(2)}, u32[]{:S(2)}) collective-permute-start(bf16[8,2,112,128]{3,2,1,0:T(8,128)(2,1)S(1)} %get-tuple-element.58), channel_id=1, source_target_pairs={{0,64},{1,65},{2,66},{3,67},{4,68},{5,69},{6,70},{7,71},{64,0},{65... | collective-permute-start | bytes 1376264 | tf_op jit(solution)/shard_map/ppermute | solution.py:275
  131.4 47.8 %collective-permute-start.15 = (bf16[8,2,112,128]{3,2,1,0:T(8,128)(2,1)S(1)}, bf16[8,2,112,128]{3,2,1,0:T(8,128)(2,1)}, u32[]{:S(2)}, u32[]{:S(2)}) collective-permute-start(bf16[8,2,112,128]{3,2,1,0:T(8,128)(2,1)S(1)} %get-tuple-element.59), channel_id=1, source_target_pairs={{0,69},{1,70},{2,71},{3,68},{4,65},{5,66},{6,67},{7,64},{64,5},{65... | collective-permute-start | bytes 1376264 | tf_op jit(solution)/shard_map/ppermute | solution.py:275
  159.3 30.2 %collective-permute-start.14 = (bf16[8,2,112,128]{3,2,1,0:T(8,128)(2,1)S(1)}, bf16[8,2,112,128]{3,2,1,0:T(8,128)(2,1)}, u32[]{:S(2)}, u32[]{:S(2)}) collective-permute-start(bf16[8,2,112,128]{3,2,1,0:T(8,128)(2,1)S(1)} %get-tuple-element.60), channel_id=1, source_target_pairs={{0,68},{1,69},{2,70},{3,71},{4,64},{5,65},{6,66},{7,67},{64,4},{65... | collective-permute-start | bytes 1376264 | tf_op jit(solution)/shard_map/ppermute | solution.py:275
  162.0 28.4 %collective-permute-start.6 = (bf16[8,2,112,128]{3,2,1,0:T(8,128)(2,1)}, bf16[8,2,112,128]{3,2,1,0:T(8,128)(2,1)}, u32[]{:S(2)}, u32[]{:S(2)}) collective-permute-start(bf16[8,2,112,128]{3,2,1,0:T(8,128)(2,1)} %get-tuple-element.61), channel_id=1, source_target_pairs={{0,2},{1,3},{2,0},{3,1},{4,6},{5,7},{6,4},{7,5},{64,66},{65,67},{6... | collective-permute-start | bytes 1376264 | tf_op jit(solution)/shard_map/ppermute | solution.py:275
  169.4 40.1 %collective-permute-start.5 = (bf16[8,2,112,128]{3,2,1,0:T(8,128)(2,1)}, bf16[8,2,112,128]{3,2,1,0:T(8,128)(2,1)}, u32[]{:S(2)}, u32[]{:S(2)}) collective-permute-start(bf16[8,2,112,128]{3,2,1,0:T(8,128)(2,1)} %get-tuple-element.62), channel_id=1, source_target_pairs={{0,3},{1,0},{2,1},{3,2},{4,7},{5,4},{6,5},{7,6},{64,67},{65,64},{6... | collective-permute-start | bytes 1376264 | tf_op jit(solution)/shard_map/ppermute | solution.py:275
  172.1 42.3 %collective-permute-start.4 = (bf16[8,2,112,128]{3,2,1,0:T(8,128)(2,1)}, bf16[8,2,112,128]{3,2,1,0:T(8,128)(2,1)}, u32[]{:S(2)}, u32[]{:S(2)}) collective-permute-start(bf16[8,2,112,128]{3,2,1,0:T(8,128)(2,1)} %get-tuple-element.63), channel_id=1, source_target_pairs={{0,1},{1,2},{2,3},{3,0},{4,5},{5,6},{6,7},{7,4},{64,65},{65,66},{6... | collective-permute-start | bytes 1376264 | tf_op jit(solution)/shard_map/ppermute | solution.py:275
  179.2 36.7 %collective-permute-start.3 = (bf16[8,2,112,128]{3,2,1,0:T(8,128)(2,1)}, bf16[8,2,112,128]{3,2,1,0:T(8,128)(2,1)}, u32[]{:S(2)}, u32[]{:S(2)}) collective-permute-start(bf16[8,2,112,128]{3,2,1,0:T(8,128)(2,1)} %get-tuple-element.64), channel_id=1, source_target_pairs={{0,6},{1,7},{2,4},{3,5},{4,2},{5,3},{6,0},{7,1},{64,70},{65,71},{6... | collective-permute-start | bytes 1376264 | tf_op jit(solution)/shard_map/ppermute | solution.py:275
  189.5 31.8 %collective-permute-start.2 = (bf16[8,2,112,128]{3,2,1,0:T(8,128)(2,1)}, bf16[8,2,112,128]{3,2,1,0:T(8,128)(2,1)}, u32[]{:S(2)}, u32[]{:S(2)}) collective-permute-start(bf16[8,2,112,128]{3,2,1,0:T(8,128)(2,1)} %get-tuple-element.65), channel_id=1, source_target_pairs={{0,7},{1,4},{2,5},{3,6},{4,3},{5,0},{6,1},{7,2},{64,71},{65,68},{6... | collective-permute-start | bytes 1376264 | tf_op jit(solution)/shard_map/ppermute | solution.py:275
  190.4 31.0 %collective-permute-start.1 = (bf16[8,2,112,128]{3,2,1,0:T(8,128)(2,1)}, bf16[8,2,112,128]{3,2,1,0:T(8,128)(2,1)}, u32[]{:S(2)}, u32[]{:S(2)}) collective-permute-start(bf16[8,2,112,128]{3,2,1,0:T(8,128)(2,1)} %get-tuple-element.66), channel_id=1, source_target_pairs={{0,5},{1,6},{2,7},{3,4},{4,1},{5,2},{6,3},{7,0},{64,69},{65,70},{6... | collective-permute-start | bytes 1376264 | tf_op jit(solution)/shard_map/ppermute | solution.py:275
  214.4 20.0 %collective-permute-start.20 = (bf16[16,112,128]{2,1,0:T(8,128)(2,1)}, bf16[16,112,128]{2,1,0:T(8,128)(2,1)S(1)}, u32[]{:S(2)}, u32[]{:S(2)}) collective-permute-start(bf16[16,112,128]{2,1,0:T(8,128)(2,1)} %get-tuple-element.38), channel_id=1, source_target_pairs={{0,16},{8,24},{16,32},{24,40},{32,48},{40,56},{48,0},{56,8},{1,17}... | collective-permute-start | bytes 1376264 | tf_op jit(solution)/shard_map/ppermute | solution.py:254
  215.9 23.0 %collective-permute-start.21 = (bf16[16,112,128]{2,1,0:T(8,128)(2,1)}, bf16[16,112,128]{2,1,0:T(8,128)(2,1)}, u32[]{:S(2)}, u32[]{:S(2)}) collective-permute-start(bf16[16,112,128]{2,1,0:T(8,128)(2,1)} %get-tuple-element.39), channel_id=1, source_target_pairs={{0,48},{8,56},{16,0},{24,8},{32,16},{40,24},{48,32},{56,40},{1,49}... | collective-permute-start | bytes 1376264 | tf_op jit(solution)/shard_map/ppermute | solution.py:254
  221.4 21.9 %collective-permute-start.22 = (bf16[16,112,128]{2,1,0:T(8,128)(2,1)}, bf16[16,112,128]{2,1,0:T(8,128)(2,1)}, u32[]{:S(2)}, u32[]{:S(2)}) collective-permute-start(bf16[16,112,128]{2,1,0:T(8,128)(2,1)} %get-tuple-element.40), channel_id=1, source_target_pairs={{0,24},{8,16},{16,40},{24,32},{32,56},{40,48},{48,8},{56,0},{1,25}... | collective-permute-start | bytes 1376264 | tf_op jit(solution)/shard_map/ppermute | solution.py:254
  224.1 22.0 %collective-permute-start.23 = (bf16[16,112,128]{2,1,0:T(8,128)(2,1)}, bf16[16,112,128]{2,1,0:T(8,128)(2,1)}, u32[]{:S(2)}, u32[]{:S(2)}) collective-permute-start(bf16[16,112,128]{2,1,0:T(8,128)(2,1)} %get-tuple-element.41), channel_id=1, source_target_pairs={{0,56},{8,48},{16,8},{24,0},{32,24},{40,16},{48,40},{56,32},{1,57}... | collective-permute-start | bytes 1376264 | tf_op jit(solution)/shard_map/ppermute | solution.py:254
  231.9 21.6 %collective-permute-start.24 = (bf16[16,112,128]{2,1,0:T(8,128)(2,1)}, bf16[16,112,128]{2,1,0:T(8,128)(2,1)}, u32[]{:S(2)}, u32[]{:S(2)}) collective-permute-start(bf16[16,112,128]{2,1,0:T(8,128)(2,1)} %get-tuple-element.42), channel_id=1, source_target_pairs={{0,32},{8,40},{16,48},{24,56},{32,0},{40,8},{48,16},{56,24},{1,33}... | collective-permute-start | bytes 1376264 | tf_op jit(solution)/shard_map/ppermute | solution.py:254
  234.4 30.0 %collective-permute-start.25 = (bf16[16,112,128]{2,1,0:T(8,128)(2,1)}, bf16[16,112,128]{2,1,0:T(8,128)(2,1)}, u32[]{:S(2)}, u32[]{:S(2)}) collective-permute-start(bf16[16,112,128]{2,1,0:T(8,128)(2,1)} %get-tuple-element.43), channel_id=1, source_target_pairs={{0,40},{8,32},{16,56},{24,48},{32,8},{40,0},{48,24},{56,16},{1,41}... | collective-permute-start | bytes 1376264 | tf_op jit(solution)/shard_map/ppermute | solution.py:254
  238.9 25.8 %collective-permute-start.26 = (bf16[16,112,128]{2,1,0:T(8,128)(2,1)}, bf16[16,112,128]{2,1,0:T(8,128)(2,1)}, u32[]{:S(2)}, u32[]{:S(2)}) collective-permute-start(bf16[16,112,128]{2,1,0:T(8,128)(2,1)} %get-tuple-element.44), channel_id=1, source_target_pairs={{0,8},{8,0},{16,24},{24,16},{32,40},{40,32},{48,56},{56,48},{1,9},... | collective-permute-start | bytes 1376264 | tf_op jit(solution)/shard_map/ppermute | solution.py:254
  243.3 35.3 %collective-permute-start.8 = (bf16[8,112,128]{2,1,0:T(8,128)(2,1)}, bf16[8,112,128]{2,1,0:T(8,128)(2,1)S(1)}, u32[]{:S(2)}, u32[]{:S(2)}) collective-permute-start(bf16[8,112,128]{2,1,0:T(8,128)(2,1)} %get-tuple-element.31), channel_id=1, source_target_pairs={{0,48},{8,56},{16,0},{24,8},{32,16},{40,24},{48,32},{56,40},{1,49}... | collective-permute-start | bytes 688136 | tf_op jit(solution)/shard_map/ppermute | solution.py:254
  246.1 44.4 %collective-permute-start.28 = (bf16[16,112,128]{2,1,0:T(8,128)(2,1)}, bf16[16,112,128]{2,1,0:T(8,128)(2,1)S(1)}, u32[]{:S(2)}, u32[]{:S(2)}) collective-permute-start(bf16[16,112,128]{2,1,0:T(8,128)(2,1)} %get-tuple-element.46), channel_id=1, source_target_pairs={{0,16},{8,24},{16,32},{24,40},{32,48},{40,56},{48,0},{56,8},{1,17}... | collective-permute-start | bytes 1376264 | tf_op jit(solution)/shard_map/ppermute | solution.py:254
  253.5 38.4 %collective-permute-start.29 = (bf16[16,112,128]{2,1,0:T(8,128)(2,1)}, bf16[16,112,128]{2,1,0:T(8,128)(2,1)}, u32[]{:S(2)}, u32[]{:S(2)}) collective-permute-start(bf16[16,112,128]{2,1,0:T(8,128)(2,1)} %get-tuple-element.47), channel_id=1, source_target_pairs={{0,48},{8,56},{16,0},{24,8},{32,16},{40,24},{48,32},{56,40},{1,49}... | collective-permute-start | bytes 1376264 | tf_op jit(solution)/shard_map/ppermute | solution.py:254
  264.4 25.9 %collective-permute-start.9 = (bf16[8,112,128]{2,1,0:T(8,128)(2,1)}, bf16[8,112,128]{2,1,0:T(8,128)(2,1)}, u32[]{:S(2)}, u32[]{:S(2)}) collective-permute-start(bf16[8,112,128]{2,1,0:T(8,128)(2,1)} %get-tuple-element.32), channel_id=1, source_target_pairs={{0,24},{8,16},{16,40},{24,32},{32,56},{40,48},{48,8},{56,0},{1,25}... | collective-permute-start | bytes 688136 | tf_op jit(solution)/shard_map/ppermute | solution.py:254
  264.7 33.4 %collective-permute-start.30 = (bf16[16,112,128]{2,1,0:T(8,128)(2,1)}, bf16[16,112,128]{2,1,0:T(8,128)(2,1)}, u32[]{:S(2)}, u32[]{:S(2)}) collective-permute-start(bf16[16,112,128]{2,1,0:T(8,128)(2,1)} %get-tuple-element.48), channel_id=1, source_target_pairs={{0,24},{8,16},{16,40},{24,32},{32,56},{40,48},{48,8},{56,0},{1,25}... | collective-permute-start | bytes 1376264 | tf_op jit(solution)/shard_map/ppermute | solution.py:254
  278.6 50.8 %collective-permute-start.35 = (f32[2,2,256,256]{3,2,1,0:T(8,128)}, f32[2,2,256,256]{3,2,1,0:T(8,128)}, u32[]{:S(2)}, u32[]{:S(2)}) collective-permute-start(f32[2,2,256,256]{3,2,1,0:T(8,128)} %cross.7), channel_id=1, source_target_pairs={{0,64},{64,0},{1,65},{65,1},{2,66},{66,2},{3,67},{67,3},{4,68},{68... | collective-permute-start | bytes 3145736 | tf_op jit(solution)/shard_map/ppermute | solution.py:294
  290.4 42.1 %collective-permute-start.36 = (f32[2,2,256,256]{3,2,1,0:T(8,128)}, f32[2,2,256,256]{3,2,1,0:T(8,128)}, u32[]{:S(2)}, u32[]{:S(2)}) collective-permute-start(f32[2,2,256,256]{3,2,1,0:T(8,128)} %cross.8), channel_id=1, source_target_pairs={{0,64},{64,0},{1,65},{65,1},{2,66},{66,2},{3,67},{67,3},{4,68},{68... | collective-permute-start | bytes 3145736 | tf_op jit(solution)/shard_map/ppermute | solution.py:294
  290.5 20.9 %collective-permute-start.31 = (bf16[16,112,128]{2,1,0:T(8,128)(2,1)S(1)}, bf16[16,112,128]{2,1,0:T(8,128)(2,1)S(1)}, u32[]{:S(2)}, u32[]{:S(2)}) collective-permute-start(bf16[16,112,128]{2,1,0:T(8,128)(2,1)S(1)} %copy-done.23), channel_id=1, source_target_pairs={{0,56},{8,48},{16,8},{24,0},{32,24},{40,16},{48,40},{56,32},{1,57}... | collective-permute-start | bytes 1376264 | tf_op jit(solution)/shard_map/ppermute | solution.py:254
  291.9 19.5 %collective-permute-start.32 = (bf16[16,112,128]{2,1,0:T(8,128)(2,1)}, bf16[16,112,128]{2,1,0:T(8,128)(2,1)S(1)}, u32[]{:S(2)}, u32[]{:S(2)}) collective-permute-start(bf16[16,112,128]{2,1,0:T(8,128)(2,1)} %get-tuple-element.50), channel_id=1, source_target_pairs={{0,32},{8,40},{16,48},{24,56},{32,0},{40,8},{48,16},{56,24},{1,33}... | collective-permute-start | bytes 1376264 | tf_op jit(solution)/shard_map/ppermute | solution.py:254
  298.2 53.9 %collective-permute-start.27 = (f32[2,2,256,256]{3,2,1,0:T(8,128)}, f32[2,2,256,256]{3,2,1,0:T(8,128)S(1)}, u32[]{:S(2)}, u32[]{:S(2)}) collective-permute-start(f32[2,2,256,256]{3,2,1,0:T(8,128)} %cross.6), channel_id=1, source_target_pairs={{0,64},{64,0},{1,65},{65,1},{2,66},{66,2},{3,67},{67,3},{4,68},{68... | collective-permute-start | bytes 3145736 | tf_op jit(solution)/shard_map/ppermute | solution.py:294
  321.4 23.4 %collective-permute-start.10 = (bf16[8,112,128]{2,1,0:T(8,128)(2,1)}, bf16[8,112,128]{2,1,0:T(8,128)(2,1)S(1)}, u32[]{:S(2)}, u32[]{:S(2)}) collective-permute-start(bf16[8,112,128]{2,1,0:T(8,128)(2,1)} %get-tuple-element.33), channel_id=1, source_target_pairs={{0,56},{8,48},{16,8},{24,0},{32,24},{40,16},{48,40},{56,32},{1,57}... | collective-permute-start | bytes 688136 | tf_op jit(solution)/shard_map/ppermute | solution.py:254
  (31 other events, 395.3 us)
